TPU v7x, 256 devices: a whole 4x4x8 slice. The times are simulated.
256 devices in a mesh: row: 32 (over z, x_lo, core), col: 8 (over y, x_hi).
Axes of the slice: x: 4 (x_hi: 2, x_lo: 2; x = x_hi * 2 + x_lo), y: 4, z: 8, core: 2. Of those that a mesh axis runs over, the one named last changes fastest.
Arguments:
- first_homolog_embedding: bfloat16 [128, 1024, 32], P(None, ('row', 'col')), may hold values from -12 to 12
- second_homolog_embedding: bfloat16 [128, 1024, 32], P(None, ('row', 'col')), may hold values from -12 to 12
- token_chain_index: int32 [1024], replicated, may hold values from 0 to 7, never falling along the last dimension, each value on 1 to 384 neighbouring positions
- incoming_pair_state: bfloat16 [1024, 1024, 128], P('row', 'col'), may hold values from -6 to 6
- tensor_mixing_matrix: bfloat16 [1024, 128], replicated, may hold values from -0.1875 to 0.1875
- outer_product_bias: float32 [128], replicated, may hold values from -3 to 3
- transition_norm_gain: float32 [128], replicated, may hold values from 0.5 to 1.5
- transition_gate_weight: bfloat16 [128, 512], replicated, may hold values from -0.5 to 0.5
- transition_up_weight: bfloat16 [128, 512], replicated, may hold values from -0.5 to 0.5
- transition_down_weight: bfloat16 [512, 128], replicated, may hold values from -0.25 to 0.25
- distogram_weight: bfloat16 [128, 64], replicated, may hold values from -0.5 to 0.5
- distogram_bias: float32 [64], replicated, may hold values from -3 to 3
Outputs:
- pair_out: bfloat16 [1024, 1024, 128], P('row', 'col')
- logits: float32 [64, 1024, 1024], P(None, 'row', 'col')
Inputs may be any that keep to these rules, and one draw needn't show every extreme that they name: `token_chain_index`: chain numbers never fall along the tokens; each chain has 1 to 384 tokens and one chain has exactly 384.
All inputs are finite; a program needn't handle non-finite values.
Results may differ from a plain program's by a relative error of at most 0.006.
Values may be sent and summed in bfloat16 or wider, within the bound.
No kernel may reach another device: no remote copies, remote signals or barrier semaphores. Data moves between devices by JAX's collectives and lax.ppermute only.
A program may use at most 64 MiB of HBM per device.

v0:
```python
import jax
import jax.numpy as jnp
from jax import lax
from jax.experimental import pallas as pl
from jax.experimental.pallas import tpu as pltpu
from jax.sharding import PartitionSpec as P


AXES = ("row", "col")
F32 = jnp.float32
BF16 = jnp.bfloat16
DEVICES = [(a, b, c) for a in range(8) for b in range(4) for c in range(8)]
COL_MASKS = (0, 1, 4, 5, 2, 3, 6, 7)
UNROLL_D = 2
UNROLL_Q = 2


def flat(a, b, c):
    return (a * 4 + b) * 8 + c


def send(values, target):
    pairs = [(flat(*here), flat(*target(*here))) for here in DEVICES]
    return lax.ppermute(values, AXES, pairs)


def dot_nt(left, right):
    return lax.dot_general(left, right, (((1,), (1,)), ((), ())), preferred_element_type=F32)


def dot_nn(left, right):
    return lax.dot_general(left, right, (((1,), (0,)), ((), ())), preferred_element_type=F32)


def square_eye():
    down = lax.broadcasted_iota(jnp.int32, (128, 128), 0)
    along = lax.broadcasted_iota(jnp.int32, (128, 128), 1)
    return (down == along).astype(F32).astype(BF16)


def turn(values):
    return jnp.transpose(values.astype(F32), (1, 0))


def prep_kernel(
    mix, gate, up, down_w, bins_w, outer_bias, gain, bin_bias,
    mixing, gate_up, down, bins, bias_col, gain_col, bin_col, wide,
):
    wide[...] = mix[...].astype(F32)
    for block in range(8):
        parts = [wide[pl.ds(block * 4 + d, 32, stride=32), :] for d in range(4)]
        mixing[:, block * 128 : (block + 1) * 128] = turn(jnp.concatenate(parts, 0)).astype(BF16)
    for block in range(4):
        lanes = slice(block * 128, (block + 1) * 128)
        gate_up[block * 128 : (block + 1) * 128, :] = turn(gate[:, lanes]).astype(BF16)
        gate_up[512 + block * 128 : 512 + (block + 1) * 128, :] = turn(up[:, lanes]).astype(BF16)
        down[:, lanes] = turn(down_w[lanes, :]).astype(BF16)
    spread = jnp.broadcast_to(bins_w[...].astype(F32)[:, None, :], (64, 8, 128)).reshape(512, 128)
    which = lax.rem(lax.broadcasted_iota(jnp.int32, (512, 128), 0), 8)
    for one in range(8):
        bins[:, one * 128 : (one + 1) * 128] = jnp.where(which == one, spread, 0.0).astype(BF16)
    bias_col[...] = turn(jnp.broadcast_to(outer_bias[...], (128, 128)))
    gain_col[...] = turn(jnp.broadcast_to(gain[...], (128, 128)))
    bin_col[...] = turn(jnp.broadcast_to(bin_bias[...], (128, 64)))


def prep_call(mix, gate, up, down, bins, outer_bias, gain, bin_bias):
    return pl.pallas_call(
        prep_kernel,
        out_shape=(
            jax.ShapeDtypeStruct((128, 1024), BF16),
            jax.ShapeDtypeStruct((1024, 128), BF16),
            jax.ShapeDtypeStruct((128, 512), BF16),
            jax.ShapeDtypeStruct((512, 1024), BF16),
            jax.ShapeDtypeStruct((128, 128), F32),
            jax.ShapeDtypeStruct((128, 128), F32),
            jax.ShapeDtypeStruct((64, 128), F32),
        ),
        scratch_shapes=[pltpu.VMEM((1024, 128), F32)],
        name="prep",
    )(mix, gate, up, down, bins.T, outer_bias[None], gain[None], bin_bias[None])


def pair_kernel(
    meta,
    chain_at,
    left_near,
    left_far,
    right_own,
    right_other,
    chains,
    incoming,
    mixing,
    gate_up,
    down,
    bins,
    bias_col,
    gain_col,
    *rest,
):
    out, keep, give, right, left, outer, tile, rows, sent = rest[-9:]
    row_at, col_at, half_at = meta[0], meta[1], meta[2]
    z_at = lax.div(row_at, 4)
    core = lax.rem(row_at, 2)
    first_chain = chain_at[row_at * 32]
    last_chain = chain_at[row_at * 32 + 31]

    for step in range(8):
        place = lax.rem(z_at + (step + 4), 8)
        own_row = pl.multiple_of((core * 8 + place) * 128, 128)
        other_row = pl.multiple_of(((1 - core) * 8 + place) * 128, 128)
        right[pl.ds(own_row, 128), :] = right_own[step].astype(F32)
        right[pl.ds(other_row, 128), :] = right_other[step].astype(F32)

    paired = lax.broadcasted_iota(jnp.int32, (64, 128), 1) < 64
    token = lax.broadcasted_iota(jnp.int32, (64, 128), 0) + (col_at * 128 + half_at * 64)
    zeros = jnp.zeros((64, 128), BF16)

    def one_chain(chain, add):
        for step, mask in enumerate(COL_MASKS):
            place = jnp.bitwise_xor(col_at, mask)
            chunk = left_near[step] if step < 4 else left_far[step - 4]
            for t in range(4):
                of_row = chain_at[row_at * 32 + place * 4 + t]
                values = chunk[t * 32 : (t + 1) * 32, :]
                values = jnp.where(of_row == chain, values, jnp.zeros_like(values))
                at = pl.multiple_of((place * 2 + t // 2) * 32, 32)
                left[pl.ds(at, 32), (t % 2) * 128 : (t % 2) * 128 + 128] = values
        start = jnp.sum((chains[...] < chain).astype(F32)).astype(jnp.int32)
        stop = jnp.sum((chains[...] <= chain).astype(F32)).astype(jnp.int32)
        same = jnp.logical_and(token >= start, token < stop)
        scale = jnp.where(
            same,
            F32(1.0 / 128.0),
            jnp.where(paired, F32(1.0 / 64.0), F32(0.0)),
        )

        def channels(step, inner):
            weights = []
            for pair in range(UNROLL_D):
                blocks = []
                for half in range(2):
                    d = step * (2 * UNROLL_D) + pair * 2 + half
                    values = (right[pl.ds(d, 64, stride=32), :] * scale).astype(BF16)
                    blocks.append(jnp.concatenate([values, zeros], 1))
                    blocks.append(jnp.concatenate([zeros, values], 1))
                weights.append(jnp.concatenate(blocks, 0))
            for pair in range(UNROLL_D):
                product = dot_nt(left[...], weights[pair]).astype(BF16)
                for ip in range(16):
                    for half in range(2):
                        at = pl.multiple_of((step * (2 * UNROLL_D) + pair * 2 + half) * 32, 32)
                        lanes = (ip % 2) * 128
                        piece = product[ip * 32 : (ip + 1) * 32, half * 128 : (half + 1) * 128]
                        if add:
                            piece = piece + outer[ip // 2, pl.ds(at, 32), lanes : lanes + 128]
                        outer[ip // 2, pl.ds(at, 32), lanes : lanes + 128] = piece
            return inner

        lax.fori_loop(0, 16 // UNROLL_D, channels, 0)

    one_chain(first_chain, False)

    def more_chains(chain, carry):
        one_chain(chain, True)
        return carry

    lax.fori_loop(first_chain + 1, last_chain + 1, more_chains, 0)

    eye = square_eye()
    bias = jnp.concatenate([bias_col[...], bias_col[...]], 1)
    scale_by = jnp.concatenate([gain_col[...], gain_col[...]], 1)

    def some_rows(step, carry):
        quads = [step * UNROLL_Q + q for q in range(UNROLL_Q)]
        mids = []
        for quad in quads:
            arriving = incoming[pl.ds(pl.multiple_of(quad * 4, 4), 4)].reshape(256, 128)
            mid = dot_nn(mixing[...], outer[quad]) + dot_nt(eye, arriving) + bias
            mids.append(mid.astype(BF16).astype(F32))
        normeds = []
        for mid in mids:
            center = jnp.sum(mid, axis=0, keepdims=True) * F32(1.0 / 128.0)
            shifted = mid - center
            spread = jnp.sum(shifted * shifted, axis=0, keepdims=True) * F32(1.0 / 128.0)
            normeds.append((shifted * lax.rsqrt(spread + F32(1e-05)) * scale_by).astype(BF16))
        results = list(mids)
        for part in range(2):
            for q in range(UNROLL_Q):
                gate = dot_nn(gate_up[part * 256 : (part + 1) * 256, :], normeds[q])
                up = dot_nn(gate_up[512 + part * 256 : 512 + (part + 1) * 256, :], normeds[q])
                half_gate = gate * F32(0.5)
                hidden = ((half_gate + half_gate * jnp.tanh(half_gate)) * up).astype(BF16)
                results[q] = results[q] + dot_nn(down[:, part * 256 : (part + 1) * 256], hidden)
        for q, quad in enumerate(quads):
            turned = turn(results[q].astype(BF16))
            out[pl.ds(pl.multiple_of(quad * 4, 4), 4)] = turned.astype(BF16).reshape(4, 64, 128)
            tile[pl.ds(pl.multiple_of(quad * 256, 256), 256), :] = turned
        return carry

    lax.fori_loop(0, 8 // UNROLL_Q, some_rows, 0)

    for group in range(8):
        for one in range(8):
            values = tile[pl.ds(group * 8 + one, 32, stride=64), :].astype(BF16)
            rows[group * 32 : (group + 1) * 32, one * 128 : (one + 1) * 128] = values
    sent[...] = dot_nt(rows[...], bins[...]).astype(BF16)
    keep[...] = sent[pl.ds(pl.multiple_of(core * 128, 128), 128), :]
    give[...] = sent[pl.ds(pl.multiple_of((1 - core) * 128, 128), 128), :]


def pair_call(meta, chain_at, left_near, left_far, own, other, incoming, weights, so_far):
    whole = lambda shape: pl.BlockSpec(shape, lambda g, m, k: (0,) * len(shape))
    by_half = pl.BlockSpec((32, 64, 128), lambda g, m, k: (0, m[2], 0))
    operands = [left_near, left_far, own, other, chain_at.reshape(8, 128), incoming, *weights]
    specs = [
        whole((4, 128, 128)),
        whole((4, 128, 128)),
        whole((8, 128, 128)),
        whole((8, 128, 128)),
        whole((8, 128)),
        by_half,
        *[whole(w.shape) for w in weights],
    ]
    aliases = {}
    if so_far is not None:
        operands.append(so_far)
        specs.append(pl.BlockSpec(memory_space=pl.ANY))
        aliases = {len(operands) + 1: 0}
    return pl.pallas_call(
        pair_kernel,
        out_shape=(
            jax.ShapeDtypeStruct((32, 128, 128), BF16),
            jax.ShapeDtypeStruct((128, 512), BF16),
            jax.ShapeDtypeStruct((128, 512), BF16),
        ),
        grid_spec=pltpu.PrefetchScalarGridSpec(
            num_scalar_prefetch=2,
            grid=(1,),
            in_specs=specs,
            out_specs=(by_half, whole((128, 512)), whole((128, 512))),
            scratch_shapes=[
                pltpu.VMEM((2048, 128), F32),
                pltpu.VMEM((512, 256), BF16),
                pltpu.VMEM((8, 1024, 256), BF16),
                pltpu.VMEM((2048, 128), F32),
                pltpu.VMEM((256, 1024), BF16),
                pltpu.VMEM((256, 512), BF16),
            ],
        ),
        input_output_aliases=aliases,
        name="pair_half",
    )(meta, chain_at, *operands)


def own_kernel(tile, bins, bias, out):
    flat_rows = jnp.concatenate([tile[i] for i in range(8)], axis=1)
    product = dot_nt(bins[...], flat_rows).astype(BF16).astype(F32)
    out[...] = product.reshape(64, 8, 128) + bias[...][:, None, :]


def own_call(pair_out, bins, bias):
    return pl.pallas_call(
        own_kernel,
        out_shape=jax.ShapeDtypeStruct((64, 32, 128), F32),
        grid=(4,),
        in_specs=[
            pl.BlockSpec((8, 128, 128), lambda g: (g, 0, 0)),
            pl.BlockSpec((512, 1024), lambda g: (0, 0)),
            pl.BlockSpec((64, 128), lambda g: (0, 0)),
        ],
        out_specs=pl.BlockSpec((64, 8, 128), lambda g: (0, g, 0)),
        name="own_bins",
    )(pair_out, bins, bias)


def join_kernel(meta, own, near, far, out, block):
    b_at = lax.rem(meta[0], 4)
    eye = square_eye()
    for source in range(4):
        from_b = jnp.bitwise_xor(b_at, source)
        at = pl.multiple_of(from_b * 32, 32)
        values = near if source < 2 else far
        block[pl.ds(at, 32), :] = values[source % 2, 0]
    for part in range(4):
        turned = dot_nt(eye, block[:, part * 128 : (part + 1) * 128])
        out[part * 16 : (part + 1) * 16] = own[part * 16 : (part + 1) * 16] + turned.reshape(
            16, 8, 128
        )


def join_call(meta, own, near, far):
    arrived = pl.BlockSpec((2, 1, 32, 512), lambda g, m: (0, g, 0, 0))
    piece = pl.BlockSpec((64, 8, 128), lambda g, m: (0, g, 0))
    return pl.pallas_call(
        join_kernel,
        out_shape=jax.ShapeDtypeStruct((64, 32, 128), F32),
        grid_spec=pltpu.PrefetchScalarGridSpec(
            num_scalar_prefetch=1,
            grid=(4,),
            in_specs=[piece, arrived, arrived],
            out_specs=piece,
            scratch_shapes=[pltpu.VMEM((128, 512), BF16)],
        ),
        name="join_bins",
    )(meta, own, near, far)


def per_device(
    first_homolog_embedding,
    second_homolog_embedding,
    token_chain_index,
    incoming_pair_state,
    tensor_mixing_matrix,
    outer_product_bias,
    transition_norm_gain,
    transition_gate_weight,
    transition_up_weight,
    transition_down_weight,
    distogram_weight,
    distogram_bias,
):
    row_at = lax.axis_index("row").astype(jnp.int32)
    col_at = lax.axis_index("col").astype(jnp.int32)
    x_lo = (row_at // 2) % 2
    meta_a = jnp.stack([row_at, col_at, x_lo])
    meta_b = jnp.stack([row_at, col_at, 1 - x_lo])

    left = jnp.transpose(first_homolog_embedding, (1, 2, 0)).reshape(1, 128, 128)
    right = jnp.transpose(second_homolog_embedding, (1, 2, 0)).reshape(1, 128, 128)

    centre = send(right, lambda a, b, c: (c, b, a))
    *weights, bin_col = prep_call(
        tensor_mixing_matrix,
        transition_gate_weight,
        transition_up_weight,
        transition_down_weight,
        distogram_weight,
        outer_product_bias,
        transition_norm_gain,
        distogram_bias,
    )
    left_two = jnp.concatenate([left, send(left, lambda a, b, c: (a, b, c ^ 1))], 0)
    before = send(centre, lambda a, b, c: ((a + 1) % 8, b, c))
    after = send(centre, lambda a, b, c: ((a - 1) % 8, b, c))
    left_near = jnp.concatenate([left_two, send(left_two, lambda a, b, c: (a, b, c ^ 4))], 0)
    three = jnp.concatenate([before, centre, after], 0)
    low = send(three, lambda a, b, c: ((a + 3) % 8, b, c))
    high = send(three[:2], lambda a, b, c: ((a - 3) % 8, b, c))
    left_far = send(left_near, lambda a, b, c: (a, b, c ^ 2))
    own = jnp.concatenate([low, three, high], 0)
    other = send(own, lambda a, b, c: (a, b ^ 1, c))
    own_far = send(own, lambda a, b, c: (a, b ^ 2, c))

    pair_out, keep, give = pair_call(
        meta_a, token_chain_index, left_near, left_far, own, other,
        incoming_pair_state, weights, None,
    )
    other_far = send(own_far, lambda a, b, c: (a, b ^ 1, c))
    given = send(give, lambda a, b, c: (a, b ^ 1, c))
    near = send(jnp.stack([keep, given]), lambda a, b, c: (c, b, a))
    pair_out, keep, give = pair_call(
        meta_b, token_chain_index, left_near, left_far, own_far, other_far,
        incoming_pair_state, weights, pair_out,
    )
    given = send(give, lambda a, b, c: (a, b ^ 1, c))
    far = send(jnp.stack([keep, given]), lambda a, b, c: (c, b ^ 2, a))

    own_bins = own_call(pair_out, weights[3], bin_col)
    logits = join_call(meta_a, own_bins, near.reshape(2, 4, 32, 512), far.reshape(2, 4, 32, 512))
    return (pair_out, logits)


def solution(mesh):
    placed = (
        P(None, ("row", "col"), None),
        P(None, ("row", "col"), None),
        P(),
        P("row", "col", None),
        P(),
        P(),
        P(),
        P(),
        P(),
        P(),
        P(),
        P(),
    )
    return jax.shard_map(
        per_device,
        mesh=mesh,
        in_specs=placed,
        out_specs=(P("row", "col", None), P(None, "row", "col")),
        check_vma=False,
    )
```

profile of v0, /device:TPU:227, one launch (start us, length us, event | category | flops | bytes accessed | tf_op | source)
XLA Modules:
  0.0 167.3 jit_solution(4455826454320335873)
XLA Ops:
  0.6 3.0 %collective-permute-start.3 = (bf16[1,128,128]{2,1,0:T(8,128)(2,1)}, bf16[1,128,128]{2,1,0:T(8,128)(2,1)S(1)}, u32[]{:S(2)}, u32[]{:S(2)}) collective-permute-start(bf16[1,128,128]{2,1,0:T(8,128)(2,1)} %bitcast.36), channel_id=1, source_target_pairs={{0,0},{1,32},{2,64},{3,96},{4,128},{5,160},{6,192},{7,224},{8,8},{... | collective-permute-start | bytes 98312 | tf_op jit(solution)/shard_map/ppermute | solution.py:24
  3.7 8.0 %collective-permute-done.3 = bf16[1,128,128]{2,1,0:T(8,128)(2,1)S(1)} collective-permute-done((bf16[1,128,128]{2,1,0:T(8,128)(2,1)}, bf16[1,128,128]{2,1,0:T(8,128)(2,1)S(1)}, u32[]{:S(2)}, u32[]{:S(2)}) %collective-permute-start.3) | collective-permute-done | bytes 32800 | tf_op jit(solution)/shard_map/ppermute | solution.py:24
  11.7 0.0 collective-permute-start.5
  11.7 2.7 %collective-permute-start.4 = (bf16[1,128,128]{2,1,0:T(8,128)(2,1)S(1)}, bf16[1,128,128]{2,1,0:T(8,128)(2,1)S(1)}, u32[]{:S(2)}, u32[]{:S(2)}) collective-permute-start(bf16[1,128,128]{2,1,0:T(8,128)(2,1)S(1)} %collective-permute-done.3), channel_id=1, source_target_pairs={{0,32},{1,33},{2,34},{3,35},{4,36},{5,37},{6,38},{7,39},{8,40},{9,... | collective-permute-start | bytes 98312 | tf_op jit(solution)/shard_map/ppermute | solution.py:24
  14.3 1.3 collective-permute-done.5
  15.6 0.8 collective-permute-done.4
  16.5 0.1 collective-permute-start.6
  16.6 3.3 %collective-permute-start.7 = (bf16[2,128,128]{2,1,0:T(8,128)(2,1)S(1)}, bf16[2,128,128]{2,1,0:T(8,128)(2,1)S(1)}, u32[]{:S(2)}, u32[]{:S(2)}) collective-permute-start(bf16[2,128,128]{2,1,0:T(8,128)(2,1)S(1)} %pad_maximum_fusion.5), channel_id=1, source_target_pairs={{0,160},{1,161},{2,162},{3,163},{4,164},{5,165},{6,166},{7,167},{8... | collective-permute-start | bytes 196616 | tf_op jit(solution)/shard_map/ppermute | solution.py:24
  19.9 2.0 %collective-permute-done.6 = bf16[3,128,128]{2,1,0:T(8,128)(2,1)S(1)} collective-permute-done((bf16[3,128,128]{2,1,0:T(8,128)(2,1)S(1)}, bf16[3,128,128]{2,1,0:T(8,128)(2,1)S(1)}, u32[]{:S(2)}, u32[]{:S(2)}) %collective-permute-start.6) | collective-permute-done | bytes 98336 | tf_op jit(solution)/shard_map/ppermute | solution.py:24
  21.9 0.0 copy-start.10
  21.9 0.9 collective-permute-done.7
  22.8 0.0 copy-start.2
  22.8 0.2 collective-permute-start.8
  23.1 0.0 copy-done.10
  23.1 3.8 %collective-permute-start = (bf16[1,128,128]{2,1,0:T(8,128)(2,1)S(1)}, bf16[1,128,128]{2,1,0:T(8,128)(2,1)S(1)}, u32[]{:S(2)}, u32[]{:S(2)}) collective-permute-start(bf16[1,128,128]{2,1,0:T(8,128)(2,1)S(1)} %bitcast.27), channel_id=1, source_target_pairs={{0,1},{1,0},{2,3},{3,2},{4,5},{5,4},{6,7},{7,6},{8,9},{9,8},{10,11... | collective-permute-start | bytes 98312 | tf_op jit(solution)/shard_map/ppermute | solution.py:24
  26.9 4.1 %collective-permute-done = bf16[1,128,128]{2,1,0:T(8,128)(2,1)S(1)} collective-permute-done((bf16[1,128,128]{2,1,0:T(8,128)(2,1)S(1)}, bf16[1,128,128]{2,1,0:T(8,128)(2,1)S(1)}, u32[]{:S(2)}, u32[]{:S(2)}) %collective-permute-start) | collective-permute-done | bytes 32800 | tf_op jit(solution)/shard_map/ppermute | solution.py:24
  31.0 0.1 collective-permute-start.1
  31.1 6.0 %collective-permute-start.10 = (bf16[8,128,128]{2,1,0:T(8,128)(2,1)S(1)}, bf16[8,128,128]{2,1,0:T(8,128)(2,1)S(1)}, u32[]{:S(2)}, u32[]{:S(2)}) collective-permute-start(bf16[8,128,128]{2,1,0:T(8,128)(2,1)S(1)} %constant_dynamic-update-slice_fusion.right_own), channel_id=1, source_target_pairs={{0,8},{1,9},{2,10},{3,11},{4,12},{5,13},{6,14},{7,15},{8,0},{9,1},... | collective-permute-start | bytes 786440 | tf_op jit(solution)/shard_map/ppermute | solution.py:24
  37.1 0.0 collective-permute-done.8.right_own
  37.2 0.0 copy-start.3
  37.2 0.1 collective-permute-start.9
  37.2 0.0 collective-permute-done.1
  37.3 0.0 copy-start
  37.3 2.2 %collective-permute-start.2 = (bf16[4,128,128]{2,1,0:T(8,128)(2,1)S(1)}, bf16[4,128,128]{2,1,0:T(8,128)(2,1)S(1)}, u32[]{:S(2)}, u32[]{:S(2)}) collective-permute-start(bf16[4,128,128]{2,1,0:T(8,128)(2,1)S(1)} %pad_maximum_fusion.2.left_near), channel_id=1, source_target_pairs={{0,2},{1,3},{2,0},{3,1},{4,6},{5,7},{6,4},{7,5},{8,10},{9,11},{10,... | collective-permute-start | bytes 393224 | tf_op jit(solution)/shard_map/ppermute | solution.py:24
  39.4 3.1 %prep.1 = (bf16[128,1024]{1,0:T(8,128)(2,1)}, bf16[1024,128]{1,0:T(8,128)(2,1)}, bf16[128,512]{1,0:T(8,128)(2,1)}, bf16[512,1024]{1,0:T(8,128)(2,1)}, f32[128,12...) custom-call(bf16[1024,128]{1,0:T(8,128)(2,1)} %mix.1, bf16[128,512]{1,0:T(8,128)(2,1)} %gate.1, ...), custom_call_target="tpu_custom_call" | custom-call | tf_op jit(solution)/shard_map/prep/pallas_call | solution.py:68
  42.5 0.0 copy-done.2
  42.5 0.0 copy-done.3
  42.5 0.0 copy-done
  42.5 0.7 pad_add_fusion.2.meta
  43.2 0.0 collective-permute-done.2.left_far
  43.2 0.0 copy-start.1
  43.2 0.0 collective-permute-done.10.right_other
  43.2 0.0 copy-start.5
  43.2 0.6 copy-done.1
  43.9 0.1 copy-done.5
  44.0 13.8 %pair_half.2 = (bf16[32,128,128]{2,1,0:T(8,128)(2,1)}, bf16[128,512]{1,0:T(8,128)(2,1)}, bf16[128,512]{1,0:T(8,128)(2,1)}) custom-call(s32[3]{0:T(128)} %pad_add_fusion.2.meta, s32[1024]{0:T(1024)} %chain_at.3, bf16[4,128,128]{2,1,0:T(8,128)(2,1)} %copy-done, bf16[4,128,128]{2,1,0:T(8,128)(2,1)} %copy-done.1, bf16[8,128,128]{2,1,0:T(8,128)(2,1)} %copy-done.2, ...), custom_call_target="tpu_custom_call" | custom-call | tf_op jit(solution)/shard_map/pair_half/pallas_call | solution.py:230
  57.8 5.5 %collective-permute-start.11 = (bf16[128,512]{1,0:T(8,128)(2,1)}, bf16[128,512]{1,0:T(8,128)(2,1)S(1)}, u32[]{:S(2)}, u32[]{:S(2)}) collective-permute-start(bf16[128,512]{1,0:T(8,128)(2,1)} %get-tuple-element.25), channel_id=1, source_target_pairs={{0,8},{1,9},{2,10},{3,11},{4,12},{5,13},{6,14},{7,15},{8,0},{9,1},... | collective-permute-start | bytes 393224 | tf_op jit(solution)/shard_map/ppermute | solution.py:24
  63.2 0.6 pad_add_fusion.meta
  63.8 0.0 collective-permute-done.9.right_other
  63.8 0.0 copy-start.4
  63.8 0.7 copy-done.4
  64.5 0.0 copy-start.8
  64.5 14.0 %pair_half.3 = (bf16[32,128,128]{2,1,0:T(8,128)(2,1)}, bf16[128,512]{1,0:T(8,128)(2,1)}, bf16[128,512]{1,0:T(8,128)(2,1)}) custom-call(s32[3]{0:T(128)} %pad_add_fusion.meta, s32[1024]{0:T(1024)} %chain_at.3, bf16[4,128,128]{2,1,0:T(8,128)(2,1)} %copy-done, bf16[4,128,128]{2,1,0:T(8,128)(2,1)} %copy-done.1, ...), custom_call_target="tpu_custom_call", output_to_operand_aliasing={{0}: (14, {})} | custom-call | tf_op jit(solution)/shard_map/pair_half/pallas_call | solution.py:230
  78.6 0.0 collective-permute-start.13
  78.6 0.0 collective-permute-done.11
  78.6 0.0 copy-done.8
  78.6 0.0 copy-start.9
  78.6 6.0 %collective-permute-start.12 = (bf16[2,128,512]{2,1,0:T(8,128)(2,1)S(1)}, bf16[2,128,512]{2,1,0:T(8,128)(2,1)S(1)}, u32[]{:S(2)}, u32[]{:S(2)}) collective-permute-start(bf16[2,128,512]{2,1,0:T(8,128)(2,1)S(1)} %pad_maximum_fusion), channel_id=1, source_target_pairs={{0,0},{1,32},{2,64},{3,96},{4,128},{5,160},{6,192},{7,224},{8,8},{... | collective-permute-start | bytes 786440 | tf_op jit(solution)/shard_map/ppermute | solution.py:24
  84.6 0.0 collective-permute-done.13
  84.6 0.0 copy-done.9
  84.7 22.6 %collective-permute-start.14 = (bf16[2,128,512]{2,1,0:T(8,128)(2,1)S(1)}, bf16[2,128,512]{2,1,0:T(8,128)(2,1)S(1)}, u32[]{:S(2)}, u32[]{:S(2)}) collective-permute-start(bf16[2,128,512]{2,1,0:T(8,128)(2,1)S(1)} %pad_maximum_fusion.1), channel_id=1, source_target_pairs={{0,16},{1,48},{2,80},{3,112},{4,144},{5,176},{6,208},{7,240},{8,24... | collective-permute-start | bytes 786440 | tf_op jit(solution)/shard_map/ppermute | solution.py:24
  107.3 4.6 %own_bins.1.own = f32[64,32,128]{2,1,0:T(8,128)} custom-call(bf16[32,128,128]{2,1,0:T(8,128)(2,1)} %get-tuple-element.13.tile, bf16[512,1024]{1,0:T(8,128)(2,1)} %get-tuple-element.18.bins, f32[64,128]{1,0:T(8,128)} %get-tuple-element.23.bias), custom_call_target="tpu_custom_call" | custom-call | tf_op jit(solution)/shard_map/own_bins/pallas_call | solution.py:263
  111.9 16.0 %collective-permute-done.12 = bf16[2,128,512]{2,1,0:T(8,128)(2,1)S(1)} collective-permute-done((bf16[2,128,512]{2,1,0:T(8,128)(2,1)S(1)}, bf16[2,128,512]{2,1,0:T(8,128)(2,1)S(1)}, u32[]{:S(2)}, u32[]{:S(2)}) %collective-permute-start.12) | collective-permute-done | bytes 262176 | tf_op jit(solution)/shard_map/ppermute | solution.py:24
  127.9 0.0 copy-start.6
  127.9 34.2 %collective-permute-done.14 = bf16[2,128,512]{2,1,0:T(8,128)(2,1)S(1)} collective-permute-done((bf16[2,128,512]{2,1,0:T(8,128)(2,1)S(1)}, bf16[2,128,512]{2,1,0:T(8,128)(2,1)S(1)}, u32[]{:S(2)}, u32[]{:S(2)}) %collective-permute-start.14) | collective-permute-done | bytes 262176 | tf_op jit(solution)/shard_map/ppermute | solution.py:24
  162.1 0.0 copy-start.7
  162.1 0.0 copy-done.6
  162.1 0.7 copy-done.7
  162.8 4.5 %join_bins.1 = f32[64,32,128]{2,1,0:T(8,128)} custom-call(s32[3]{0:T(128)} %pad_add_fusion.2.meta, f32[64,32,128]{2,1,0:T(8,128)} %own_bins.1.own, bf16[2,4,32,512]{3,2,1,0:T(8,128)(2,1)} %bitcast.21, bf16[2,4,32,512]{3,2,1,0:T(8,128)(2,1)} %bitcast.22), custom_call_target="tpu_custom_call" | custom-call | tf_op jit(solution)/shard_map/join_bins/pallas_call | solution.py:295
  (11 shorter events, 0.2 us)
Async XLA Ops:
  0.6 11.0 %collective-permute-start.3 = (bf16[1,128,128]{2,1,0:T(8,128)(2,1)}, bf16[1,128,128]{2,1,0:T(8,128)(2,1)S(1)}, u32[]{:S(2)}, u32[]{:S(2)}) collective-permute-start(bf16[1,128,128]{2,1,0:T(8,128)(2,1)} %bitcast.36), channel_id=1, source_target_pairs={{0,0},{1,32},{2,64},{3,96},{4,128},{5,160},{6,192},{7,224},{8,8},{... | collective-permute-start | bytes 98312 | tf_op jit(solution)/shard_map/ppermute | solution.py:24
  11.7 4.0 %collective-permute-start.5 = (bf16[1,128,128]{2,1,0:T(8,128)(2,1)S(1)}, bf16[1,128,128]{2,1,0:T(8,128)(2,1)S(1)}, u32[]{:S(2)}, u32[]{:S(2)}) collective-permute-start(bf16[1,128,128]{2,1,0:T(8,128)(2,1)S(1)} %collective-permute-done.3), channel_id=1, source_target_pairs={{0,224},{1,225},{2,226},{3,227},{4,228},{5,229},{6,230},{7,231},{8... | collective-permute-start | bytes 98312 | tf_op jit(solution)/shard_map/ppermute | solution.py:24
  11.7 4.8 %collective-permute-start.4 = (bf16[1,128,128]{2,1,0:T(8,128)(2,1)S(1)}, bf16[1,128,128]{2,1,0:T(8,128)(2,1)S(1)}, u32[]{:S(2)}, u32[]{:S(2)}) collective-permute-start(bf16[1,128,128]{2,1,0:T(8,128)(2,1)S(1)} %collective-permute-done.3), channel_id=1, source_target_pairs={{0,32},{1,33},{2,34},{3,35},{4,36},{5,37},{6,38},{7,39},{8,40},{9,... | collective-permute-start | bytes 98312 | tf_op jit(solution)/shard_map/ppermute | solution.py:24
  16.5 5.4 %collective-permute-start.6 = (bf16[3,128,128]{2,1,0:T(8,128)(2,1)S(1)}, bf16[3,128,128]{2,1,0:T(8,128)(2,1)S(1)}, u32[]{:S(2)}, u32[]{:S(2)}) collective-permute-start(bf16[3,128,128]{2,1,0:T(8,128)(2,1)S(1)} %pad_maximum_fusion.3), channel_id=1, source_target_pairs={{0,96},{1,97},{2,98},{3,99},{4,100},{5,101},{6,102},{7,103},{8,104... | collective-permute-start | bytes 294920 | tf_op jit(solution)/shard_map/ppermute | solution.py:24
  16.6 6.2 %collective-permute-start.7 = (bf16[2,128,128]{2,1,0:T(8,128)(2,1)S(1)}, bf16[2,128,128]{2,1,0:T(8,128)(2,1)S(1)}, u32[]{:S(2)}, u32[]{:S(2)}) collective-permute-start(bf16[2,128,128]{2,1,0:T(8,128)(2,1)S(1)} %pad_maximum_fusion.5), channel_id=1, source_target_pairs={{0,160},{1,161},{2,162},{3,163},{4,164},{5,165},{6,166},{7,167},{8... | collective-permute-start | bytes 196616 | tf_op jit(solution)/shard_map/ppermute | solution.py:24
  21.9 1.2 copy-start.10
  22.8 19.7 %copy-start.2 = (bf16[8,128,128]{2,1,0:T(8,128)(2,1)}, bf16[8,128,128]{2,1,0:T(8,128)(2,1)S(1)}, u32[]{:S(2)}) copy-start(bf16[8,128,128]{2,1,0:T(8,128)(2,1)S(1)} %constant_dynamic-update-slice_fusion.right_own) | copy-start | bytes 786436
  22.8 14.3 %collective-permute-start.8 = (bf16[8,128,128]{2,1,0:T(8,128)(2,1)S(1)}, bf16[8,128,128]{2,1,0:T(8,128)(2,1)S(1)}, u32[]{:S(2)}, u32[]{:S(2)}) collective-permute-start(bf16[8,128,128]{2,1,0:T(8,128)(2,1)S(1)} %constant_dynamic-update-slice_fusion.right_own), channel_id=1, source_target_pairs={{0,16},{1,17},{2,18},{3,19},{4,20},{5,21},{6,22},{7,23},{8,24},{9,... | collective-permute-start | bytes 786440 | tf_op jit(solution)/shard_map/ppermute | solution.py:24
  23.1 7.9 %collective-permute-start = (bf16[1,128,128]{2,1,0:T(8,128)(2,1)S(1)}, bf16[1,128,128]{2,1,0:T(8,128)(2,1)S(1)}, u32[]{:S(2)}, u32[]{:S(2)}) collective-permute-start(bf16[1,128,128]{2,1,0:T(8,128)(2,1)S(1)} %bitcast.27), channel_id=1, source_target_pairs={{0,1},{1,0},{2,3},{3,2},{4,5},{5,4},{6,7},{7,6},{8,9},{9,8},{10,11... | collective-permute-start | bytes 98312 | tf_op jit(solution)/shard_map/ppermute | solution.py:24
  31.0 6.3 %collective-permute-start.1 = (bf16[2,128,128]{2,1,0:T(8,128)(2,1)S(1)}, bf16[2,128,128]{2,1,0:T(8,128)(2,1)S(1)}, u32[]{:S(2)}, u32[]{:S(2)}) collective-permute-start(bf16[2,128,128]{2,1,0:T(8,128)(2,1)S(1)} %pad_maximum_fusion.4), channel_id=1, source_target_pairs={{0,4},{1,5},{2,6},{3,7},{4,0},{5,1},{6,2},{7,3},{8,12},{9,13},{10,... | collective-permute-start | bytes 196616 | tf_op jit(solution)/shard_map/ppermute | solution.py:24
  31.1 12.1 %collective-permute-start.10 = (bf16[8,128,128]{2,1,0:T(8,128)(2,1)S(1)}, bf16[8,128,128]{2,1,0:T(8,128)(2,1)S(1)}, u32[]{:S(2)}, u32[]{:S(2)}) collective-permute-start(bf16[8,128,128]{2,1,0:T(8,128)(2,1)S(1)} %constant_dynamic-update-slice_fusion.right_own), channel_id=1, source_target_pairs={{0,8},{1,9},{2,10},{3,11},{4,12},{5,13},{6,14},{7,15},{8,0},{9,1},... | collective-permute-start | bytes 786440 | tf_op jit(solution)/shard_map/ppermute | solution.py:24
  37.2 5.4 %copy-start.3 = (bf16[8,128,128]{2,1,0:T(8,128)(2,1)}, bf16[8,128,128]{2,1,0:T(8,128)(2,1)S(1)}, u32[]{:S(2)}) copy-start(bf16[8,128,128]{2,1,0:T(8,128)(2,1)S(1)} %collective-permute-done.8.right_own) | copy-start | bytes 786436
  37.2 26.7 %collective-permute-start.9 = (bf16[8,128,128]{2,1,0:T(8,128)(2,1)S(1)}, bf16[8,128,128]{2,1,0:T(8,128)(2,1)S(1)}, u32[]{:S(2)}, u32[]{:S(2)}) collective-permute-start(bf16[8,128,128]{2,1,0:T(8,128)(2,1)S(1)} %collective-permute-done.8.right_own), channel_id=1, source_target_pairs={{0,8},{1,9},{2,10},{3,11},{4,12},{5,13},{6,14},{7,15},{8,0},{9,1},... | collective-permute-start | bytes 786440 | tf_op jit(solution)/shard_map/ppermute | solution.py:24
  37.3 5.3 %copy-start = (bf16[4,128,128]{2,1,0:T(8,128)(2,1)}, bf16[4,128,128]{2,1,0:T(8,128)(2,1)S(1)}, u32[]{:S(2)}) copy-start(bf16[4,128,128]{2,1,0:T(8,128)(2,1)S(1)} %pad_maximum_fusion.2.left_near) | copy-start | bytes 393220
  37.3 5.9 %collective-permute-start.2 = (bf16[4,128,128]{2,1,0:T(8,128)(2,1)S(1)}, bf16[4,128,128]{2,1,0:T(8,128)(2,1)S(1)}, u32[]{:S(2)}, u32[]{:S(2)}) collective-permute-start(bf16[4,128,128]{2,1,0:T(8,128)(2,1)S(1)} %pad_maximum_fusion.2.left_near), channel_id=1, source_target_pairs={{0,2},{1,3},{2,0},{3,1},{4,6},{5,7},{6,4},{7,5},{8,10},{9,11},{10,... | collective-permute-start | bytes 393224 | tf_op jit(solution)/shard_map/ppermute | solution.py:24
  43.2 0.6 copy-start.1
  43.2 0.8 copy-start.5
  57.8 20.8 %collective-permute-start.11 = (bf16[128,512]{1,0:T(8,128)(2,1)}, bf16[128,512]{1,0:T(8,128)(2,1)S(1)}, u32[]{:S(2)}, u32[]{:S(2)}) collective-permute-start(bf16[128,512]{1,0:T(8,128)(2,1)} %get-tuple-element.25), channel_id=1, source_target_pairs={{0,8},{1,9},{2,10},{3,11},{4,12},{5,13},{6,14},{7,15},{8,0},{9,1},... | collective-permute-start | bytes 393224 | tf_op jit(solution)/shard_map/ppermute | solution.py:24
  63.8 0.7 copy-start.4
  64.5 14.1 %copy-start.8 = (bf16[128,512]{1,0:T(8,128)(2,1)S(1)}, bf16[128,512]{1,0:T(8,128)(2,1)}, u32[]{:S(2)}) copy-start(bf16[128,512]{1,0:T(8,128)(2,1)} %get-tuple-element.24) | copy-start | bytes 393220
  78.6 6.1 %collective-permute-start.13 = (bf16[128,512]{1,0:T(8,128)(2,1)}, bf16[128,512]{1,0:T(8,128)(2,1)S(1)}, u32[]{:S(2)}, u32[]{:S(2)}) collective-permute-start(bf16[128,512]{1,0:T(8,128)(2,1)} %get-tuple-element.27), channel_id=1, source_target_pairs={{0,8},{1,9},{2,10},{3,11},{4,12},{5,13},{6,14},{7,15},{8,0},{9,1},... | collective-permute-start | bytes 393224 | tf_op jit(solution)/shard_map/ppermute | solution.py:24
  78.6 6.0 %copy-start.9 = (bf16[128,512]{1,0:T(8,128)(2,1)S(1)}, bf16[128,512]{1,0:T(8,128)(2,1)}, u32[]{:S(2)}) copy-start(bf16[128,512]{1,0:T(8,128)(2,1)} %get-tuple-element.26) | copy-start | bytes 393220
  78.6 49.3 %collective-permute-start.12 = (bf16[2,128,512]{2,1,0:T(8,128)(2,1)S(1)}, bf16[2,128,512]{2,1,0:T(8,128)(2,1)S(1)}, u32[]{:S(2)}, u32[]{:S(2)}) collective-permute-start(bf16[2,128,512]{2,1,0:T(8,128)(2,1)S(1)} %pad_maximum_fusion), channel_id=1, source_target_pairs={{0,0},{1,32},{2,64},{3,96},{4,128},{5,160},{6,192},{7,224},{8,8},{... | collective-permute-start | bytes 786440 | tf_op jit(solution)/shard_map/ppermute | solution.py:24
  84.7 77.4 %collective-permute-start.14 = (bf16[2,128,512]{2,1,0:T(8,128)(2,1)S(1)}, bf16[2,128,512]{2,1,0:T(8,128)(2,1)S(1)}, u32[]{:S(2)}, u32[]{:S(2)}) collective-permute-start(bf16[2,128,512]{2,1,0:T(8,128)(2,1)S(1)} %pad_maximum_fusion.1), channel_id=1, source_target_pairs={{0,16},{1,48},{2,80},{3,112},{4,144},{5,176},{6,208},{7,240},{8,24... | collective-permute-start | bytes 786440 | tf_op jit(solution)/shard_map/ppermute | solution.py:24
  127.9 34.2 %copy-start.6 = (bf16[2,128,512]{2,1,0:T(8,128)(2,1)}, bf16[2,128,512]{2,1,0:T(8,128)(2,1)S(1)}, u32[]{:S(2)}) copy-start(bf16[2,128,512]{2,1,0:T(8,128)(2,1)S(1)} %collective-permute-done.12) | copy-start | bytes 786436
  162.1 0.7 copy-start.7
where the time goes:
time: 168 us; the launch traced here: 167 us
  waiting for transfers between devices  67.3 us (40%)
  starting transfers between devices  55.6 us (33%)
  Pallas kernels  40 us (24%)
  local copies, waits for them, and re-layouts  2.26 us (1%)
    ppermute x15, waiting for transfers between devices, send(): return lax.ppermute(values, AXES, pairs)  67.3 us
    ppermute x15, starting transfers between devices, send(): return lax.ppermute(values, AXES, pairs)  55.6 us
    pallas_call x2, Pallas kernels, pair_call(): pl.pallas_call(pair_kernel, out_shape=(jax.ShapeDtypeStruct((32, 128, 128...  27.8 us
    pallas_call x1, Pallas kernels, own_call(): pl.pallas_call(own_kernel, out_shape=jax.ShapeDtypeStruct((64, 32, 128),...  4.62 us
    pallas_call x1, Pallas kernels, join_call(): pl.pallas_call(join_kernel, out_shape=jax.ShapeDtypeStruct((64, 32, 128),...  4.47 us
  transfers between devices with their start and end apart: 15, of which 8 were waited for; matrix products, arithmetic and copies ran while one was open for 1% of the time, Pallas kernels for 21%

commit v1 on v0

--- a/solution.py
+++ b/solution.py
@@ -1,3 +1,5 @@
+import functools
+
 import jax
 import jax.numpy as jnp
 from jax import lax
@@ -11,8 +13,14 @@
 BF16 = jnp.bfloat16
 DEVICES = [(a, b, c) for a in range(8) for b in range(4) for c in range(8)]
 COL_MASKS = (0, 1, 4, 5, 2, 3, 6, 7)
-UNROLL_D = 2
-UNROLL_Q = 2
+QUADS = 2
+
+
+def in_vmem(values):
+    return pltpu.with_memory_space_constraint(values, pltpu.VMEM)
+
+
+VMEM_SPEC = pl.BlockSpec(memory_space=pltpu.VMEM)
 
 
 def flat(a, b, c):
@@ -65,20 +73,28 @@
 
 
 def prep_call(mix, gate, up, down, bins, outer_bias, gain, bin_bias):
+    operands = (mix, gate, up, down, bins.T, outer_bias[None], gain[None], bin_bias[None])
     return pl.pallas_call(
         prep_kernel,
         out_shape=(
-            jax.ShapeDtypeStruct((128, 1024), BF16),
-            jax.ShapeDtypeStruct((1024, 128), BF16),
-            jax.ShapeDtypeStruct((128, 512), BF16),
-            jax.ShapeDtypeStruct((512, 1024), BF16),
-            jax.ShapeDtypeStruct((128, 128), F32),
-            jax.ShapeDtypeStruct((128, 128), F32),
-            jax.ShapeDtypeStruct((64, 128), F32),
+            pltpu.VMEM((128, 1024), BF16),
+            pltpu.VMEM((1024, 128), BF16),
+            pltpu.VMEM((128, 512), BF16),
+            pltpu.VMEM((512, 1024), BF16),
+            pltpu.VMEM((128, 128), F32),
+            pltpu.VMEM((128, 128), F32),
+            pltpu.VMEM((64, 128), F32),
         ),
+        out_specs=[VMEM_SPEC] * 7,
         scratch_shapes=[pltpu.VMEM((1024, 128), F32)],
+        compiler_params=pltpu.CompilerParams(vmem_limit_bytes=16 << 20),
         name="prep",
-    )(mix, gate, up, down, bins.T, outer_bias[None], gain[None], bin_bias[None])
+    )(*[pltpu.with_memory_space_constraint(v, pltpu.HBM) for v in operands])
+
+
+def half_of(row_at, flip):
+    x_lo = lax.rem(lax.div(row_at, 2), 2)
+    return 1 - x_lo if flip else x_lo
 
 
 def pair_kernel(
@@ -97,9 +113,11 @@
     bias_col,
     gain_col,
     *rest,
+    flip,
 ):
     out, keep, give, right, left, outer, tile, rows, sent = rest[-9:]
-    row_at, col_at, half_at = meta[0], meta[1], meta[2]
+    row_at, col_at = meta[0], meta[1]
+    half_at = half_of(row_at, flip)
     z_at = lax.div(row_at, 4)
     core = lax.rem(row_at, 2)
     first_chain = chain_at[row_at * 32]
@@ -116,7 +134,7 @@
     token = lax.broadcasted_iota(jnp.int32, (64, 128), 0) + (col_at * 128 + half_at * 64)
     zeros = jnp.zeros((64, 128), BF16)
 
-    def one_chain(chain, add):
+    def one_chain(chain, window, unroll):
         for step, mask in enumerate(COL_MASKS):
             place = jnp.bitwise_xor(col_at, mask)
             chunk = left_near[step] if step < 4 else left_far[step - 4]
@@ -137,45 +155,54 @@
 
         def channels(step, inner):
             weights = []
-            for pair in range(UNROLL_D):
+            for pair in range(unroll):
                 blocks = []
                 for half in range(2):
-                    d = step * (2 * UNROLL_D) + pair * 2 + half
+                    d = step * (2 * unroll) + pair * 2 + half
                     values = (right[pl.ds(d, 64, stride=32), :] * scale).astype(BF16)
                     blocks.append(jnp.concatenate([values, zeros], 1))
                     blocks.append(jnp.concatenate([zeros, values], 1))
                 weights.append(jnp.concatenate(blocks, 0))
-            for pair in range(UNROLL_D):
-                product = dot_nt(left[...], weights[pair]).astype(BF16)
-                for ip in range(16):
+            for pair in range(unroll):
+                if window is None:
+                    rows_in = left[...]
+                else:
+                    rows_in = left[pl.ds(pl.multiple_of(window * 256, 256), 256), :]
+                product = dot_nt(rows_in, weights[pair]).astype(BF16)
+                for ip in range(16 if window is None else 8):
+                    quad = ip // 2 if window is None else window * 4 + ip // 2
                     for half in range(2):
-                        at = pl.multiple_of((step * (2 * UNROLL_D) + pair * 2 + half) * 32, 32)
+                        at = pl.multiple_of((step * (2 * unroll) + pair * 2 + half) * 32, 32)
                         lanes = (ip % 2) * 128
                         piece = product[ip * 32 : (ip + 1) * 32, half * 128 : (half + 1) * 128]
-                        if add:
-                            piece = piece + outer[ip // 2, pl.ds(at, 32), lanes : lanes + 128]
-                        outer[ip // 2, pl.ds(at, 32), lanes : lanes + 128] = piece
+                        if window is not None:
+                            piece = piece + outer[quad, pl.ds(at, 32), lanes : lanes + 128]
+                        outer[quad, pl.ds(at, 32), lanes : lanes + 128] = piece
             return inner
 
-        lax.fori_loop(0, 16 // UNROLL_D, channels, 0)
-
-    one_chain(first_chain, False)
-
-    def more_chains(chain, carry):
-        one_chain(chain, True)
+        lax.fori_loop(0, 16 // unroll, channels, 0)
+
+    main_chain = chain_at[row_at * 32 + 16]
+    one_chain(main_chain, None, 4)
+
+    def more_chains(step, carry):
+        chain = step + (step >= main_chain).astype(jnp.int32)
+        one_chain(chain, (chain > main_chain).astype(jnp.int32), 2)
         return carry
 
-    lax.fori_loop(first_chain + 1, last_chain + 1, more_chains, 0)
+    lax.fori_loop(first_chain, last_chain, more_chains, 0)
 
     eye = square_eye()
     bias = jnp.concatenate([bias_col[...], bias_col[...]], 1)
     scale_by = jnp.concatenate([gain_col[...], gain_col[...]], 1)
 
     def some_rows(step, carry):
-        quads = [step * UNROLL_Q + q for q in range(UNROLL_Q)]
+        quads = [step * QUADS + q for q in range(QUADS)]
         mids = []
         for quad in quads:
-            arriving = incoming[pl.ds(pl.multiple_of(quad * 4, 4), 4)].reshape(256, 128)
+            arriving = incoming[
+                pl.ds(pl.multiple_of(quad * 4, 4), 4), pl.ds(pl.multiple_of(half_at * 64, 64), 64), :
+            ].reshape(256, 128)
             mid = dot_nn(mixing[...], outer[quad]) + dot_nt(eye, arriving) + bias
             mids.append(mid.astype(BF16).astype(F32))
         normeds = []
@@ -186,7 +213,7 @@
             normeds.append((shifted * lax.rsqrt(spread + F32(1e-05)) * scale_by).astype(BF16))
         results = list(mids)
         for part in range(2):
-            for q in range(UNROLL_Q):
+            for q in range(QUADS):
                 gate = dot_nn(gate_up[part * 256 : (part + 1) * 256, :], normeds[q])
                 up = dot_nn(gate_up[512 + part * 256 : 512 + (part + 1) * 256, :], normeds[q])
                 half_gate = gate * F32(0.5)
@@ -198,7 +225,7 @@
             tile[pl.ds(pl.multiple_of(quad * 256, 256), 256), :] = turned
         return carry
 
-    lax.fori_loop(0, 8 // UNROLL_Q, some_rows, 0)
+    lax.fori_loop(0, 8 // QUADS, some_rows, 0)
 
     for group in range(8):
         for one in range(8):
@@ -209,36 +236,28 @@
     give[...] = sent[pl.ds(pl.multiple_of((1 - core) * 128, 128), 128), :]
 
 
-def pair_call(meta, chain_at, left_near, left_far, own, other, incoming, weights, so_far):
-    whole = lambda shape: pl.BlockSpec(shape, lambda g, m, k: (0,) * len(shape))
-    by_half = pl.BlockSpec((32, 64, 128), lambda g, m, k: (0, m[2], 0))
+def pair_call(meta, flip, chain_at, left_near, left_far, own, other, incoming, weights, so_far):
+    by_half = pl.BlockSpec((32, 64, 128), lambda g, m, k: (0, half_of(m[0], flip), 0))
     operands = [left_near, left_far, own, other, chain_at.reshape(8, 128), incoming, *weights]
-    specs = [
-        whole((4, 128, 128)),
-        whole((4, 128, 128)),
-        whole((8, 128, 128)),
-        whole((8, 128, 128)),
-        whole((8, 128)),
-        by_half,
-        *[whole(w.shape) for w in weights],
-    ]
+    operands = [in_vmem(values) for values in operands]
+    specs = [VMEM_SPEC] * len(operands)
     aliases = {}
     if so_far is not None:
         operands.append(so_far)
         specs.append(pl.BlockSpec(memory_space=pl.ANY))
         aliases = {len(operands) + 1: 0}
     return pl.pallas_call(
-        pair_kernel,
+        functools.partial(pair_kernel, flip=flip),
         out_shape=(
             jax.ShapeDtypeStruct((32, 128, 128), BF16),
-            jax.ShapeDtypeStruct((128, 512), BF16),
-            jax.ShapeDtypeStruct((128, 512), BF16),
+            pltpu.VMEM((128, 512), BF16),
+            pltpu.VMEM((128, 512), BF16),
         ),
         grid_spec=pltpu.PrefetchScalarGridSpec(
             num_scalar_prefetch=2,
             grid=(1,),
             in_specs=specs,
-            out_specs=(by_half, whole((128, 512)), whole((128, 512))),
+            out_specs=(by_half, VMEM_SPEC, VMEM_SPEC),
             scratch_shapes=[
                 pltpu.VMEM((2048, 128), F32),
                 pltpu.VMEM((512, 256), BF16),
@@ -249,61 +268,61 @@
             ],
         ),
         input_output_aliases=aliases,
+        compiler_params=pltpu.CompilerParams(vmem_limit_bytes=24 << 20),
         name="pair_half",
     )(meta, chain_at, *operands)
 
 
 def own_kernel(tile, bins, bias, out):
+    rows = pl.ds(pl.multiple_of(pl.program_id(0) * 8, 8), 8)
     flat_rows = jnp.concatenate([tile[i] for i in range(8)], axis=1)
     product = dot_nt(bins[...], flat_rows).astype(BF16).astype(F32)
-    out[...] = product.reshape(64, 8, 128) + bias[...][:, None, :]
+    out[:, rows, :] = product.reshape(64, 8, 128) + bias[...][:, None, :]
 
 
 def own_call(pair_out, bins, bias):
     return pl.pallas_call(
         own_kernel,
-        out_shape=jax.ShapeDtypeStruct((64, 32, 128), F32),
+        out_shape=pltpu.VMEM((64, 32, 128), F32),
         grid=(4,),
-        in_specs=[
-            pl.BlockSpec((8, 128, 128), lambda g: (g, 0, 0)),
-            pl.BlockSpec((512, 1024), lambda g: (0, 0)),
-            pl.BlockSpec((64, 128), lambda g: (0, 0)),
-        ],
-        out_specs=pl.BlockSpec((64, 8, 128), lambda g: (0, g, 0)),
+        in_specs=[pl.BlockSpec((8, 128, 128), lambda g: (g, 0, 0)), VMEM_SPEC, VMEM_SPEC],
+        out_specs=VMEM_SPEC,
+        compiler_params=pltpu.CompilerParams(vmem_limit_bytes=16 << 20),
         name="own_bins",
-    )(pair_out, bins, bias)
+    )(pair_out, in_vmem(bins), in_vmem(bias))
 
 
 def join_kernel(meta, own, near, far, out, block):
     b_at = lax.rem(meta[0], 4)
+    step = pl.program_id(0)
+    rows = pl.ds(pl.multiple_of(step * 8, 8), 8)
     eye = square_eye()
     for source in range(4):
         from_b = jnp.bitwise_xor(b_at, source)
         at = pl.multiple_of(from_b * 32, 32)
         values = near if source < 2 else far
-        block[pl.ds(at, 32), :] = values[source % 2, 0]
+        block[pl.ds(at, 32), :] = values[source % 2, step]
     for part in range(4):
         turned = dot_nt(eye, block[:, part * 128 : (part + 1) * 128])
-        out[part * 16 : (part + 1) * 16] = own[part * 16 : (part + 1) * 16] + turned.reshape(
-            16, 8, 128
-        )
+        out[part * 16 : (part + 1) * 16] = own[
+            part * 16 : (part + 1) * 16, rows, :
+        ] + turned.reshape(16, 8, 128)
 
 
 def join_call(meta, own, near, far):
-    arrived = pl.BlockSpec((2, 1, 32, 512), lambda g, m: (0, g, 0, 0))
-    piece = pl.BlockSpec((64, 8, 128), lambda g, m: (0, g, 0))
     return pl.pallas_call(
         join_kernel,
         out_shape=jax.ShapeDtypeStruct((64, 32, 128), F32),
         grid_spec=pltpu.PrefetchScalarGridSpec(
             num_scalar_prefetch=1,
             grid=(4,),
-            in_specs=[piece, arrived, arrived],
-            out_specs=piece,
+            in_specs=[VMEM_SPEC, VMEM_SPEC, VMEM_SPEC],
+            out_specs=pl.BlockSpec((64, 8, 128), lambda g, m: (0, g, 0)),
             scratch_shapes=[pltpu.VMEM((128, 512), BF16)],
         ),
+        compiler_params=pltpu.CompilerParams(vmem_limit_bytes=16 << 20),
         name="join_bins",
-    )(meta, own, near, far)
+    )(meta, in_vmem(own), in_vmem(near), in_vmem(far))
 
 
 def per_device(
@@ -322,9 +341,7 @@
 ):
     row_at = lax.axis_index("row").astype(jnp.int32)
     col_at = lax.axis_index("col").astype(jnp.int32)
-    x_lo = (row_at // 2) % 2
-    meta_a = jnp.stack([row_at, col_at, x_lo])
-    meta_b = jnp.stack([row_at, col_at, 1 - x_lo])
+    meta = jnp.stack([row_at, col_at])
 
     left = jnp.transpose(first_homolog_embedding, (1, 2, 0)).reshape(1, 128, 128)
     right = jnp.transpose(second_homolog_embedding, (1, 2, 0)).reshape(1, 128, 128)
@@ -353,21 +370,23 @@
     own_far = send(own, lambda a, b, c: (a, b ^ 2, c))
 
     pair_out, keep, give = pair_call(
-        meta_a, token_chain_index, left_near, left_far, own, other,
+        meta, False, token_chain_index, left_near, left_far, own, other,
         incoming_pair_state, weights, None,
     )
     other_far = send(own_far, lambda a, b, c: (a, b ^ 1, c))
     given = send(give, lambda a, b, c: (a, b ^ 1, c))
     near = send(jnp.stack([keep, given]), lambda a, b, c: (c, b, a))
     pair_out, keep, give = pair_call(
-        meta_b, token_chain_index, left_near, left_far, own_far, other_far,
+        meta, True, token_chain_index, left_near, left_far, own_far, other_far,
         incoming_pair_state, weights, pair_out,
     )
     given = send(give, lambda a, b, c: (a, b ^ 1, c))
     far = send(jnp.stack([keep, given]), lambda a, b, c: (c, b ^ 2, a))
 
     own_bins = own_call(pair_out, weights[3], bin_col)
-    logits = join_call(meta_a, own_bins, near.reshape(2, 4, 32, 512), far.reshape(2, 4, 32, 512))
+    logits = join_call(
+        meta, own_bins, near.reshape(2, 4, 32, 512), far.reshape(2, 4, 32, 512)
+    )
     return (pair_out, logits)
 
 

time: 168 us -> 150 us (0.89)
  Pallas kernels: 40 us -> 28.3 us
  starting transfers between devices: 55.6 us -> 48.5 us
  waiting for transfers between devices: 67.3 us -> 69.6 us
    pallas_call x4, Pallas kernels: 35.5 us -> 25.7 us  [the longest x2 21.7 us: pair_call(): pl.pallas_call(functools.partial(pair_kernel, flip=flip), out_shape=(jax....]
    ppermute x15, starting transfers between devices: 55.6 us -> 48.5 us  [send(): return lax.ppermute(values, AXES, pairs)]
    ppermute x15, waiting for transfers between devices: 67.3 us -> 69.6 us  [send(): return lax.ppermute(values, AXES, pairs)]
    pallas_call x1, Pallas kernels: 4.47 us -> 2.66 us  [join_call(): pl.pallas_call(join_kernel, out_shape=jax.ShapeDtypeStruct((64, 32, 128),...]
  transfers between devices with their start and end apart: 15 -> 15, of which waited for: 8 -> 9; matrix products, arithmetic and copies ran while one was open for 1% -> 1% of each run, Pallas kernels for 21% -> 17%
where the time goes in v1:
time: 150 us
  waiting for transfers between devices  69.6 us (46%)
  starting transfers between devices  48.5 us (32%)
  Pallas kernels  28.3 us (19%)
  other arithmetic  1.7 us (1%)
    ppermute x15, waiting for transfers between devices, send(): return lax.ppermute(values, AXES, pairs)  69.6 us
    ppermute x15, starting transfers between devices, send(): return lax.ppermute(values, AXES, pairs)  48.5 us
    pallas_call x2, Pallas kernels, pair_call(): pl.pallas_call(functools.partial(pair_kernel, flip=flip), out_shape=(jax....  21.7 us
  transfers between devices with their start and end apart: 15, of which 9 were waited for; matrix products, arithmetic and copies ran while one was open for 1% of the time, Pallas kernels for 17%

profile of v1, /device:TPU:227, one launch (start us, length us, event | category | flops | bytes accessed | tf_op | source)
XLA Modules:
  0.0 149.6 jit_solution(5496435604610080133)
XLA Ops:
  0.6 0.0 copy-start.1
  0.6 3.2 %collective-permute-start.3 = (bf16[1,128,128]{2,1,0:T(8,128)(2,1)}, bf16[1,128,128]{2,1,0:T(8,128)(2,1)S(1)}, u32[]{:S(2)}, u32[]{:S(2)}) collective-permute-start(bf16[1,128,128]{2,1,0:T(8,128)(2,1)} %bitcast.34), channel_id=1, source_target_pairs={{0,0},{1,32},{2,64},{3,96},{4,128},{5,160},{6,192},{7,224},{8,8},{... | collective-permute-start | bytes 98312 | tf_op jit(solution)/shard_map/ppermute | solution.py:32
  3.8 8.0 %collective-permute-done.3 = bf16[1,128,128]{2,1,0:T(8,128)(2,1)S(1)} collective-permute-done((bf16[1,128,128]{2,1,0:T(8,128)(2,1)}, bf16[1,128,128]{2,1,0:T(8,128)(2,1)S(1)}, u32[]{:S(2)}, u32[]{:S(2)}) %collective-permute-start.3) | collective-permute-done | bytes 32800 | tf_op jit(solution)/shard_map/ppermute | solution.py:32
  11.8 0.0 collective-permute-start.5
  11.8 2.7 %collective-permute-start.4 = (bf16[1,128,128]{2,1,0:T(8,128)(2,1)S(1)}, bf16[1,128,128]{2,1,0:T(8,128)(2,1)S(1)}, u32[]{:S(2)}, u32[]{:S(2)}) collective-permute-start(bf16[1,128,128]{2,1,0:T(8,128)(2,1)S(1)} %collective-permute-done.3), channel_id=1, source_target_pairs={{0,32},{1,33},{2,34},{3,35},{4,36},{5,37},{6,38},{7,39},{8,40},{9,... | collective-permute-start | bytes 98312 | tf_op jit(solution)/shard_map/ppermute | solution.py:32
  14.5 1.3 collective-permute-done.5
  15.8 0.8 collective-permute-done.4
  16.6 0.1 collective-permute-start.6
  16.7 3.3 %collective-permute-start.7 = (bf16[2,128,128]{2,1,0:T(8,128)(2,1)S(1)}, bf16[2,128,128]{2,1,0:T(8,128)(2,1)S(1)}, u32[]{:S(2)}, u32[]{:S(2)}) collective-permute-start(bf16[2,128,128]{2,1,0:T(8,128)(2,1)S(1)} %pad_maximum_fusion.5), channel_id=1, source_target_pairs={{0,160},{1,161},{2,162},{3,163},{4,164},{5,165},{6,166},{7,167},{8... | collective-permute-start | bytes 196616 | tf_op jit(solution)/shard_map/ppermute | solution.py:32
  20.0 2.0 %collective-permute-done.6 = bf16[3,128,128]{2,1,0:T(8,128)(2,1)S(1)} collective-permute-done((bf16[3,128,128]{2,1,0:T(8,128)(2,1)S(1)}, bf16[3,128,128]{2,1,0:T(8,128)(2,1)S(1)}, u32[]{:S(2)}, u32[]{:S(2)}) %collective-permute-start.6) | collective-permute-done | bytes 98336 | tf_op jit(solution)/shard_map/ppermute | solution.py:32
  22.0 0.9 collective-permute-done.7
  22.9 0.2 collective-permute-start.8
  23.2 3.8 %collective-permute-start = (bf16[1,128,128]{2,1,0:T(8,128)(2,1)}, bf16[1,128,128]{2,1,0:T(8,128)(2,1)S(1)}, u32[]{:S(2)}, u32[]{:S(2)}) collective-permute-start(bf16[1,128,128]{2,1,0:T(8,128)(2,1)} %bitcast.27), channel_id=1, source_target_pairs={{0,1},{1,0},{2,3},{3,2},{4,5},{5,4},{6,7},{7,6},{8,9},{9,8},{10,11... | collective-permute-start | bytes 98312 | tf_op jit(solution)/shard_map/ppermute | solution.py:32
  27.0 4.1 %collective-permute-done = bf16[1,128,128]{2,1,0:T(8,128)(2,1)S(1)} collective-permute-done((bf16[1,128,128]{2,1,0:T(8,128)(2,1)}, bf16[1,128,128]{2,1,0:T(8,128)(2,1)S(1)}, u32[]{:S(2)}, u32[]{:S(2)}) %collective-permute-start) | collective-permute-done | bytes 32800 | tf_op jit(solution)/shard_map/ppermute | solution.py:32
  31.1 0.8 pad_maximum_fusion.4
  31.9 0.0 collective-permute-start.1
  31.9 6.0 %collective-permute-start.10 = (bf16[8,128,128]{2,1,0:T(8,128)(2,1)S(1)}, bf16[8,128,128]{2,1,0:T(8,128)(2,1)S(1)}, u32[]{:S(2)}, u32[]{:S(2)}) collective-permute-start(bf16[8,128,128]{2,1,0:T(8,128)(2,1)S(1)} %constant_dynamic-update-slice_fusion.right_own), channel_id=1, source_target_pairs={{0,8},{1,9},{2,10},{3,11},{4,12},{5,13},{6,14},{7,15},{8,0},{9,1},... | collective-permute-start | bytes 786440 | tf_op jit(solution)/shard_map/ppermute | solution.py:32
  37.9 0.0 collective-permute-done.8.right_own
  38.0 0.0 collective-permute-start.9
  38.0 0.0 collective-permute-done.1
  38.0 0.8 pad_maximum_fusion.2.left_near
  38.7 2.2 %collective-permute-start.2 = (bf16[4,128,128]{2,1,0:T(8,128)(2,1)S(1)}, bf16[4,128,128]{2,1,0:T(8,128)(2,1)S(1)}, u32[]{:S(2)}, u32[]{:S(2)}) collective-permute-start(bf16[4,128,128]{2,1,0:T(8,128)(2,1)S(1)} %pad_maximum_fusion.2.left_near), channel_id=1, source_target_pairs={{0,2},{1,3},{2,0},{3,1},{4,6},{5,7},{6,4},{7,5},{8,10},{9,11},{10,... | collective-permute-start | bytes 393224 | tf_op jit(solution)/shard_map/ppermute | solution.py:32
  40.9 2.1 %prep.1 = (bf16[128,1024]{1,0:T(8,128)(2,1)S(1)}, bf16[1024,128]{1,0:T(8,128)(2,1)S(1)}, bf16[128,512]{1,0:T(8,128)(2,1)S(1)}, bf16[512,1024]{1,0:T(8,128)(2,1)S...) custom-call(bf16[1024,128]{1,0:T(8,128)(2,1)} %mix.1, bf16[128,512]{1,0:T(8,128)(2,1)} %gate.1, ...), custom_call_target="tpu_custom_call" | custom-call | tf_op jit(solution)/shard_map/prep/pallas_call | solution.py:77
  43.0 0.1 pad_add_fusion.meta
  43.1 0.1 collective-permute-done.2.left_far
  43.2 0.0 collective-permute-done.10.right_other
  43.3 0.0 copy-start.2
  43.3 0.0 copy-done.1
  43.3 0.7 copy-done.2
  43.9 10.8 %pair_half.2 = (bf16[32,128,128]{2,1,0:T(8,128)(2,1)}, bf16[128,512]{1,0:T(8,128)(2,1)S(1)}, bf16[128,512]{1,0:T(8,128)(2,1)S(1)}) custom-call(s32[2]{0:T(128)S(1)} %pad_add_fusion.meta, s32[1024]{0:T(1024)S(1)} %copy-done.2, bf16[4,128,128]{2,1,0:T(8,128)(2,1)S(1)} %pad_maximum_fusion.2.left_near, bf16[4,128,128]{2,1,0:T(8,128)(2,1)S(1)} %collective-permute-done.2.left_far, ...), custom_call_target="tpu_custom_call" | custom-call | tf_op jit(solution)/shard_map/pair_half/pallas_call | solution.py:249
  54.7 5.5 %collective-permute-start.11 = (bf16[128,512]{1,0:T(8,128)(2,1)S(1)}, bf16[128,512]{1,0:T(8,128)(2,1)S(1)}, u32[]{:S(2)}, u32[]{:S(2)}) collective-permute-start(bf16[128,512]{1,0:T(8,128)(2,1)S(1)} %get-tuple-element.25), channel_id=1, source_target_pairs={{0,8},{1,9},{2,10},{3,11},{4,12},{5,13},{6,14},{7,15},{8,0},{9,1},... | collective-permute-start | bytes 393224 | tf_op jit(solution)/shard_map/ppermute | solution.py:32
  60.2 0.0 collective-permute-done.9.right_other
  60.2 11.0 %pair_half.3 = (bf16[32,128,128]{2,1,0:T(8,128)(2,1)}, bf16[128,512]{1,0:T(8,128)(2,1)S(1)}, bf16[128,512]{1,0:T(8,128)(2,1)S(1)}) custom-call(s32[2]{0:T(128)S(1)} %pad_add_fusion.meta, s32[1024]{0:T(1024)S(1)} %copy-done.2, bf16[4,128,128]{2,1,0:T(8,128)(2,1)S(1)} %pad_maximum_fusion.2.left_near, ...), custom_call_target="tpu_custom_call", output_to_operand_aliasing={{0}: (14, {})} | custom-call | tf_op jit(solution)/shard_map/pair_half/pallas_call | solution.py:249
  71.2 0.0 copy-start
  71.2 0.0 collective-permute-start.13
  71.2 0.0 collective-permute-done.11
  71.3 7.2 %collective-permute-start.12 = (bf16[2,128,512]{2,1,0:T(8,128)(2,1)S(1)}, bf16[2,128,512]{2,1,0:T(8,128)(2,1)S(1)}, u32[]{:S(2)}, u32[]{:S(2)}) collective-permute-start(bf16[2,128,512]{2,1,0:T(8,128)(2,1)S(1)} %pad_maximum_fusion), channel_id=1, source_target_pairs={{0,0},{1,32},{2,64},{3,96},{4,128},{5,160},{6,192},{7,224},{8,8},{... | collective-permute-start | bytes 786440 | tf_op jit(solution)/shard_map/ppermute | solution.py:32
  78.5 0.0 collective-permute-done.13
  78.5 14.2 %collective-permute-start.14 = (bf16[2,128,512]{2,1,0:T(8,128)(2,1)S(1)}, bf16[2,128,512]{2,1,0:T(8,128)(2,1)S(1)}, u32[]{:S(2)}, u32[]{:S(2)}) collective-permute-start(bf16[2,128,512]{2,1,0:T(8,128)(2,1)S(1)} %pad_maximum_fusion.1), channel_id=1, source_target_pairs={{0,16},{1,48},{2,80},{3,112},{4,144},{5,176},{6,208},{7,240},{8,24... | collective-permute-start | bytes 786440 | tf_op jit(solution)/shard_map/ppermute | solution.py:32
  92.7 0.0 copy-done
  92.8 1.8 %own_bins.1.own = f32[64,32,128]{2,1,0:T(8,128)S(1)} custom-call(bf16[32,128,128]{2,1,0:T(8,128)(2,1)S(1)} %copy-done, bf16[512,1024]{1,0:T(8,128)(2,1)S(1)} %get-tuple-element.18.bins, f32[64,128]{1,0:T(8,128)S(1)} %get-tuple-element.23.bias), custom_call_target="tpu_custom_call" | custom-call | tf_op jit(solution)/shard_map/own_bins/pallas_call | solution.py:284
  94.6 28.8 %collective-permute-done.12 = bf16[2,128,512]{2,1,0:T(8,128)(2,1)S(1)} collective-permute-done((bf16[2,128,512]{2,1,0:T(8,128)(2,1)S(1)}, bf16[2,128,512]{2,1,0:T(8,128)(2,1)S(1)}, u32[]{:S(2)}, u32[]{:S(2)}) %collective-permute-start.12) | collective-permute-done | bytes 262176 | tf_op jit(solution)/shard_map/ppermute | solution.py:32
  123.3 23.7 %collective-permute-done.14 = bf16[2,128,512]{2,1,0:T(8,128)(2,1)S(1)} collective-permute-done((bf16[2,128,512]{2,1,0:T(8,128)(2,1)S(1)}, bf16[2,128,512]{2,1,0:T(8,128)(2,1)S(1)}, u32[]{:S(2)}, u32[]{:S(2)}) %collective-permute-start.14) | collective-permute-done | bytes 262176 | tf_op jit(solution)/shard_map/ppermute | solution.py:32
  147.0 2.7 %join_bins.1 = f32[64,32,128]{2,1,0:T(8,128)} custom-call(s32[2]{0:T(128)S(1)} %pad_add_fusion.meta, f32[64,32,128]{2,1,0:T(8,128)S(1)} %own_bins.1.own, bf16[2,4,32,512]{3,2,1,0:T(8,128)(2,1)S(1)} %bitcast.19, bf16[2,4,32,512]{3,2,1,0:T(8,128)(2,1)S(1)} %bitcast.20), custom_call_target="tpu_custom_call" | custom-call | tf_op jit(solution)/shard_map/join_bins/pallas_call | solution.py:313
  (9 shorter events, 0.1 us)
Async XLA Ops:
  0.6 42.6 %copy-start.1 = (bf16[32,128,128]{2,1,0:T(8,128)(2,1)S(1)}, bf16[32,128,128]{2,1,0:T(8,128)(2,1)}, u32[]{:S(2)}) copy-start(bf16[32,128,128]{2,1,0:T(8,128)(2,1)} %incoming.3) | copy-start | bytes 3145732
  0.6 11.2 %collective-permute-start.3 = (bf16[1,128,128]{2,1,0:T(8,128)(2,1)}, bf16[1,128,128]{2,1,0:T(8,128)(2,1)S(1)}, u32[]{:S(2)}, u32[]{:S(2)}) collective-permute-start(bf16[1,128,128]{2,1,0:T(8,128)(2,1)} %bitcast.34), channel_id=1, source_target_pairs={{0,0},{1,32},{2,64},{3,96},{4,128},{5,160},{6,192},{7,224},{8,8},{... | collective-permute-start | bytes 98312 | tf_op jit(solution)/shard_map/ppermute | solution.py:32
  11.8 4.0 %collective-permute-start.5 = (bf16[1,128,128]{2,1,0:T(8,128)(2,1)S(1)}, bf16[1,128,128]{2,1,0:T(8,128)(2,1)S(1)}, u32[]{:S(2)}, u32[]{:S(2)}) collective-permute-start(bf16[1,128,128]{2,1,0:T(8,128)(2,1)S(1)} %collective-permute-done.3), channel_id=1, source_target_pairs={{0,224},{1,225},{2,226},{3,227},{4,228},{5,229},{6,230},{7,231},{8... | collective-permute-start | bytes 98312 | tf_op jit(solution)/shard_map/ppermute | solution.py:32
  11.8 4.8 %collective-permute-start.4 = (bf16[1,128,128]{2,1,0:T(8,128)(2,1)S(1)}, bf16[1,128,128]{2,1,0:T(8,128)(2,1)S(1)}, u32[]{:S(2)}, u32[]{:S(2)}) collective-permute-start(bf16[1,128,128]{2,1,0:T(8,128)(2,1)S(1)} %collective-permute-done.3), channel_id=1, source_target_pairs={{0,32},{1,33},{2,34},{3,35},{4,36},{5,37},{6,38},{7,39},{8,40},{9,... | collective-permute-start | bytes 98312 | tf_op jit(solution)/shard_map/ppermute | solution.py:32
  16.6 5.4 %collective-permute-start.6 = (bf16[3,128,128]{2,1,0:T(8,128)(2,1)S(1)}, bf16[3,128,128]{2,1,0:T(8,128)(2,1)S(1)}, u32[]{:S(2)}, u32[]{:S(2)}) collective-permute-start(bf16[3,128,128]{2,1,0:T(8,128)(2,1)S(1)} %pad_maximum_fusion.3), channel_id=1, source_target_pairs={{0,96},{1,97},{2,98},{3,99},{4,100},{5,101},{6,102},{7,103},{8,104... | collective-permute-start | bytes 294920 | tf_op jit(solution)/shard_map/ppermute | solution.py:32
  16.7 6.2 %collective-permute-start.7 = (bf16[2,128,128]{2,1,0:T(8,128)(2,1)S(1)}, bf16[2,128,128]{2,1,0:T(8,128)(2,1)S(1)}, u32[]{:S(2)}, u32[]{:S(2)}) collective-permute-start(bf16[2,128,128]{2,1,0:T(8,128)(2,1)S(1)} %pad_maximum_fusion.5), channel_id=1, source_target_pairs={{0,160},{1,161},{2,162},{3,163},{4,164},{5,165},{6,166},{7,167},{8... | collective-permute-start | bytes 196616 | tf_op jit(solution)/shard_map/ppermute | solution.py:32
  22.9 15.0 %collective-permute-start.8 = (bf16[8,128,128]{2,1,0:T(8,128)(2,1)S(1)}, bf16[8,128,128]{2,1,0:T(8,128)(2,1)S(1)}, u32[]{:S(2)}, u32[]{:S(2)}) collective-permute-start(bf16[8,128,128]{2,1,0:T(8,128)(2,1)S(1)} %constant_dynamic-update-slice_fusion.right_own), channel_id=1, source_target_pairs={{0,16},{1,17},{2,18},{3,19},{4,20},{5,21},{6,22},{7,23},{8,24},{9,... | collective-permute-start | bytes 786440 | tf_op jit(solution)/shard_map/ppermute | solution.py:32
  23.2 7.9 %collective-permute-start = (bf16[1,128,128]{2,1,0:T(8,128)(2,1)}, bf16[1,128,128]{2,1,0:T(8,128)(2,1)S(1)}, u32[]{:S(2)}, u32[]{:S(2)}) collective-permute-start(bf16[1,128,128]{2,1,0:T(8,128)(2,1)} %bitcast.27), channel_id=1, source_target_pairs={{0,1},{1,0},{2,3},{3,2},{4,5},{5,4},{6,7},{7,6},{8,9},{9,8},{10,11... | collective-permute-start | bytes 98312 | tf_op jit(solution)/shard_map/ppermute | solution.py:32
  31.9 6.1 %collective-permute-start.1 = (bf16[2,128,128]{2,1,0:T(8,128)(2,1)S(1)}, bf16[2,128,128]{2,1,0:T(8,128)(2,1)S(1)}, u32[]{:S(2)}, u32[]{:S(2)}) collective-permute-start(bf16[2,128,128]{2,1,0:T(8,128)(2,1)S(1)} %pad_maximum_fusion.4), channel_id=1, source_target_pairs={{0,4},{1,5},{2,6},{3,7},{4,0},{5,1},{6,2},{7,3},{8,12},{9,13},{10,... | collective-permute-start | bytes 196616 | tf_op jit(solution)/shard_map/ppermute | solution.py:32
  31.9 11.3 %collective-permute-start.10 = (bf16[8,128,128]{2,1,0:T(8,128)(2,1)S(1)}, bf16[8,128,128]{2,1,0:T(8,128)(2,1)S(1)}, u32[]{:S(2)}, u32[]{:S(2)}) collective-permute-start(bf16[8,128,128]{2,1,0:T(8,128)(2,1)S(1)} %constant_dynamic-update-slice_fusion.right_own), channel_id=1, source_target_pairs={{0,8},{1,9},{2,10},{3,11},{4,12},{5,13},{6,14},{7,15},{8,0},{9,1},... | collective-permute-start | bytes 786440 | tf_op jit(solution)/shard_map/ppermute | solution.py:32
  38.0 22.3 %collective-permute-start.9 = (bf16[8,128,128]{2,1,0:T(8,128)(2,1)S(1)}, bf16[8,128,128]{2,1,0:T(8,128)(2,1)S(1)}, u32[]{:S(2)}, u32[]{:S(2)}) collective-permute-start(bf16[8,128,128]{2,1,0:T(8,128)(2,1)S(1)} %collective-permute-done.8.right_own), channel_id=1, source_target_pairs={{0,8},{1,9},{2,10},{3,11},{4,12},{5,13},{6,14},{7,15},{8,0},{9,1},... | collective-permute-start | bytes 786440 | tf_op jit(solution)/shard_map/ppermute | solution.py:32
  38.7 4.5 %collective-permute-start.2 = (bf16[4,128,128]{2,1,0:T(8,128)(2,1)S(1)}, bf16[4,128,128]{2,1,0:T(8,128)(2,1)S(1)}, u32[]{:S(2)}, u32[]{:S(2)}) collective-permute-start(bf16[4,128,128]{2,1,0:T(8,128)(2,1)S(1)} %pad_maximum_fusion.2.left_near), channel_id=1, source_target_pairs={{0,2},{1,3},{2,0},{3,1},{4,6},{5,7},{6,4},{7,5},{8,10},{9,11},{10,... | collective-permute-start | bytes 393224 | tf_op jit(solution)/shard_map/ppermute | solution.py:32
  43.3 0.7 copy-start.2
  54.7 16.5 %collective-permute-start.11 = (bf16[128,512]{1,0:T(8,128)(2,1)S(1)}, bf16[128,512]{1,0:T(8,128)(2,1)S(1)}, u32[]{:S(2)}, u32[]{:S(2)}) collective-permute-start(bf16[128,512]{1,0:T(8,128)(2,1)S(1)} %get-tuple-element.25), channel_id=1, source_target_pairs={{0,8},{1,9},{2,10},{3,11},{4,12},{5,13},{6,14},{7,15},{8,0},{9,1},... | collective-permute-start | bytes 393224 | tf_op jit(solution)/shard_map/ppermute | solution.py:32
  71.2 21.5 %copy-start = (bf16[32,128,128]{2,1,0:T(8,128)(2,1)S(1)}, bf16[32,128,128]{2,1,0:T(8,128)(2,1)}, u32[]{:S(2)}) copy-start(bf16[32,128,128]{2,1,0:T(8,128)(2,1)} %get-tuple-element.13.tile) | copy-start | bytes 3145732
  71.2 7.3 %collective-permute-start.13 = (bf16[128,512]{1,0:T(8,128)(2,1)S(1)}, bf16[128,512]{1,0:T(8,128)(2,1)S(1)}, u32[]{:S(2)}, u32[]{:S(2)}) collective-permute-start(bf16[128,512]{1,0:T(8,128)(2,1)S(1)} %get-tuple-element.27), channel_id=1, source_target_pairs={{0,8},{1,9},{2,10},{3,11},{4,12},{5,13},{6,14},{7,15},{8,0},{9,1},... | collective-permute-start | bytes 393224 | tf_op jit(solution)/shard_map/ppermute | solution.py:32
  71.3 52.1 %collective-permute-start.12 = (bf16[2,128,512]{2,1,0:T(8,128)(2,1)S(1)}, bf16[2,128,512]{2,1,0:T(8,128)(2,1)S(1)}, u32[]{:S(2)}, u32[]{:S(2)}) collective-permute-start(bf16[2,128,512]{2,1,0:T(8,128)(2,1)S(1)} %pad_maximum_fusion), channel_id=1, source_target_pairs={{0,0},{1,32},{2,64},{3,96},{4,128},{5,160},{6,192},{7,224},{8,8},{... | collective-permute-start | bytes 786440 | tf_op jit(solution)/shard_map/ppermute | solution.py:32
  78.5 68.4 %collective-permute-start.14 = (bf16[2,128,512]{2,1,0:T(8,128)(2,1)S(1)}, bf16[2,128,512]{2,1,0:T(8,128)(2,1)S(1)}, u32[]{:S(2)}, u32[]{:S(2)}) collective-permute-start(bf16[2,128,512]{2,1,0:T(8,128)(2,1)S(1)} %pad_maximum_fusion.1), channel_id=1, source_target_pairs={{0,16},{1,48},{2,80},{3,112},{4,144},{5,176},{6,208},{7,240},{8,24... | collective-permute-start | bytes 786440 | tf_op jit(solution)/shard_map/ppermute | solution.py:32

commit v2 on v1

--- a/solution.py
+++ b/solution.py
@@ -97,7 +97,7 @@
     return 1 - x_lo if flip else x_lo
 
 
-def pair_kernel(
+def outer_kernel(
     meta,
     chain_at,
     left_near,
@@ -105,17 +105,12 @@
     right_own,
     right_other,
     chains,
-    incoming,
-    mixing,
-    gate_up,
-    down,
-    bins,
-    bias_col,
-    gain_col,
-    *rest,
+    outer,
+    right,
+    left,
+    *,
     flip,
 ):
-    out, keep, give, right, left, outer, tile, rows, sent = rest[-9:]
     row_at, col_at = meta[0], meta[1]
     half_at = half_of(row_at, flip)
     z_at = lax.div(row_at, 4)
@@ -192,6 +187,31 @@
 
     lax.fori_loop(first_chain, last_chain, more_chains, 0)
 
+
+def outer_call(meta, flip, chain_at, left_near, left_far, own, other):
+    operands = [left_near, left_far, own, other, chain_at.reshape(8, 128)]
+    return pl.pallas_call(
+        functools.partial(outer_kernel, flip=flip),
+        out_shape=pltpu.VMEM((8, 1024, 256), BF16),
+        grid_spec=pltpu.PrefetchScalarGridSpec(
+            num_scalar_prefetch=2,
+            grid=(1,),
+            in_specs=[VMEM_SPEC] * len(operands),
+            out_specs=VMEM_SPEC,
+            scratch_shapes=[pltpu.VMEM((2048, 128), F32), pltpu.VMEM((512, 256), BF16)],
+        ),
+        compiler_params=pltpu.CompilerParams(vmem_limit_bytes=12 << 20),
+        name="outer_half",
+    )(meta, chain_at, *[in_vmem(values) for values in operands])
+
+
+def rows_kernel(
+    meta, outer, incoming, mixing, gate_up, down, bins, bias_col, gain_col, *rest, flip, part_at
+):
+    out, sent, tile, rows = rest[-4:]
+    row_at = meta[0]
+    core = lax.rem(row_at, 2)
+    half_at = half_of(row_at, flip)
     eye = square_eye()
     bias = jnp.concatenate([bias_col[...], bias_col[...]], 1)
     scale_by = jnp.concatenate([gain_col[...], gain_col[...]], 1)
@@ -201,9 +221,11 @@
         mids = []
         for quad in quads:
             arriving = incoming[
-                pl.ds(pl.multiple_of(quad * 4, 4), 4), pl.ds(pl.multiple_of(half_at * 64, 64), 64), :
+                pl.ds(pl.multiple_of(part_at * 16 + quad * 4, 4), 4),
+                pl.ds(pl.multiple_of(half_at * 64, 64), 64),
+                :,
             ].reshape(256, 128)
-            mid = dot_nn(mixing[...], outer[quad]) + dot_nt(eye, arriving) + bias
+            mid = dot_nn(mixing[...], outer[part_at * 4 + quad]) + dot_nt(eye, arriving) + bias
             mids.append(mid.astype(BF16).astype(F32))
         normeds = []
         for mid in mids:
@@ -225,52 +247,43 @@
             tile[pl.ds(pl.multiple_of(quad * 256, 256), 256), :] = turned
         return carry
 
-    lax.fori_loop(0, 8 // QUADS, some_rows, 0)
+    lax.fori_loop(0, 4 // QUADS, some_rows, 0)
 
     for group in range(8):
         for one in range(8):
-            values = tile[pl.ds(group * 8 + one, 32, stride=64), :].astype(BF16)
-            rows[group * 32 : (group + 1) * 32, one * 128 : (one + 1) * 128] = values
-    sent[...] = dot_nt(rows[...], bins[...]).astype(BF16)
-    keep[...] = sent[pl.ds(pl.multiple_of(core * 128, 128), 128), :]
-    give[...] = sent[pl.ds(pl.multiple_of((1 - core) * 128, 128), 128), :]
-
-
-def pair_call(meta, flip, chain_at, left_near, left_far, own, other, incoming, weights, so_far):
-    by_half = pl.BlockSpec((32, 64, 128), lambda g, m, k: (0, half_of(m[0], flip), 0))
-    operands = [left_near, left_far, own, other, chain_at.reshape(8, 128), incoming, *weights]
-    operands = [in_vmem(values) for values in operands]
+            values = tile[pl.ds(group * 8 + one, 16, stride=64), :].astype(BF16)
+            rows[group * 16 : (group + 1) * 16, one * 128 : (one + 1) * 128] = values
+    product = dot_nt(rows[...], bins[...]).astype(BF16).reshape(2, 4, 16, 512)
+    sent[core] = product[0]
+    sent[1 - core] = product[1]
+
+
+def rows_call(meta, flip, part_at, outer, incoming, weights, so_far):
+    block = pl.BlockSpec((16, 64, 128), lambda g, m: (part_at, half_of(m[0], flip), 0))
+    operands = [in_vmem(values) for values in (outer, incoming, *weights)]
     specs = [VMEM_SPEC] * len(operands)
     aliases = {}
     if so_far is not None:
         operands.append(so_far)
         specs.append(pl.BlockSpec(memory_space=pl.ANY))
-        aliases = {len(operands) + 1: 0}
+        aliases = {len(operands): 0}
     return pl.pallas_call(
-        functools.partial(pair_kernel, flip=flip),
+        functools.partial(rows_kernel, flip=flip, part_at=part_at),
         out_shape=(
             jax.ShapeDtypeStruct((32, 128, 128), BF16),
-            pltpu.VMEM((128, 512), BF16),
-            pltpu.VMEM((128, 512), BF16),
+            pltpu.VMEM((2, 4, 16, 512), BF16),
         ),
         grid_spec=pltpu.PrefetchScalarGridSpec(
-            num_scalar_prefetch=2,
+            num_scalar_prefetch=1,
             grid=(1,),
             in_specs=specs,
-            out_specs=(by_half, VMEM_SPEC, VMEM_SPEC),
-            scratch_shapes=[
-                pltpu.VMEM((2048, 128), F32),
-                pltpu.VMEM((512, 256), BF16),
-                pltpu.VMEM((8, 1024, 256), BF16),
-                pltpu.VMEM((2048, 128), F32),
-                pltpu.VMEM((256, 1024), BF16),
-                pltpu.VMEM((256, 512), BF16),
-            ],
+            out_specs=(block, VMEM_SPEC),
+            scratch_shapes=[pltpu.VMEM((1024, 128), F32), pltpu.VMEM((128, 1024), BF16)],
         ),
         input_output_aliases=aliases,
-        compiler_params=pltpu.CompilerParams(vmem_limit_bytes=24 << 20),
-        name="pair_half",
-    )(meta, chain_at, *operands)
+        compiler_params=pltpu.CompilerParams(vmem_limit_bytes=12 << 20),
+        name="rows_part",
+    )(meta, *operands)
 
 
 def own_kernel(tile, bins, bias, out):
@@ -292,16 +305,18 @@
     )(pair_out, in_vmem(bins), in_vmem(bias))
 
 
-def join_kernel(meta, own, near, far, out, block):
+def join_kernel(meta, own, *rest):
+    out, block = rest[-2:]
     b_at = lax.rem(meta[0], 4)
     step = pl.program_id(0)
     rows = pl.ds(pl.multiple_of(step * 8, 8), 8)
     eye = square_eye()
-    for source in range(4):
-        from_b = jnp.bitwise_xor(b_at, source)
-        at = pl.multiple_of(from_b * 32, 32)
-        values = near if source < 2 else far
-        block[pl.ds(at, 32), :] = values[source % 2, step]
+    for piece in range(4):
+        mine, partner = rest[piece * 2], rest[piece * 2 + 1]
+        for side, values in enumerate((mine, partner)):
+            from_b = jnp.bitwise_xor(b_at, (piece // 2) * 2 + side)
+            at = pl.multiple_of(from_b * 32 + (piece % 2) * 16, 16)
+            block[pl.ds(at, 16), :] = values[side, step]
     for part in range(4):
         turned = dot_nt(eye, block[:, part * 128 : (part + 1) * 128])
         out[part * 16 : (part + 1) * 16] = own[
@@ -309,20 +324,20 @@
         ] + turned.reshape(16, 8, 128)
 
 
-def join_call(meta, own, near, far):
+def join_call(meta, own, pieces):
     return pl.pallas_call(
         join_kernel,
         out_shape=jax.ShapeDtypeStruct((64, 32, 128), F32),
         grid_spec=pltpu.PrefetchScalarGridSpec(
             num_scalar_prefetch=1,
             grid=(4,),
-            in_specs=[VMEM_SPEC, VMEM_SPEC, VMEM_SPEC],
+            in_specs=[VMEM_SPEC] * 9,
             out_specs=pl.BlockSpec((64, 8, 128), lambda g, m: (0, g, 0)),
             scratch_shapes=[pltpu.VMEM((128, 512), BF16)],
         ),
         compiler_params=pltpu.CompilerParams(vmem_limit_bytes=16 << 20),
         name="join_bins",
-    )(meta, in_vmem(own), in_vmem(near), in_vmem(far))
+    )(meta, in_vmem(own), *[in_vmem(values) for values in pieces])
 
 
 def per_device(
@@ -369,24 +384,24 @@
     other = send(own, lambda a, b, c: (a, b ^ 1, c))
     own_far = send(own, lambda a, b, c: (a, b ^ 2, c))
 
-    pair_out, keep, give = pair_call(
-        meta, False, token_chain_index, left_near, left_far, own, other,
-        incoming_pair_state, weights, None,
-    )
-    other_far = send(own_far, lambda a, b, c: (a, b ^ 1, c))
-    given = send(give, lambda a, b, c: (a, b ^ 1, c))
-    near = send(jnp.stack([keep, given]), lambda a, b, c: (c, b, a))
-    pair_out, keep, give = pair_call(
-        meta, True, token_chain_index, left_near, left_far, own_far, other_far,
-        incoming_pair_state, weights, pair_out,
-    )
-    given = send(give, lambda a, b, c: (a, b ^ 1, c))
-    far = send(jnp.stack([keep, given]), lambda a, b, c: (c, b ^ 2, a))
+    pieces = []
+    pair_out = None
+    for flip in (False, True):
+        if flip:
+            other = send(own_far, lambda a, b, c: (a, b ^ 1, c))
+            own = own_far
+        outer = outer_call(meta, flip, token_chain_index, left_near, left_far, own, other)
+        for part_at in range(2):
+            pair_out, sent = rows_call(
+                meta, flip, part_at, outer, incoming_pair_state, weights, pair_out
+            )
+            pieces.append(send(sent, lambda a, b, c, x=2 * flip: (c, b ^ x, a)))
+    arrived = []
+    for piece in pieces:
+        arrived += [piece, send(piece, lambda a, b, c: (a, b ^ 1, c))]
 
     own_bins = own_call(pair_out, weights[3], bin_col)
-    logits = join_call(
-        meta, own_bins, near.reshape(2, 4, 32, 512), far.reshape(2, 4, 32, 512)
-    )
+    logits = join_call(meta, own_bins, arrived)
     return (pair_out, logits)
 
 

time: 150 us -> 131 us (0.87)
  the two profiles are of different devices: /device:TPU:227 before, /device:TPU:41 now
where the time goes in v2:
time: 131 us; the launch traced here: 130 us
  starting transfers between devices  78.3 us (60%)
  Pallas kernels  32 us (24%)
  waiting for transfers between devices  15.5 us (12%)
  local copies, waits for them, and re-layouts  1.97 us (2%)
  other arithmetic  1.64 us (1%)
    ppermute x19, starting transfers between devices, send(): return lax.ppermute(values, AXES, pairs)  78.3 us
    pallas_call x4, Pallas kernels, rows_call(): pl.pallas_call(functools.partial(rows_kernel, flip=flip, part_at=part_at)...  19.4 us
    ppermute x19, waiting for transfers between devices, send(): return lax.ppermute(values, AXES, pairs)  15.5 us
    pallas_call x2, Pallas kernels, outer_call(): pl.pallas_call(functools.partial(outer_kernel, flip=flip), out_shape=pltp...  5.94 us
    pallas_call x1, Pallas kernels, join_call(): pl.pallas_call(join_kernel, out_shape=jax.ShapeDtypeStruct((64, 32, 128),...  2.67 us
  transfers between devices with their start and end apart: 19, of which 8 were waited for; matrix products, arithmetic and copies ran while one was open for 1% of the time, Pallas kernels for 22%

profile of v2, /device:TPU:41, one launch (start us, length us, event | category | flops | bytes accessed | tf_op | source)
XLA Modules:
  0.0 130.2 jit_solution(7594202332695630427)
XLA Ops:
  0.6 0.0 copy-start
  0.6 6.0 %collective-permute-start.3 = (bf16[1,128,128]{2,1,0:T(8,128)(2,1)}, bf16[1,128,128]{2,1,0:T(8,128)(2,1)S(1)}, u32[]{:S(2)}, u32[]{:S(2)}) collective-permute-start(bf16[1,128,128]{2,1,0:T(8,128)(2,1)} %bitcast.22), channel_id=1, source_target_pairs={{0,0},{1,32},{2,64},{3,96},{4,128},{5,160},{6,192},{7,224},{8,8},{... | collective-permute-start | bytes 98312 | tf_op jit(solution)/shard_map/ppermute | solution.py:32
  6.7 2.5 %collective-permute-done.3 = bf16[1,128,128]{2,1,0:T(8,128)(2,1)S(1)} collective-permute-done((bf16[1,128,128]{2,1,0:T(8,128)(2,1)}, bf16[1,128,128]{2,1,0:T(8,128)(2,1)S(1)}, u32[]{:S(2)}, u32[]{:S(2)}) %collective-permute-start.3) | collective-permute-done | bytes 32800 | tf_op jit(solution)/shard_map/ppermute | solution.py:32
  9.2 0.0 collective-permute-start.4
  9.2 1.5 %collective-permute-start.5 = (bf16[1,128,128]{2,1,0:T(8,128)(2,1)S(1)}, bf16[1,128,128]{2,1,0:T(8,128)(2,1)S(1)}, u32[]{:S(2)}, u32[]{:S(2)}) collective-permute-start(bf16[1,128,128]{2,1,0:T(8,128)(2,1)S(1)} %collective-permute-done.3), channel_id=1, source_target_pairs={{0,224},{1,225},{2,226},{3,227},{4,228},{5,229},{6,230},{7,231},{8... | collective-permute-start | bytes 98312 | tf_op jit(solution)/shard_map/ppermute | solution.py:32
  10.6 1.4 %collective-permute-done.4 = bf16[1,128,128]{2,1,0:T(8,128)(2,1)S(1)} collective-permute-done((bf16[1,128,128]{2,1,0:T(8,128)(2,1)S(1)}, bf16[1,128,128]{2,1,0:T(8,128)(2,1)S(1)}, u32[]{:S(2)}, u32[]{:S(2)}) %collective-permute-start.4) | collective-permute-done | bytes 32800 | tf_op jit(solution)/shard_map/ppermute | solution.py:32
  12.1 0.5 collective-permute-done.5
  12.6 8.7 %collective-permute-start.6 = (bf16[3,128,128]{2,1,0:T(8,128)(2,1)S(1)}, bf16[3,128,128]{2,1,0:T(8,128)(2,1)S(1)}, u32[]{:S(2)}, u32[]{:S(2)}) collective-permute-start(bf16[3,128,128]{2,1,0:T(8,128)(2,1)S(1)} %pad_maximum_fusion.1), channel_id=1, source_target_pairs={{0,96},{1,97},{2,98},{3,99},{4,100},{5,101},{6,102},{7,103},{8,104... | collective-permute-start | bytes 294920 | tf_op jit(solution)/shard_map/ppermute | solution.py:32
  21.4 1.7 %collective-permute-start.7 = (bf16[2,128,128]{2,1,0:T(8,128)(2,1)S(1)}, bf16[2,128,128]{2,1,0:T(8,128)(2,1)S(1)}, u32[]{:S(2)}, u32[]{:S(2)}) collective-permute-start(bf16[2,128,128]{2,1,0:T(8,128)(2,1)S(1)} %pad_maximum_fusion.3), channel_id=1, source_target_pairs={{0,160},{1,161},{2,162},{3,163},{4,164},{5,165},{6,166},{7,167},{8... | collective-permute-start | bytes 196616 | tf_op jit(solution)/shard_map/ppermute | solution.py:32
  23.0 2.0 %collective-permute-done.6 = bf16[3,128,128]{2,1,0:T(8,128)(2,1)S(1)} collective-permute-done((bf16[3,128,128]{2,1,0:T(8,128)(2,1)S(1)}, bf16[3,128,128]{2,1,0:T(8,128)(2,1)S(1)}, u32[]{:S(2)}, u32[]{:S(2)}) %collective-permute-start.6) | collective-permute-done | bytes 98336 | tf_op jit(solution)/shard_map/ppermute | solution.py:32
  25.1 2.8 %collective-permute-done.7 = bf16[2,128,128]{2,1,0:T(8,128)(2,1)S(1)} collective-permute-done((bf16[2,128,128]{2,1,0:T(8,128)(2,1)S(1)}, bf16[2,128,128]{2,1,0:T(8,128)(2,1)S(1)}, u32[]{:S(2)}, u32[]{:S(2)}) %collective-permute-start.7) | collective-permute-done | bytes 65568 | tf_op jit(solution)/shard_map/ppermute | solution.py:32
  27.9 0.8 collective-permute-start.8
  28.7 3.4 %collective-permute-start = (bf16[1,128,128]{2,1,0:T(8,128)(2,1)}, bf16[1,128,128]{2,1,0:T(8,128)(2,1)S(1)}, u32[]{:S(2)}, u32[]{:S(2)}) collective-permute-start(bf16[1,128,128]{2,1,0:T(8,128)(2,1)} %bitcast.15), channel_id=1, source_target_pairs={{0,1},{1,0},{2,3},{3,2},{4,5},{5,4},{6,7},{7,6},{8,9},{9,8},{10,11... | collective-permute-start | bytes 98312 | tf_op jit(solution)/shard_map/ppermute | solution.py:32
  32.1 4.1 %collective-permute-done = bf16[1,128,128]{2,1,0:T(8,128)(2,1)S(1)} collective-permute-done((bf16[1,128,128]{2,1,0:T(8,128)(2,1)}, bf16[1,128,128]{2,1,0:T(8,128)(2,1)S(1)}, u32[]{:S(2)}, u32[]{:S(2)}) %collective-permute-start) | collective-permute-done | bytes 32800 | tf_op jit(solution)/shard_map/ppermute | solution.py:32
  36.2 0.8 pad_maximum_fusion.2
  37.0 1.6 %collective-permute-start.1 = (bf16[2,128,128]{2,1,0:T(8,128)(2,1)S(1)}, bf16[2,128,128]{2,1,0:T(8,128)(2,1)S(1)}, u32[]{:S(2)}, u32[]{:S(2)}) collective-permute-start(bf16[2,128,128]{2,1,0:T(8,128)(2,1)S(1)} %pad_maximum_fusion.2), channel_id=1, source_target_pairs={{0,4},{1,5},{2,6},{3,7},{4,0},{5,1},{6,2},{7,3},{8,12},{9,13},{10,... | collective-permute-start | bytes 196616 | tf_op jit(solution)/shard_map/ppermute | solution.py:32
  38.6 5.3 %collective-permute-start.10 = (bf16[8,128,128]{2,1,0:T(8,128)(2,1)S(1)}, bf16[8,128,128]{2,1,0:T(8,128)(2,1)S(1)}, u32[]{:S(2)}, u32[]{:S(2)}) collective-permute-start(bf16[8,128,128]{2,1,0:T(8,128)(2,1)S(1)} %constant_dynamic-update-slice_fusion.right_own), channel_id=1, source_target_pairs={{0,8},{1,9},{2,10},{3,11},{4,12},{5,13},{6,14},{7,15},{8,0},{9,1},... | collective-permute-start | bytes 786440 | tf_op jit(solution)/shard_map/ppermute | solution.py:32
  43.8 0.0 collective-permute-done.8.right_own
  43.8 0.0 collective-permute-start.9
  43.9 0.0 collective-permute-done.1
  43.9 0.8 pad_maximum_fusion.left_near
  44.6 1.6 %collective-permute-start.2 = (bf16[4,128,128]{2,1,0:T(8,128)(2,1)S(1)}, bf16[4,128,128]{2,1,0:T(8,128)(2,1)S(1)}, u32[]{:S(2)}, u32[]{:S(2)}) collective-permute-start(bf16[4,128,128]{2,1,0:T(8,128)(2,1)S(1)} %pad_maximum_fusion.left_near), channel_id=1, source_target_pairs={{0,2},{1,3},{2,0},{3,1},{4,6},{5,7},{6,4},{7,5},{8,10},{9,11},{10,... | collective-permute-start | bytes 393224 | tf_op jit(solution)/shard_map/ppermute | solution.py:32
  46.2 2.1 %prep.1 = (bf16[128,1024]{1,0:T(8,128)(2,1)S(1)}, bf16[1024,128]{1,0:T(8,128)(2,1)S(1)}, bf16[128,512]{1,0:T(8,128)(2,1)S(1)}, bf16[512,1024]{1,0:T(8,128)(2,1)S...) custom-call(bf16[1024,128]{1,0:T(8,128)(2,1)} %mix.1, bf16[128,512]{1,0:T(8,128)(2,1)} %gate.1, ...), custom_call_target="tpu_custom_call" | custom-call | tf_op jit(solution)/shard_map/prep/pallas_call | solution.py:77
  48.4 0.1 pad_add_fusion.meta
  48.4 0.1 collective-permute-done.2.left_far
  48.6 0.0 collective-permute-done.10.right_other
  48.6 0.0 copy-start.2
  48.6 0.7 copy-done.2
  49.3 3.0 %outer_half.3.outer = bf16[8,1024,256]{2,1,0:T(8,128)(2,1)S(1)} custom-call(s32[2]{0:T(128)S(1)} %pad_add_fusion.meta, s32[1024]{0:T(1024)S(1)} %copy-done.2, bf16[4,128,128]{2,1,0:T(8,128)(2,1)S(1)} %pad_maximum_fusion.left_near, bf16[4,128,128]{2,1,0:T(8,128)(2,1)S(1)} %collective-permute-done.2.left_far, ...), custom_call_target="tpu_custom_call" | custom-call | tf_op jit(solution)/shard_map/outer_half/pallas_call | solution.py:193
  52.2 0.0 copy-done
  52.3 4.8 %rows_part.4 = (bf16[32,128,128]{2,1,0:T(8,128)(2,1)}, bf16[2,4,16,512]{3,2,1,0:T(8,128)(2,1)S(1)}) custom-call(s32[2]{0:T(128)S(1)} %pad_add_fusion.meta, bf16[8,1024,256]{2,1,0:T(8,128)(2,1)S(1)} %outer_half.3.outer, bf16[32,128,128]{2,1,0:T(8,128)(2,1)S(1)} %copy-done, bf16[128,1024]{1,0:T(8,128)(2,1)S(1)} %get-tuple-element.17.mixing, ...), custom_call_target="tpu_custom_call" | custom-call | tf_op jit(solution)/shard_map/rows_part/pallas_call | solution.py:270
  57.1 4.8 %rows_part.5 = (bf16[32,128,128]{2,1,0:T(8,128)(2,1)}, bf16[2,4,16,512]{3,2,1,0:T(8,128)(2,1)S(1)}) custom-call(s32[2]{0:T(128)S(1)} %pad_add_fusion.meta, bf16[8,1024,256]{2,1,0:T(8,128)(2,1)S(1)} %outer_half.3.outer, bf16[32,128,128]{2,1,0:T(8,128)(2,1)S(1)} %copy-done, ...), custom_call_target="tpu_custom_call", output_to_operand_aliasing={{0}: (9, {})} | custom-call | tf_op jit(solution)/shard_map/rows_part/pallas_call | solution.py:270
  62.0 3.4 %collective-permute-start.13 = (bf16[2,4,16,512]{3,2,1,0:T(8,128)(2,1)S(1)}, bf16[2,4,16,512]{3,2,1,0:T(8,128)(2,1)S(1)}, u32[]{:S(2)}, u32[]{:S(2)}) collective-permute-start(bf16[2,4,16,512]{3,2,1,0:T(8,128)(2,1)S(1)} %get-tuple-element.29), channel_id=1, source_target_pairs={{0,0},{1,32},{2,64},{3,96},{4,128},{5,160},{6,192},{7,224},{8,8},{... | collective-permute-start | bytes 393224 | tf_op jit(solution)/shard_map/ppermute | solution.py:32
  65.4 5.3 %collective-permute-start.11 = (bf16[2,4,16,512]{3,2,1,0:T(8,128)(2,1)S(1)}, bf16[2,4,16,512]{3,2,1,0:T(8,128)(2,1)S(1)}, u32[]{:S(2)}, u32[]{:S(2)}) collective-permute-start(bf16[2,4,16,512]{3,2,1,0:T(8,128)(2,1)S(1)} %get-tuple-element.28), channel_id=1, source_target_pairs={{0,0},{1,32},{2,64},{3,96},{4,128},{5,160},{6,192},{7,224},{8,8},{... | collective-permute-start | bytes 393224 | tf_op jit(solution)/shard_map/ppermute | solution.py:32
  70.7 0.0 collective-permute-done.9.right_other
  70.7 3.0 %outer_half.2.outer = bf16[8,1024,256]{2,1,0:T(8,128)(2,1)S(1)} custom-call(s32[2]{0:T(128)S(1)} %pad_add_fusion.meta, s32[1024]{0:T(1024)S(1)} %copy-done.2, bf16[4,128,128]{2,1,0:T(8,128)(2,1)S(1)} %pad_maximum_fusion.left_near, bf16[4,128,128]{2,1,0:T(8,128)(2,1)S(1)} %collective-permute-done.2.left_far, ...), custom_call_target="tpu_custom_call" | custom-call | tf_op jit(solution)/shard_map/outer_half/pallas_call | solution.py:193
  73.7 4.9 %rows_part.6 = (bf16[32,128,128]{2,1,0:T(8,128)(2,1)}, bf16[2,4,16,512]{3,2,1,0:T(8,128)(2,1)S(1)}) custom-call(s32[2]{0:T(128)S(1)} %pad_add_fusion.meta, bf16[8,1024,256]{2,1,0:T(8,128)(2,1)S(1)} %outer_half.2.outer, bf16[32,128,128]{2,1,0:T(8,128)(2,1)S(1)} %copy-done, ...), custom_call_target="tpu_custom_call", output_to_operand_aliasing={{0}: (9, {})} | custom-call | tf_op jit(solution)/shard_map/rows_part/pallas_call | solution.py:270
  78.6 4.8 %rows_part.7 = (bf16[32,128,128]{2,1,0:T(8,128)(2,1)}, bf16[2,4,16,512]{3,2,1,0:T(8,128)(2,1)S(1)}) custom-call(s32[2]{0:T(128)S(1)} %pad_add_fusion.meta, bf16[8,1024,256]{2,1,0:T(8,128)(2,1)S(1)} %outer_half.2.outer, bf16[32,128,128]{2,1,0:T(8,128)(2,1)S(1)} %copy-done, ...), custom_call_target="tpu_custom_call", output_to_operand_aliasing={{0}: (9, {})} | custom-call | tf_op jit(solution)/shard_map/rows_part/pallas_call | solution.py:270
  83.4 7.2 %collective-permute-start.17 = (bf16[2,4,16,512]{3,2,1,0:T(8,128)(2,1)S(1)}, bf16[2,4,16,512]{3,2,1,0:T(8,128)(2,1)S(1)}, u32[]{:S(2)}, u32[]{:S(2)}) collective-permute-start(bf16[2,4,16,512]{3,2,1,0:T(8,128)(2,1)S(1)} %get-tuple-element.31), channel_id=1, source_target_pairs={{0,16},{1,48},{2,80},{3,112},{4,144},{5,176},{6,208},{7,240},{8,24... | collective-permute-start | bytes 393224 | tf_op jit(solution)/shard_map/ppermute | solution.py:32
  90.6 0.0 collective-permute-start.15
  90.6 0.0 collective-permute-done.13.rest_2_
  90.6 4.8 %collective-permute-start.14 = (bf16[2,4,16,512]{3,2,1,0:T(8,128)(2,1)S(1)}, bf16[2,4,16,512]{3,2,1,0:T(8,128)(2,1)S(1)}, u32[]{:S(2)}, u32[]{:S(2)}) collective-permute-start(bf16[2,4,16,512]{3,2,1,0:T(8,128)(2,1)S(1)} %collective-permute-done.13.rest_2_), channel_id=1, source_target_pairs={{0,8},{1,9},{2,10},{3,11},{4,12},{5,13},{6,14},{7,15},{8,0},{9,1},... | collective-permute-start | bytes 393224 | tf_op jit(solution)/shard_map/ppermute | solution.py:32
  95.4 0.0 collective-permute-done.11.rest_0_
  95.4 18.9 %collective-permute-start.12 = (bf16[2,4,16,512]{3,2,1,0:T(8,128)(2,1)S(1)}, bf16[2,4,16,512]{3,2,1,0:T(8,128)(2,1)S(1)}, u32[]{:S(2)}, u32[]{:S(2)}) collective-permute-start(bf16[2,4,16,512]{3,2,1,0:T(8,128)(2,1)S(1)} %collective-permute-done.11.rest_0_), channel_id=1, source_target_pairs={{0,8},{1,9},{2,10},{3,11},{4,12},{5,13},{6,14},{7,15},{8,0},{9,1},... | collective-permute-start | bytes 393224 | tf_op jit(solution)/shard_map/ppermute | solution.py:32
  114.3 2.0 %collective-permute-done.17.rest_6_ = bf16[2,4,16,512]{3,2,1,0:T(8,128)(2,1)S(1)} collective-permute-done((bf16[2,4,16,512]{3,2,1,0:T(8,128)(2,1)S(1)}, bf16[2,4,16,512]{3,2,1,0:T(8,128)(2,1)S(1)}, u32[]{:S(2)}, u32[]{:S(2)}) %collective-permute-start.17) | collective-permute-done | bytes 131104 | tf_op jit(solution)/shard_map/ppermute | solution.py:32
  116.3 6.7 %collective-permute-start.18 = (bf16[2,4,16,512]{3,2,1,0:T(8,128)(2,1)S(1)}, bf16[2,4,16,512]{3,2,1,0:T(8,128)(2,1)S(1)}, u32[]{:S(2)}, u32[]{:S(2)}) collective-permute-start(bf16[2,4,16,512]{3,2,1,0:T(8,128)(2,1)S(1)} %collective-permute-done.17.rest_6_), channel_id=1, source_target_pairs={{0,8},{1,9},{2,10},{3,11},{4,12},{5,13},{6,14},{7,15},{8,0},{9,1},... | collective-permute-start | bytes 393224 | tf_op jit(solution)/shard_map/ppermute | solution.py:32
  123.0 0.0 collective-permute-done.15.rest_4_
  123.0 1.4 %collective-permute-start.16 = (bf16[2,4,16,512]{3,2,1,0:T(8,128)(2,1)S(1)}, bf16[2,4,16,512]{3,2,1,0:T(8,128)(2,1)S(1)}, u32[]{:S(2)}, u32[]{:S(2)}) collective-permute-start(bf16[2,4,16,512]{3,2,1,0:T(8,128)(2,1)S(1)} %collective-permute-done.15.rest_4_), channel_id=1, source_target_pairs={{0,8},{1,9},{2,10},{3,11},{4,12},{5,13},{6,14},{7,15},{8,0},{9,1},... | collective-permute-start | bytes 393224 | tf_op jit(solution)/shard_map/ppermute | solution.py:32
  124.4 0.0 copy-start.1
  124.4 1.2 copy-done.1
  125.7 1.8 %own_bins.1.own = f32[64,32,128]{2,1,0:T(8,128)S(1)} custom-call(bf16[32,128,128]{2,1,0:T(8,128)(2,1)S(1)} %copy-done.1, bf16[512,1024]{1,0:T(8,128)(2,1)S(1)} %get-tuple-element.20.bins, f32[64,128]{1,0:T(8,128)S(1)} %get-tuple-element.27.bias), custom_call_target="tpu_custom_call" | custom-call | tf_op jit(solution)/shard_map/own_bins/pallas_call | solution.py:297
  127.5 0.0 collective-permute-done.14.rest_3_
  127.5 0.0 collective-permute-done.12.rest_1_
  127.5 0.0 collective-permute-done.18.rest_7_
  127.5 0.0 collective-permute-done.16.rest_5_
  127.5 2.7 %join_bins.1 = f32[64,32,128]{2,1,0:T(8,128)} custom-call(s32[2]{0:T(128)S(1)} %pad_add_fusion.meta, f32[64,32,128]{2,1,0:T(8,128)S(1)} %own_bins.1.own, bf16[2,4,16,512]{3,2,1,0:T(8,128)(2,1)S(1)} %collective-permute-done.11.rest_0_, bf16[2,4,16,512]{3,2,1,0:T(8,128)(2,1)S(1)} %collective-permute-done.12.rest_1_, ...), custom_call_target="tpu_custom_call" | custom-call | tf_op jit(solution)/shard_map/join_bins/pallas_call | solution.py:328
  (7 shorter events, 0.1 us)
Async XLA Ops:
  0.6 51.6 %copy-start = (bf16[32,128,128]{2,1,0:T(8,128)(2,1)S(1)}, bf16[32,128,128]{2,1,0:T(8,128)(2,1)}, u32[]{:S(2)}) copy-start(bf16[32,128,128]{2,1,0:T(8,128)(2,1)} %incoming.7) | copy-start | bytes 3145732
  0.6 8.5 %collective-permute-start.3 = (bf16[1,128,128]{2,1,0:T(8,128)(2,1)}, bf16[1,128,128]{2,1,0:T(8,128)(2,1)S(1)}, u32[]{:S(2)}, u32[]{:S(2)}) collective-permute-start(bf16[1,128,128]{2,1,0:T(8,128)(2,1)} %bitcast.22), channel_id=1, source_target_pairs={{0,0},{1,32},{2,64},{3,96},{4,128},{5,160},{6,192},{7,224},{8,8},{... | collective-permute-start | bytes 98312 | tf_op jit(solution)/shard_map/ppermute | solution.py:32
  9.2 2.9 %collective-permute-start.4 = (bf16[1,128,128]{2,1,0:T(8,128)(2,1)S(1)}, bf16[1,128,128]{2,1,0:T(8,128)(2,1)S(1)}, u32[]{:S(2)}, u32[]{:S(2)}) collective-permute-start(bf16[1,128,128]{2,1,0:T(8,128)(2,1)S(1)} %collective-permute-done.3), channel_id=1, source_target_pairs={{0,32},{1,33},{2,34},{3,35},{4,36},{5,37},{6,38},{7,39},{8,40},{9,... | collective-permute-start | bytes 98312 | tf_op jit(solution)/shard_map/ppermute | solution.py:32
  9.2 3.5 %collective-permute-start.5 = (bf16[1,128,128]{2,1,0:T(8,128)(2,1)S(1)}, bf16[1,128,128]{2,1,0:T(8,128)(2,1)S(1)}, u32[]{:S(2)}, u32[]{:S(2)}) collective-permute-start(bf16[1,128,128]{2,1,0:T(8,128)(2,1)S(1)} %collective-permute-done.3), channel_id=1, source_target_pairs={{0,224},{1,225},{2,226},{3,227},{4,228},{5,229},{6,230},{7,231},{8... | collective-permute-start | bytes 98312 | tf_op jit(solution)/shard_map/ppermute | solution.py:32
  12.6 12.4 %collective-permute-start.6 = (bf16[3,128,128]{2,1,0:T(8,128)(2,1)S(1)}, bf16[3,128,128]{2,1,0:T(8,128)(2,1)S(1)}, u32[]{:S(2)}, u32[]{:S(2)}) collective-permute-start(bf16[3,128,128]{2,1,0:T(8,128)(2,1)S(1)} %pad_maximum_fusion.1), channel_id=1, source_target_pairs={{0,96},{1,97},{2,98},{3,99},{4,100},{5,101},{6,102},{7,103},{8,104... | collective-permute-start | bytes 294920 | tf_op jit(solution)/shard_map/ppermute | solution.py:32
  21.4 6.5 %collective-permute-start.7 = (bf16[2,128,128]{2,1,0:T(8,128)(2,1)S(1)}, bf16[2,128,128]{2,1,0:T(8,128)(2,1)S(1)}, u32[]{:S(2)}, u32[]{:S(2)}) collective-permute-start(bf16[2,128,128]{2,1,0:T(8,128)(2,1)S(1)} %pad_maximum_fusion.3), channel_id=1, source_target_pairs={{0,160},{1,161},{2,162},{3,163},{4,164},{5,165},{6,166},{7,167},{8... | collective-permute-start | bytes 196616 | tf_op jit(solution)/shard_map/ppermute | solution.py:32
  27.9 16.0 %collective-permute-start.8 = (bf16[8,128,128]{2,1,0:T(8,128)(2,1)S(1)}, bf16[8,128,128]{2,1,0:T(8,128)(2,1)S(1)}, u32[]{:S(2)}, u32[]{:S(2)}) collective-permute-start(bf16[8,128,128]{2,1,0:T(8,128)(2,1)S(1)} %constant_dynamic-update-slice_fusion.right_own), channel_id=1, source_target_pairs={{0,16},{1,17},{2,18},{3,19},{4,20},{5,21},{6,22},{7,23},{8,24},{9,... | collective-permute-start | bytes 786440 | tf_op jit(solution)/shard_map/ppermute | solution.py:32
  28.7 7.5 %collective-permute-start = (bf16[1,128,128]{2,1,0:T(8,128)(2,1)}, bf16[1,128,128]{2,1,0:T(8,128)(2,1)S(1)}, u32[]{:S(2)}, u32[]{:S(2)}) collective-permute-start(bf16[1,128,128]{2,1,0:T(8,128)(2,1)} %bitcast.15), channel_id=1, source_target_pairs={{0,1},{1,0},{2,3},{3,2},{4,5},{5,4},{6,7},{7,6},{8,9},{9,8},{10,11... | collective-permute-start | bytes 98312 | tf_op jit(solution)/shard_map/ppermute | solution.py:32
  37.0 6.9 %collective-permute-start.1 = (bf16[2,128,128]{2,1,0:T(8,128)(2,1)S(1)}, bf16[2,128,128]{2,1,0:T(8,128)(2,1)S(1)}, u32[]{:S(2)}, u32[]{:S(2)}) collective-permute-start(bf16[2,128,128]{2,1,0:T(8,128)(2,1)S(1)} %pad_maximum_fusion.2), channel_id=1, source_target_pairs={{0,4},{1,5},{2,6},{3,7},{4,0},{5,1},{6,2},{7,3},{8,12},{9,13},{10,... | collective-permute-start | bytes 196616 | tf_op jit(solution)/shard_map/ppermute | solution.py:32
  38.6 10.0 %collective-permute-start.10 = (bf16[8,128,128]{2,1,0:T(8,128)(2,1)S(1)}, bf16[8,128,128]{2,1,0:T(8,128)(2,1)S(1)}, u32[]{:S(2)}, u32[]{:S(2)}) collective-permute-start(bf16[8,128,128]{2,1,0:T(8,128)(2,1)S(1)} %constant_dynamic-update-slice_fusion.right_own), channel_id=1, source_target_pairs={{0,8},{1,9},{2,10},{3,11},{4,12},{5,13},{6,14},{7,15},{8,0},{9,1},... | collective-permute-start | bytes 786440 | tf_op jit(solution)/shard_map/ppermute | solution.py:32
  43.8 26.9 %collective-permute-start.9 = (bf16[8,128,128]{2,1,0:T(8,128)(2,1)S(1)}, bf16[8,128,128]{2,1,0:T(8,128)(2,1)S(1)}, u32[]{:S(2)}, u32[]{:S(2)}) collective-permute-start(bf16[8,128,128]{2,1,0:T(8,128)(2,1)S(1)} %collective-permute-done.8.right_own), channel_id=1, source_target_pairs={{0,8},{1,9},{2,10},{3,11},{4,12},{5,13},{6,14},{7,15},{8,0},{9,1},... | collective-permute-start | bytes 786440 | tf_op jit(solution)/shard_map/ppermute | solution.py:32
  44.6 3.9 %collective-permute-start.2 = (bf16[4,128,128]{2,1,0:T(8,128)(2,1)S(1)}, bf16[4,128,128]{2,1,0:T(8,128)(2,1)S(1)}, u32[]{:S(2)}, u32[]{:S(2)}) collective-permute-start(bf16[4,128,128]{2,1,0:T(8,128)(2,1)S(1)} %pad_maximum_fusion.left_near), channel_id=1, source_target_pairs={{0,2},{1,3},{2,0},{3,1},{4,6},{5,7},{6,4},{7,5},{8,10},{9,11},{10,... | collective-permute-start | bytes 393224 | tf_op jit(solution)/shard_map/ppermute | solution.py:32
  48.6 0.7 copy-start.2
  62.0 28.7 %collective-permute-start.13 = (bf16[2,4,16,512]{3,2,1,0:T(8,128)(2,1)S(1)}, bf16[2,4,16,512]{3,2,1,0:T(8,128)(2,1)S(1)}, u32[]{:S(2)}, u32[]{:S(2)}) collective-permute-start(bf16[2,4,16,512]{3,2,1,0:T(8,128)(2,1)S(1)} %get-tuple-element.29), channel_id=1, source_target_pairs={{0,0},{1,32},{2,64},{3,96},{4,128},{5,160},{6,192},{7,224},{8,8},{... | collective-permute-start | bytes 393224 | tf_op jit(solution)/shard_map/ppermute | solution.py:32
  65.4 30.1 %collective-permute-start.11 = (bf16[2,4,16,512]{3,2,1,0:T(8,128)(2,1)S(1)}, bf16[2,4,16,512]{3,2,1,0:T(8,128)(2,1)S(1)}, u32[]{:S(2)}, u32[]{:S(2)}) collective-permute-start(bf16[2,4,16,512]{3,2,1,0:T(8,128)(2,1)S(1)} %get-tuple-element.28), channel_id=1, source_target_pairs={{0,0},{1,32},{2,64},{3,96},{4,128},{5,160},{6,192},{7,224},{8,8},{... | collective-permute-start | bytes 393224 | tf_op jit(solution)/shard_map/ppermute | solution.py:32
  83.4 32.9 %collective-permute-start.17 = (bf16[2,4,16,512]{3,2,1,0:T(8,128)(2,1)S(1)}, bf16[2,4,16,512]{3,2,1,0:T(8,128)(2,1)S(1)}, u32[]{:S(2)}, u32[]{:S(2)}) collective-permute-start(bf16[2,4,16,512]{3,2,1,0:T(8,128)(2,1)S(1)} %get-tuple-element.31), channel_id=1, source_target_pairs={{0,16},{1,48},{2,80},{3,112},{4,144},{5,176},{6,208},{7,240},{8,24... | collective-permute-start | bytes 393224 | tf_op jit(solution)/shard_map/ppermute | solution.py:32
  90.6 32.4 %collective-permute-start.15 = (bf16[2,4,16,512]{3,2,1,0:T(8,128)(2,1)S(1)}, bf16[2,4,16,512]{3,2,1,0:T(8,128)(2,1)S(1)}, u32[]{:S(2)}, u32[]{:S(2)}) collective-permute-start(bf16[2,4,16,512]{3,2,1,0:T(8,128)(2,1)S(1)} %get-tuple-element.30), channel_id=1, source_target_pairs={{0,16},{1,48},{2,80},{3,112},{4,144},{5,176},{6,208},{7,240},{8,24... | collective-permute-start | bytes 393224 | tf_op jit(solution)/shard_map/ppermute | solution.py:32
  90.6 36.8 %collective-permute-start.14 = (bf16[2,4,16,512]{3,2,1,0:T(8,128)(2,1)S(1)}, bf16[2,4,16,512]{3,2,1,0:T(8,128)(2,1)S(1)}, u32[]{:S(2)}, u32[]{:S(2)}) collective-permute-start(bf16[2,4,16,512]{3,2,1,0:T(8,128)(2,1)S(1)} %collective-permute-done.13.rest_2_), channel_id=1, source_target_pairs={{0,8},{1,9},{2,10},{3,11},{4,12},{5,13},{6,14},{7,15},{8,0},{9,1},... | collective-permute-start | bytes 393224 | tf_op jit(solution)/shard_map/ppermute | solution.py:32
  95.4 32.0 %collective-permute-start.12 = (bf16[2,4,16,512]{3,2,1,0:T(8,128)(2,1)S(1)}, bf16[2,4,16,512]{3,2,1,0:T(8,128)(2,1)S(1)}, u32[]{:S(2)}, u32[]{:S(2)}) collective-permute-start(bf16[2,4,16,512]{3,2,1,0:T(8,128)(2,1)S(1)} %collective-permute-done.11.rest_0_), channel_id=1, source_target_pairs={{0,8},{1,9},{2,10},{3,11},{4,12},{5,13},{6,14},{7,15},{8,0},{9,1},... | collective-permute-start | bytes 393224 | tf_op jit(solution)/shard_map/ppermute | solution.py:32
  116.3 11.2 %collective-permute-start.18 = (bf16[2,4,16,512]{3,2,1,0:T(8,128)(2,1)S(1)}, bf16[2,4,16,512]{3,2,1,0:T(8,128)(2,1)S(1)}, u32[]{:S(2)}, u32[]{:S(2)}) collective-permute-start(bf16[2,4,16,512]{3,2,1,0:T(8,128)(2,1)S(1)} %collective-permute-done.17.rest_6_), channel_id=1, source_target_pairs={{0,8},{1,9},{2,10},{3,11},{4,12},{5,13},{6,14},{7,15},{8,0},{9,1},... | collective-permute-start | bytes 393224 | tf_op jit(solution)/shard_map/ppermute | solution.py:32
  123.0 4.5 %collective-permute-start.16 = (bf16[2,4,16,512]{3,2,1,0:T(8,128)(2,1)S(1)}, bf16[2,4,16,512]{3,2,1,0:T(8,128)(2,1)S(1)}, u32[]{:S(2)}, u32[]{:S(2)}) collective-permute-start(bf16[2,4,16,512]{3,2,1,0:T(8,128)(2,1)S(1)} %collective-permute-done.15.rest_4_), channel_id=1, source_target_pairs={{0,8},{1,9},{2,10},{3,11},{4,12},{5,13},{6,14},{7,15},{8,0},{9,1},... | collective-permute-start | bytes 393224 | tf_op jit(solution)/shard_map/ppermute | solution.py:32
  124.4 1.2 copy-start.1

commit v3 on v2

--- a/solution.py
+++ b/solution.py
@@ -13,7 +13,6 @@
 BF16 = jnp.bfloat16
 DEVICES = [(a, b, c) for a in range(8) for b in range(4) for c in range(8)]
 COL_MASKS = (0, 1, 4, 5, 2, 3, 6, 7)
-QUADS = 2
 
 
 def in_vmem(values):
@@ -51,9 +50,10 @@
 
 
 def prep_kernel(
-    mix, gate, up, down_w, bins_w, outer_bias, gain, bin_bias,
-    mixing, gate_up, down, bins, bias_col, gain_col, bin_col, wide,
+    mix, gate, up, down_w, bins_w, outer_bias, gain, bin_bias, chain_in,
+    mixing, gate_up, down, bins, bias_col, gain_col, bin_col, chains, wide,
 ):
+    chains[...] = chain_in[...]
     wide[...] = mix[...].astype(F32)
     for block in range(8):
         parts = [wide[pl.ds(block * 4 + d, 32, stride=32), :] for d in range(4)]
@@ -72,8 +72,9 @@
     bin_col[...] = turn(jnp.broadcast_to(bin_bias[...], (128, 64)))
 
 
-def prep_call(mix, gate, up, down, bins, outer_bias, gain, bin_bias):
+def prep_call(mix, gate, up, down, bins, outer_bias, gain, bin_bias, chain_at):
     operands = (mix, gate, up, down, bins.T, outer_bias[None], gain[None], bin_bias[None])
+    operands += (chain_at.reshape(8, 128),)
     return pl.pallas_call(
         prep_kernel,
         out_shape=(
@@ -84,8 +85,9 @@
             pltpu.VMEM((128, 128), F32),
             pltpu.VMEM((128, 128), F32),
             pltpu.VMEM((64, 128), F32),
+            pltpu.VMEM((8, 128), jnp.int32),
         ),
-        out_specs=[VMEM_SPEC] * 7,
+        out_specs=[VMEM_SPEC] * 8,
         scratch_shapes=[pltpu.VMEM((1024, 128), F32)],
         compiler_params=pltpu.CompilerParams(vmem_limit_bytes=16 << 20),
         name="prep",
@@ -108,6 +110,7 @@
     outer,
     right,
     left,
+    packed,
     *,
     flip,
 ):
@@ -146,7 +149,7 @@
             same,
             F32(1.0 / 128.0),
             jnp.where(paired, F32(1.0 / 64.0), F32(0.0)),
-        )
+        ).astype(BF16)
 
         def channels(step, inner):
             weights = []
@@ -154,7 +157,13 @@
                 blocks = []
                 for half in range(2):
                     d = step * (2 * unroll) + pair * 2 + half
-                    values = (right[pl.ds(d, 64, stride=32), :] * scale).astype(BF16)
+                    at = pl.multiple_of(d * 64, 64)
+                    if window is None:
+                        values = right[pl.ds(d, 64, stride=32), :].astype(BF16)
+                        packed[pl.ds(at, 64), :] = values
+                    else:
+                        values = packed[pl.ds(at, 64), :]
+                    values = values * scale
                     blocks.append(jnp.concatenate([values, zeros], 1))
                     blocks.append(jnp.concatenate([zeros, values], 1))
                 weights.append(jnp.concatenate(blocks, 0))
@@ -182,14 +191,14 @@
 
     def more_chains(step, carry):
         chain = step + (step >= main_chain).astype(jnp.int32)
-        one_chain(chain, (chain > main_chain).astype(jnp.int32), 2)
+        one_chain(chain, (chain > main_chain).astype(jnp.int32), 4)
         return carry
 
     lax.fori_loop(first_chain, last_chain, more_chains, 0)
 
 
-def outer_call(meta, flip, chain_at, left_near, left_far, own, other):
-    operands = [left_near, left_far, own, other, chain_at.reshape(8, 128)]
+def outer_call(meta, flip, chain_at, chains, left_near, left_far, own, other):
+    operands = [left_near, left_far, own, other, chains]
     return pl.pallas_call(
         functools.partial(outer_kernel, flip=flip),
         out_shape=pltpu.VMEM((8, 1024, 256), BF16),
@@ -198,11 +207,19 @@
             grid=(1,),
             in_specs=[VMEM_SPEC] * len(operands),
             out_specs=VMEM_SPEC,
-            scratch_shapes=[pltpu.VMEM((2048, 128), F32), pltpu.VMEM((512, 256), BF16)],
+            scratch_shapes=[
+                pltpu.VMEM((2048, 128), F32),
+                pltpu.VMEM((512, 256), BF16),
+                pltpu.VMEM((2048, 128), BF16),
+            ],
         ),
         compiler_params=pltpu.CompilerParams(vmem_limit_bytes=12 << 20),
         name="outer_half",
-    )(meta, chain_at, *[in_vmem(values) for values in operands])
+    )(
+        meta,
+        pltpu.with_memory_space_constraint(chain_at, pltpu.HBM),
+        *[in_vmem(values) for values in operands],
+    )
 
 
 def rows_kernel(
@@ -216,38 +233,50 @@
     bias = jnp.concatenate([bias_col[...], bias_col[...]], 1)
     scale_by = jnp.concatenate([gain_col[...], gain_col[...]], 1)
 
-    def some_rows(step, carry):
-        quads = [step * QUADS + q for q in range(QUADS)]
-        mids = []
-        for quad in quads:
-            arriving = incoming[
-                pl.ds(pl.multiple_of(part_at * 16 + quad * 4, 4), 4),
-                pl.ds(pl.multiple_of(half_at * 64, 64), 64),
-                :,
-            ].reshape(256, 128)
-            mid = dot_nn(mixing[...], outer[part_at * 4 + quad]) + dot_nt(eye, arriving) + bias
-            mids.append(mid.astype(BF16).astype(F32))
-        normeds = []
-        for mid in mids:
-            center = jnp.sum(mid, axis=0, keepdims=True) * F32(1.0 / 128.0)
-            shifted = mid - center
-            spread = jnp.sum(shifted * shifted, axis=0, keepdims=True) * F32(1.0 / 128.0)
-            normeds.append((shifted * lax.rsqrt(spread + F32(1e-05)) * scale_by).astype(BF16))
-        results = list(mids)
-        for part in range(2):
-            for q in range(QUADS):
-                gate = dot_nn(gate_up[part * 256 : (part + 1) * 256, :], normeds[q])
-                up = dot_nn(gate_up[512 + part * 256 : 512 + (part + 1) * 256, :], normeds[q])
-                half_gate = gate * F32(0.5)
-                hidden = ((half_gate + half_gate * jnp.tanh(half_gate)) * up).astype(BF16)
-                results[q] = results[q] + dot_nn(down[:, part * 256 : (part + 1) * 256], hidden)
-        for q, quad in enumerate(quads):
-            turned = turn(results[q].astype(BF16))
-            out[pl.ds(pl.multiple_of(quad * 4, 4), 4)] = turned.astype(BF16).reshape(4, 64, 128)
-            tile[pl.ds(pl.multiple_of(quad * 256, 256), 256), :] = turned
-        return carry
-
-    lax.fori_loop(0, 4 // QUADS, some_rows, 0)
+    def mixed(quad):
+        arriving = incoming[
+            pl.ds(pl.multiple_of(part_at * 16 + quad * 4, 4), 4),
+            pl.ds(pl.multiple_of(half_at * 64, 64), 64),
+            :,
+        ].reshape(256, 128)
+        mid = dot_nn(mixing[...], outer[part_at * 4 + quad]) + dot_nt(eye, arriving) + bias
+        return mid.astype(BF16).astype(F32)
+
+    def normalised(mid):
+        center = jnp.sum(mid, axis=0, keepdims=True) * F32(1.0 / 128.0)
+        shifted = mid - center
+        spread = jnp.sum(shifted * shifted, axis=0, keepdims=True) * F32(1.0 / 128.0)
+        return (shifted * lax.rsqrt(spread + F32(1e-05)) * scale_by).astype(BF16)
+
+    def widened(normed, part):
+        gate = dot_nn(gate_up[part * 256 : (part + 1) * 256, :], normed)
+        up = dot_nn(gate_up[512 + part * 256 : 512 + (part + 1) * 256, :], normed)
+        half_gate = gate * F32(0.5)
+        return ((half_gate + half_gate * jnp.tanh(half_gate)) * up).astype(BF16)
+
+    def narrowed(hidden, part):
+        return dot_nn(down[:, part * 256 : (part + 1) * 256], hidden)
+
+    def finish(quad, result):
+        turned = turn(result.astype(BF16))
+        out[quad * 4 : quad * 4 + 4] = turned.astype(BF16).reshape(4, 64, 128)
+        tile[quad * 256 : (quad + 1) * 256, :] = turned
+
+    mid = mixed(0)
+    normed = normalised(mid)
+    for quad in range(4):
+        following = mixed(quad + 1) if quad + 1 < 4 else None
+        result = mid
+        hidden = widened(normed, 0)
+        for part in range(1, 2):
+            ahead = widened(normed, part)
+            result = result + narrowed(hidden, part - 1)
+            hidden = ahead
+        if following is not None:
+            normed = normalised(following)
+        result = result + narrowed(hidden, 1)
+        finish(quad, result)
+        mid = following
 
     for group in range(8):
         for one in range(8):
@@ -362,7 +391,7 @@
     right = jnp.transpose(second_homolog_embedding, (1, 2, 0)).reshape(1, 128, 128)
 
     centre = send(right, lambda a, b, c: (c, b, a))
-    *weights, bin_col = prep_call(
+    *weights, bin_col, chains = prep_call(
         tensor_mixing_matrix,
         transition_gate_weight,
         transition_up_weight,
@@ -371,16 +400,17 @@
         outer_product_bias,
         transition_norm_gain,
         distogram_bias,
+        token_chain_index,
     )
     left_two = jnp.concatenate([left, send(left, lambda a, b, c: (a, b, c ^ 1))], 0)
     before = send(centre, lambda a, b, c: ((a + 1) % 8, b, c))
     after = send(centre, lambda a, b, c: ((a - 1) % 8, b, c))
     left_near = jnp.concatenate([left_two, send(left_two, lambda a, b, c: (a, b, c ^ 4))], 0)
-    three = jnp.concatenate([before, centre, after], 0)
-    low = send(three, lambda a, b, c: ((a + 3) % 8, b, c))
-    high = send(three[:2], lambda a, b, c: ((a - 3) % 8, b, c))
+    opposite = send(centre, lambda a, b, c: ((a + 4) % 8, b, c))
+    low = send(jnp.concatenate([before, centre], 0), lambda a, b, c: ((a + 2) % 8, b, c))
+    high = send(jnp.concatenate([centre, after], 0), lambda a, b, c: ((a - 2) % 8, b, c))
     left_far = send(left_near, lambda a, b, c: (a, b, c ^ 2))
-    own = jnp.concatenate([low, three, high], 0)
+    own = jnp.concatenate([opposite, low, before, centre, after, high], 0)
     other = send(own, lambda a, b, c: (a, b ^ 1, c))
     own_far = send(own, lambda a, b, c: (a, b ^ 2, c))
 
@@ -390,7 +420,7 @@
         if flip:
             other = send(own_far, lambda a, b, c: (a, b ^ 1, c))
             own = own_far
-        outer = outer_call(meta, flip, token_chain_index, left_near, left_far, own, other)
+        outer = outer_call(meta, flip, token_chain_index, chains, left_near, left_far, own, other)
         for part_at in range(2):
             pair_out, sent = rows_call(
                 meta, flip, part_at, outer, incoming_pair_state, weights, pair_out

time: 131 us -> 124 us (0.947)
  the two profiles are of different devices: /device:TPU:41 before, /device:TPU:105 now
where the time goes in v3:
time: 124 us
  starting transfers between devices  74.7 us (60%)
  Pallas kernels  29.1 us (23%)
  waiting for transfers between devices  16.5 us (13%)
  other arithmetic  1.63 us (1%)
  local copies, waits for them, and re-layouts  1.29 us (1%)
    ppermute x20, starting transfers between devices, send(): return lax.ppermute(values, AXES, pairs)  74.7 us
    ppermute x20, waiting for transfers between devices, send(): return lax.ppermute(values, AXES, pairs)  16.5 us
    pallas_call x4, Pallas kernels, rows_call(): pl.pallas_call(functools.partial(rows_kernel, flip=flip, part_at=part_at)...  16 us
    pallas_call x2, Pallas kernels, outer_call(): pl.pallas_call(functools.partial(outer_kernel, flip=flip), out_shape=pltp...  6.46 us
    pallas_call x1, Pallas kernels, join_call(): pl.pallas_call(join_kernel, out_shape=jax.ShapeDtypeStruct((64, 32, 128),...  2.67 us
  transfers between devices with their start and end apart: 20, of which 6 were waited for; matrix products, arithmetic and copies ran while one was open for 1% of the time, Pallas kernels for 21%

profile of v3, /device:TPU:105, one launch (start us, length us, event | category | flops | bytes accessed | tf_op | source)
XLA Modules:
  0.0 124.0 jit_solution(15983835095159926602)
XLA Ops:
  0.6 0.0 copy-start
  0.6 4.3 %collective-permute-start.3 = (bf16[1,128,128]{2,1,0:T(8,128)(2,1)}, bf16[1,128,128]{2,1,0:T(8,128)(2,1)S(1)}, u32[]{:S(2)}, u32[]{:S(2)}) collective-permute-start(bf16[1,128,128]{2,1,0:T(8,128)(2,1)} %bitcast.21), channel_id=1, source_target_pairs={{0,0},{1,32},{2,64},{3,96},{4,128},{5,160},{6,192},{7,224},{8,8},{... | collective-permute-start | bytes 98312 | tf_op jit(solution)/shard_map/ppermute | solution.py:31
  5.0 3.1 %collective-permute-done.3 = bf16[1,128,128]{2,1,0:T(8,128)(2,1)S(1)} collective-permute-done((bf16[1,128,128]{2,1,0:T(8,128)(2,1)}, bf16[1,128,128]{2,1,0:T(8,128)(2,1)S(1)}, u32[]{:S(2)}, u32[]{:S(2)}) %collective-permute-start.3) | collective-permute-done | bytes 32800 | tf_op jit(solution)/shard_map/ppermute | solution.py:31
  8.0 3.5 %collective-permute-start.5 = (bf16[1,128,128]{2,1,0:T(8,128)(2,1)S(1)}, bf16[1,128,128]{2,1,0:T(8,128)(2,1)S(1)}, u32[]{:S(2)}, u32[]{:S(2)}) collective-permute-start(bf16[1,128,128]{2,1,0:T(8,128)(2,1)S(1)} %collective-permute-done.3), channel_id=1, source_target_pairs={{0,32},{1,33},{2,34},{3,35},{4,36},{5,37},{6,38},{7,39},{8,40},{9,... | collective-permute-start | bytes 98312 | tf_op jit(solution)/shard_map/ppermute | solution.py:31
  11.5 0.0 collective-permute-start.7
  11.5 7.6 %collective-permute-start.4 = (bf16[1,128,128]{2,1,0:T(8,128)(2,1)S(1)}, bf16[1,128,128]{2,1,0:T(8,128)(2,1)S(1)}, u32[]{:S(2)}, u32[]{:S(2)}) collective-permute-start(bf16[1,128,128]{2,1,0:T(8,128)(2,1)S(1)} %collective-permute-done.3), channel_id=1, source_target_pairs={{0,128},{1,129},{2,130},{3,131},{4,132},{5,133},{6,134},{7,135},{8... | collective-permute-start | bytes 98312 | tf_op jit(solution)/shard_map/ppermute | solution.py:31
  19.1 0.0 collective-permute-done.5
  19.1 0.0 collective-permute-done.7
  19.2 0.5 collective-permute-start.6
  19.6 2.0 %collective-permute-start.8 = (bf16[2,128,128]{2,1,0:T(8,128)(2,1)S(1)}, bf16[2,128,128]{2,1,0:T(8,128)(2,1)S(1)}, u32[]{:S(2)}, u32[]{:S(2)}) collective-permute-start(bf16[2,128,128]{2,1,0:T(8,128)(2,1)S(1)} %get-tuple-element.34), channel_id=1, source_target_pairs={{0,192},{1,193},{2,194},{3,195},{4,196},{5,197},{6,198},{7,199},{8... | collective-permute-start | bytes 196616 | tf_op jit(solution)/shard_map/ppermute | solution.py:31
  21.6 0.0 collective-permute-done.4
  21.6 2.8 %collective-permute-done.6 = bf16[2,128,128]{2,1,0:T(8,128)(2,1)S(1)} collective-permute-done((bf16[2,128,128]{2,1,0:T(8,128)(2,1)S(1)}, bf16[2,128,128]{2,1,0:T(8,128)(2,1)S(1)}, u32[]{:S(2)}, u32[]{:S(2)}) %collective-permute-start.6) | collective-permute-done | bytes 65568 | tf_op jit(solution)/shard_map/ppermute | solution.py:31
  24.4 1.2 collective-permute-done.8
  25.7 1.6 %collective-permute-start.9 = (bf16[8,128,128]{2,1,0:T(8,128)(2,1)S(1)}, bf16[8,128,128]{2,1,0:T(8,128)(2,1)S(1)}, u32[]{:S(2)}, u32[]{:S(2)}) collective-permute-start(bf16[8,128,128]{2,1,0:T(8,128)(2,1)S(1)} %constant_dynamic-update-slice_fusion.right_own), channel_id=1, source_target_pairs={{0,16},{1,17},{2,18},{3,19},{4,20},{5,21},{6,22},{7,23},{8,24},{9,... | collective-permute-start | bytes 786440 | tf_op jit(solution)/shard_map/ppermute | solution.py:31
  27.3 2.6 %collective-permute-start = (bf16[1,128,128]{2,1,0:T(8,128)(2,1)}, bf16[1,128,128]{2,1,0:T(8,128)(2,1)S(1)}, u32[]{:S(2)}, u32[]{:S(2)}) collective-permute-start(bf16[1,128,128]{2,1,0:T(8,128)(2,1)} %bitcast.13), channel_id=1, source_target_pairs={{0,1},{1,0},{2,3},{3,2},{4,5},{5,4},{6,7},{7,6},{8,9},{9,8},{10,11... | collective-permute-start | bytes 98312 | tf_op jit(solution)/shard_map/ppermute | solution.py:31
  29.9 4.1 %collective-permute-done = bf16[1,128,128]{2,1,0:T(8,128)(2,1)S(1)} collective-permute-done((bf16[1,128,128]{2,1,0:T(8,128)(2,1)}, bf16[1,128,128]{2,1,0:T(8,128)(2,1)S(1)}, u32[]{:S(2)}, u32[]{:S(2)}) %collective-permute-start) | collective-permute-done | bytes 32800 | tf_op jit(solution)/shard_map/ppermute | solution.py:31
  34.0 0.8 pad_maximum_fusion.1
  34.8 0.0 collective-permute-start.1
  34.8 5.4 %collective-permute-start.11 = (bf16[8,128,128]{2,1,0:T(8,128)(2,1)S(1)}, bf16[8,128,128]{2,1,0:T(8,128)(2,1)S(1)}, u32[]{:S(2)}, u32[]{:S(2)}) collective-permute-start(bf16[8,128,128]{2,1,0:T(8,128)(2,1)S(1)} %constant_dynamic-update-slice_fusion.right_own), channel_id=1, source_target_pairs={{0,8},{1,9},{2,10},{3,11},{4,12},{5,13},{6,14},{7,15},{8,0},{9,1},... | collective-permute-start | bytes 786440 | tf_op jit(solution)/shard_map/ppermute | solution.py:31
  40.2 0.0 collective-permute-done.9.right_own
  40.2 0.0 collective-permute-start.10
  40.3 0.0 collective-permute-done.1
  40.3 0.8 pad_maximum_fusion.left_near
  41.0 0.9 collective-permute-start.2
  41.9 2.2 %prep.1 = (bf16[128,1024]{1,0:T(8,128)(2,1)S(1)}, bf16[1024,128]{1,0:T(8,128)(2,1)S(1)}, bf16[128,512]{1,0:T(8,128)(2,1)S(1)}, bf16[512,1024]{1,0:T(8,128)(2,1)S...) custom-call(bf16[1024,128]{1,0:T(8,128)(2,1)} %mix.1, ...), custom_call_target="tpu_custom_call" | custom-call | tf_op jit(solution)/shard_map/prep/pallas_call | solution.py:78
  44.1 0.1 pad_add_fusion.meta
  44.2 1.0 collective-permute-done.2.left_far
  45.2 0.0 collective-permute-done.11.right_other
  45.3 3.3 %outer_half.3.outer = bf16[8,1024,256]{2,1,0:T(8,128)(2,1)S(1)} custom-call(s32[2]{0:T(128)S(1)} %pad_add_fusion.meta, s32[1024]{0:T(1024)} %chain_at.3, bf16[4,128,128]{2,1,0:T(8,128)(2,1)S(1)} %pad_maximum_fusion.left_near, bf16[4,128,128]{2,1,0:T(8,128)(2,1)S(1)} %collective-permute-done.2.left_far, ...), custom_call_target="tpu_custom_call" | custom-call | tf_op jit(solution)/shard_map/outer_half/pallas_call | solution.py:202
  48.6 0.0 copy-done
  48.6 4.0 %rows_part.4 = (bf16[32,128,128]{2,1,0:T(8,128)(2,1)}, bf16[2,4,16,512]{3,2,1,0:T(8,128)(2,1)S(1)}) custom-call(s32[2]{0:T(128)S(1)} %pad_add_fusion.meta, bf16[8,1024,256]{2,1,0:T(8,128)(2,1)S(1)} %outer_half.3.outer, bf16[32,128,128]{2,1,0:T(8,128)(2,1)S(1)} %copy-done, bf16[128,1024]{1,0:T(8,128)(2,1)S(1)} %get-tuple-element.19.mixing, ...), custom_call_target="tpu_custom_call" | custom-call | tf_op jit(solution)/shard_map/rows_part/pallas_call | solution.py:299
  52.6 4.0 %rows_part.5 = (bf16[32,128,128]{2,1,0:T(8,128)(2,1)}, bf16[2,4,16,512]{3,2,1,0:T(8,128)(2,1)S(1)}) custom-call(s32[2]{0:T(128)S(1)} %pad_add_fusion.meta, bf16[8,1024,256]{2,1,0:T(8,128)(2,1)S(1)} %outer_half.3.outer, bf16[32,128,128]{2,1,0:T(8,128)(2,1)S(1)} %copy-done, ...), custom_call_target="tpu_custom_call", output_to_operand_aliasing={{0}: (9, {})} | custom-call | tf_op jit(solution)/shard_map/rows_part/pallas_call | solution.py:299
  56.6 3.4 %collective-permute-start.14 = (bf16[2,4,16,512]{3,2,1,0:T(8,128)(2,1)S(1)}, bf16[2,4,16,512]{3,2,1,0:T(8,128)(2,1)S(1)}, u32[]{:S(2)}, u32[]{:S(2)}) collective-permute-start(bf16[2,4,16,512]{3,2,1,0:T(8,128)(2,1)S(1)} %get-tuple-element.31), channel_id=1, source_target_pairs={{0,0},{1,32},{2,64},{3,96},{4,128},{5,160},{6,192},{7,224},{8,8},{... | collective-permute-start | bytes 393224 | tf_op jit(solution)/shard_map/ppermute | solution.py:31
  59.9 4.3 %collective-permute-start.12 = (bf16[2,4,16,512]{3,2,1,0:T(8,128)(2,1)S(1)}, bf16[2,4,16,512]{3,2,1,0:T(8,128)(2,1)S(1)}, u32[]{:S(2)}, u32[]{:S(2)}) collective-permute-start(bf16[2,4,16,512]{3,2,1,0:T(8,128)(2,1)S(1)} %get-tuple-element.30), channel_id=1, source_target_pairs={{0,0},{1,32},{2,64},{3,96},{4,128},{5,160},{6,192},{7,224},{8,8},{... | collective-permute-start | bytes 393224 | tf_op jit(solution)/shard_map/ppermute | solution.py:31
  64.3 0.0 collective-permute-done.10.right_other
  64.3 3.1 %outer_half.2.outer = bf16[8,1024,256]{2,1,0:T(8,128)(2,1)S(1)} custom-call(s32[2]{0:T(128)S(1)} %pad_add_fusion.meta, s32[1024]{0:T(1024)} %chain_at.3, bf16[4,128,128]{2,1,0:T(8,128)(2,1)S(1)} %pad_maximum_fusion.left_near, bf16[4,128,128]{2,1,0:T(8,128)(2,1)S(1)} %collective-permute-done.2.left_far, ...), custom_call_target="tpu_custom_call" | custom-call | tf_op jit(solution)/shard_map/outer_half/pallas_call | solution.py:202
  67.4 4.0 %rows_part.6 = (bf16[32,128,128]{2,1,0:T(8,128)(2,1)}, bf16[2,4,16,512]{3,2,1,0:T(8,128)(2,1)S(1)}) custom-call(s32[2]{0:T(128)S(1)} %pad_add_fusion.meta, bf16[8,1024,256]{2,1,0:T(8,128)(2,1)S(1)} %outer_half.2.outer, bf16[32,128,128]{2,1,0:T(8,128)(2,1)S(1)} %copy-done, ...), custom_call_target="tpu_custom_call", output_to_operand_aliasing={{0}: (9, {})} | custom-call | tf_op jit(solution)/shard_map/rows_part/pallas_call | solution.py:299
  71.4 4.0 %rows_part.7 = (bf16[32,128,128]{2,1,0:T(8,128)(2,1)}, bf16[2,4,16,512]{3,2,1,0:T(8,128)(2,1)S(1)}) custom-call(s32[2]{0:T(128)S(1)} %pad_add_fusion.meta, bf16[8,1024,256]{2,1,0:T(8,128)(2,1)S(1)} %outer_half.2.outer, bf16[32,128,128]{2,1,0:T(8,128)(2,1)S(1)} %copy-done, ...), custom_call_target="tpu_custom_call", output_to_operand_aliasing={{0}: (9, {})} | custom-call | tf_op jit(solution)/shard_map/rows_part/pallas_call | solution.py:299
  75.4 5.8 %collective-permute-start.18 = (bf16[2,4,16,512]{3,2,1,0:T(8,128)(2,1)S(1)}, bf16[2,4,16,512]{3,2,1,0:T(8,128)(2,1)S(1)}, u32[]{:S(2)}, u32[]{:S(2)}) collective-permute-start(bf16[2,4,16,512]{3,2,1,0:T(8,128)(2,1)S(1)} %get-tuple-element.33), channel_id=1, source_target_pairs={{0,16},{1,48},{2,80},{3,112},{4,144},{5,176},{6,208},{7,240},{8,24... | collective-permute-start | bytes 393224 | tf_op jit(solution)/shard_map/ppermute | solution.py:31
  81.2 0.0 collective-permute-start.16
  81.2 0.0 collective-permute-done.14.rest_2_
  81.2 5.3 %collective-permute-start.15 = (bf16[2,4,16,512]{3,2,1,0:T(8,128)(2,1)S(1)}, bf16[2,4,16,512]{3,2,1,0:T(8,128)(2,1)S(1)}, u32[]{:S(2)}, u32[]{:S(2)}) collective-permute-start(bf16[2,4,16,512]{3,2,1,0:T(8,128)(2,1)S(1)} %collective-permute-done.14.rest_2_), channel_id=1, source_target_pairs={{0,8},{1,9},{2,10},{3,11},{4,12},{5,13},{6,14},{7,15},{8,0},{9,1},... | collective-permute-start | bytes 393224 | tf_op jit(solution)/shard_map/ppermute | solution.py:31
  86.6 0.0 collective-permute-done.12.rest_0_
  86.6 19.9 %collective-permute-start.13 = (bf16[2,4,16,512]{3,2,1,0:T(8,128)(2,1)S(1)}, bf16[2,4,16,512]{3,2,1,0:T(8,128)(2,1)S(1)}, u32[]{:S(2)}, u32[]{:S(2)}) collective-permute-start(bf16[2,4,16,512]{3,2,1,0:T(8,128)(2,1)S(1)} %collective-permute-done.12.rest_0_), channel_id=1, source_target_pairs={{0,8},{1,9},{2,10},{3,11},{4,12},{5,13},{6,14},{7,15},{8,0},{9,1},... | collective-permute-start | bytes 393224 | tf_op jit(solution)/shard_map/ppermute | solution.py:31
  106.4 4.3 %collective-permute-done.18.rest_6_ = bf16[2,4,16,512]{3,2,1,0:T(8,128)(2,1)S(1)} collective-permute-done((bf16[2,4,16,512]{3,2,1,0:T(8,128)(2,1)S(1)}, bf16[2,4,16,512]{3,2,1,0:T(8,128)(2,1)S(1)}, u32[]{:S(2)}, u32[]{:S(2)}) %collective-permute-start.18) | collective-permute-done | bytes 131104 | tf_op jit(solution)/shard_map/ppermute | solution.py:31
  110.7 6.0 %collective-permute-start.19 = (bf16[2,4,16,512]{3,2,1,0:T(8,128)(2,1)S(1)}, bf16[2,4,16,512]{3,2,1,0:T(8,128)(2,1)S(1)}, u32[]{:S(2)}, u32[]{:S(2)}) collective-permute-start(bf16[2,4,16,512]{3,2,1,0:T(8,128)(2,1)S(1)} %collective-permute-done.18.rest_6_), channel_id=1, source_target_pairs={{0,8},{1,9},{2,10},{3,11},{4,12},{5,13},{6,14},{7,15},{8,0},{9,1},... | collective-permute-start | bytes 393224 | tf_op jit(solution)/shard_map/ppermute | solution.py:31
  116.7 0.0 collective-permute-done.16.rest_4_
  116.7 1.6 %collective-permute-start.17 = (bf16[2,4,16,512]{3,2,1,0:T(8,128)(2,1)S(1)}, bf16[2,4,16,512]{3,2,1,0:T(8,128)(2,1)S(1)}, u32[]{:S(2)}, u32[]{:S(2)}) collective-permute-start(bf16[2,4,16,512]{3,2,1,0:T(8,128)(2,1)S(1)} %collective-permute-done.16.rest_4_), channel_id=1, source_target_pairs={{0,8},{1,9},{2,10},{3,11},{4,12},{5,13},{6,14},{7,15},{8,0},{9,1},... | collective-permute-start | bytes 393224 | tf_op jit(solution)/shard_map/ppermute | solution.py:31
  118.2 0.0 copy-start.1
  118.2 1.2 copy-done.1
  119.5 1.8 %own_bins.1.own = f32[64,32,128]{2,1,0:T(8,128)S(1)} custom-call(bf16[32,128,128]{2,1,0:T(8,128)(2,1)S(1)} %copy-done.1, bf16[512,1024]{1,0:T(8,128)(2,1)S(1)} %get-tuple-element.22.bins, f32[64,128]{1,0:T(8,128)S(1)} %get-tuple-element.29.bias), custom_call_target="tpu_custom_call" | custom-call | tf_op jit(solution)/shard_map/own_bins/pallas_call | solution.py:326
  121.3 0.0 collective-permute-done.15.rest_3_
  121.3 0.0 collective-permute-done.13.rest_1_
  121.3 0.0 collective-permute-done.19.rest_7_
  121.3 0.0 collective-permute-done.17.rest_5_
  121.3 2.7 %join_bins.1 = f32[64,32,128]{2,1,0:T(8,128)} custom-call(s32[2]{0:T(128)S(1)} %pad_add_fusion.meta, f32[64,32,128]{2,1,0:T(8,128)S(1)} %own_bins.1.own, bf16[2,4,16,512]{3,2,1,0:T(8,128)(2,1)S(1)} %collective-permute-done.12.rest_0_, bf16[2,4,16,512]{3,2,1,0:T(8,128)(2,1)S(1)} %collective-permute-done.13.rest_1_, ...), custom_call_target="tpu_custom_call" | custom-call | tf_op jit(solution)/shard_map/join_bins/pallas_call | solution.py:357
  (7 shorter events, 0.1 us)
Async XLA Ops:
  0.6 48.0 %copy-start = (bf16[32,128,128]{2,1,0:T(8,128)(2,1)S(1)}, bf16[32,128,128]{2,1,0:T(8,128)(2,1)}, u32[]{:S(2)}) copy-start(bf16[32,128,128]{2,1,0:T(8,128)(2,1)} %incoming.7) | copy-start | bytes 3145732
  0.6 7.4 %collective-permute-start.3 = (bf16[1,128,128]{2,1,0:T(8,128)(2,1)}, bf16[1,128,128]{2,1,0:T(8,128)(2,1)S(1)}, u32[]{:S(2)}, u32[]{:S(2)}) collective-permute-start(bf16[1,128,128]{2,1,0:T(8,128)(2,1)} %bitcast.21), channel_id=1, source_target_pairs={{0,0},{1,32},{2,64},{3,96},{4,128},{5,160},{6,192},{7,224},{8,8},{... | collective-permute-start | bytes 98312 | tf_op jit(solution)/shard_map/ppermute | solution.py:31
  8.0 11.1 %collective-permute-start.5 = (bf16[1,128,128]{2,1,0:T(8,128)(2,1)S(1)}, bf16[1,128,128]{2,1,0:T(8,128)(2,1)S(1)}, u32[]{:S(2)}, u32[]{:S(2)}) collective-permute-start(bf16[1,128,128]{2,1,0:T(8,128)(2,1)S(1)} %collective-permute-done.3), channel_id=1, source_target_pairs={{0,32},{1,33},{2,34},{3,35},{4,36},{5,37},{6,38},{7,39},{8,40},{9,... | collective-permute-start | bytes 98312 | tf_op jit(solution)/shard_map/ppermute | solution.py:31
  11.5 7.6 %collective-permute-start.7 = (bf16[1,128,128]{2,1,0:T(8,128)(2,1)S(1)}, bf16[1,128,128]{2,1,0:T(8,128)(2,1)S(1)}, u32[]{:S(2)}, u32[]{:S(2)}) collective-permute-start(bf16[1,128,128]{2,1,0:T(8,128)(2,1)S(1)} %collective-permute-done.3), channel_id=1, source_target_pairs={{0,224},{1,225},{2,226},{3,227},{4,228},{5,229},{6,230},{7,231},{8... | collective-permute-start | bytes 98312 | tf_op jit(solution)/shard_map/ppermute | solution.py:31
  11.5 10.1 %collective-permute-start.4 = (bf16[1,128,128]{2,1,0:T(8,128)(2,1)S(1)}, bf16[1,128,128]{2,1,0:T(8,128)(2,1)S(1)}, u32[]{:S(2)}, u32[]{:S(2)}) collective-permute-start(bf16[1,128,128]{2,1,0:T(8,128)(2,1)S(1)} %collective-permute-done.3), channel_id=1, source_target_pairs={{0,128},{1,129},{2,130},{3,131},{4,132},{5,133},{6,134},{7,135},{8... | collective-permute-start | bytes 98312 | tf_op jit(solution)/shard_map/ppermute | solution.py:31
  19.2 5.2 %collective-permute-start.6 = (bf16[2,128,128]{2,1,0:T(8,128)(2,1)S(1)}, bf16[2,128,128]{2,1,0:T(8,128)(2,1)S(1)}, u32[]{:S(2)}, u32[]{:S(2)}) collective-permute-start(bf16[2,128,128]{2,1,0:T(8,128)(2,1)S(1)} %get-tuple-element.35), channel_id=1, source_target_pairs={{0,64},{1,65},{2,66},{3,67},{4,68},{5,69},{6,70},{7,71},{8,72},{9,... | collective-permute-start | bytes 196616 | tf_op jit(solution)/shard_map/ppermute | solution.py:31
  19.6 6.0 %collective-permute-start.8 = (bf16[2,128,128]{2,1,0:T(8,128)(2,1)S(1)}, bf16[2,128,128]{2,1,0:T(8,128)(2,1)S(1)}, u32[]{:S(2)}, u32[]{:S(2)}) collective-permute-start(bf16[2,128,128]{2,1,0:T(8,128)(2,1)S(1)} %get-tuple-element.34), channel_id=1, source_target_pairs={{0,192},{1,193},{2,194},{3,195},{4,196},{5,197},{6,198},{7,199},{8... | collective-permute-start | bytes 196616 | tf_op jit(solution)/shard_map/ppermute | solution.py:31
  25.7 14.6 %collective-permute-start.9 = (bf16[8,128,128]{2,1,0:T(8,128)(2,1)S(1)}, bf16[8,128,128]{2,1,0:T(8,128)(2,1)S(1)}, u32[]{:S(2)}, u32[]{:S(2)}) collective-permute-start(bf16[8,128,128]{2,1,0:T(8,128)(2,1)S(1)} %constant_dynamic-update-slice_fusion.right_own), channel_id=1, source_target_pairs={{0,16},{1,17},{2,18},{3,19},{4,20},{5,21},{6,22},{7,23},{8,24},{9,... | collective-permute-start | bytes 786440 | tf_op jit(solution)/shard_map/ppermute | solution.py:31
  27.3 6.8 %collective-permute-start = (bf16[1,128,128]{2,1,0:T(8,128)(2,1)}, bf16[1,128,128]{2,1,0:T(8,128)(2,1)S(1)}, u32[]{:S(2)}, u32[]{:S(2)}) collective-permute-start(bf16[1,128,128]{2,1,0:T(8,128)(2,1)} %bitcast.13), channel_id=1, source_target_pairs={{0,1},{1,0},{2,3},{3,2},{4,5},{5,4},{6,7},{7,6},{8,9},{9,8},{10,11... | collective-permute-start | bytes 98312 | tf_op jit(solution)/shard_map/ppermute | solution.py:31
  34.8 5.5 %collective-permute-start.1 = (bf16[2,128,128]{2,1,0:T(8,128)(2,1)S(1)}, bf16[2,128,128]{2,1,0:T(8,128)(2,1)S(1)}, u32[]{:S(2)}, u32[]{:S(2)}) collective-permute-start(bf16[2,128,128]{2,1,0:T(8,128)(2,1)S(1)} %pad_maximum_fusion.1), channel_id=1, source_target_pairs={{0,4},{1,5},{2,6},{3,7},{4,0},{5,1},{6,2},{7,3},{8,12},{9,13},{10,... | collective-permute-start | bytes 196616 | tf_op jit(solution)/shard_map/ppermute | solution.py:31
  34.8 10.5 %collective-permute-start.11 = (bf16[8,128,128]{2,1,0:T(8,128)(2,1)S(1)}, bf16[8,128,128]{2,1,0:T(8,128)(2,1)S(1)}, u32[]{:S(2)}, u32[]{:S(2)}) collective-permute-start(bf16[8,128,128]{2,1,0:T(8,128)(2,1)S(1)} %constant_dynamic-update-slice_fusion.right_own), channel_id=1, source_target_pairs={{0,8},{1,9},{2,10},{3,11},{4,12},{5,13},{6,14},{7,15},{8,0},{9,1},... | collective-permute-start | bytes 786440 | tf_op jit(solution)/shard_map/ppermute | solution.py:31
  40.2 24.0 %collective-permute-start.10 = (bf16[8,128,128]{2,1,0:T(8,128)(2,1)S(1)}, bf16[8,128,128]{2,1,0:T(8,128)(2,1)S(1)}, u32[]{:S(2)}, u32[]{:S(2)}) collective-permute-start(bf16[8,128,128]{2,1,0:T(8,128)(2,1)S(1)} %collective-permute-done.9.right_own), channel_id=1, source_target_pairs={{0,8},{1,9},{2,10},{3,11},{4,12},{5,13},{6,14},{7,15},{8,0},{9,1},... | collective-permute-start | bytes 786440 | tf_op jit(solution)/shard_map/ppermute | solution.py:31
  41.0 4.2 %collective-permute-start.2 = (bf16[4,128,128]{2,1,0:T(8,128)(2,1)S(1)}, bf16[4,128,128]{2,1,0:T(8,128)(2,1)S(1)}, u32[]{:S(2)}, u32[]{:S(2)}) collective-permute-start(bf16[4,128,128]{2,1,0:T(8,128)(2,1)S(1)} %pad_maximum_fusion.left_near), channel_id=1, source_target_pairs={{0,2},{1,3},{2,0},{3,1},{4,6},{5,7},{6,4},{7,5},{8,10},{9,11},{10,... | collective-permute-start | bytes 393224 | tf_op jit(solution)/shard_map/ppermute | solution.py:31
  56.6 24.7 %collective-permute-start.14 = (bf16[2,4,16,512]{3,2,1,0:T(8,128)(2,1)S(1)}, bf16[2,4,16,512]{3,2,1,0:T(8,128)(2,1)S(1)}, u32[]{:S(2)}, u32[]{:S(2)}) collective-permute-start(bf16[2,4,16,512]{3,2,1,0:T(8,128)(2,1)S(1)} %get-tuple-element.31), channel_id=1, source_target_pairs={{0,0},{1,32},{2,64},{3,96},{4,128},{5,160},{6,192},{7,224},{8,8},{... | collective-permute-start | bytes 393224 | tf_op jit(solution)/shard_map/ppermute | solution.py:31
  59.9 26.6 %collective-permute-start.12 = (bf16[2,4,16,512]{3,2,1,0:T(8,128)(2,1)S(1)}, bf16[2,4,16,512]{3,2,1,0:T(8,128)(2,1)S(1)}, u32[]{:S(2)}, u32[]{:S(2)}) collective-permute-start(bf16[2,4,16,512]{3,2,1,0:T(8,128)(2,1)S(1)} %get-tuple-element.30), channel_id=1, source_target_pairs={{0,0},{1,32},{2,64},{3,96},{4,128},{5,160},{6,192},{7,224},{8,8},{... | collective-permute-start | bytes 393224 | tf_op jit(solution)/shard_map/ppermute | solution.py:31
  75.4 35.2 %collective-permute-start.18 = (bf16[2,4,16,512]{3,2,1,0:T(8,128)(2,1)S(1)}, bf16[2,4,16,512]{3,2,1,0:T(8,128)(2,1)S(1)}, u32[]{:S(2)}, u32[]{:S(2)}) collective-permute-start(bf16[2,4,16,512]{3,2,1,0:T(8,128)(2,1)S(1)} %get-tuple-element.33), channel_id=1, source_target_pairs={{0,16},{1,48},{2,80},{3,112},{4,144},{5,176},{6,208},{7,240},{8,24... | collective-permute-start | bytes 393224 | tf_op jit(solution)/shard_map/ppermute | solution.py:31
  81.2 35.5 %collective-permute-start.16 = (bf16[2,4,16,512]{3,2,1,0:T(8,128)(2,1)S(1)}, bf16[2,4,16,512]{3,2,1,0:T(8,128)(2,1)S(1)}, u32[]{:S(2)}, u32[]{:S(2)}) collective-permute-start(bf16[2,4,16,512]{3,2,1,0:T(8,128)(2,1)S(1)} %get-tuple-element.32), channel_id=1, source_target_pairs={{0,16},{1,48},{2,80},{3,112},{4,144},{5,176},{6,208},{7,240},{8,24... | collective-permute-start | bytes 393224 | tf_op jit(solution)/shard_map/ppermute | solution.py:31
  81.2 40.0 %collective-permute-start.15 = (bf16[2,4,16,512]{3,2,1,0:T(8,128)(2,1)S(1)}, bf16[2,4,16,512]{3,2,1,0:T(8,128)(2,1)S(1)}, u32[]{:S(2)}, u32[]{:S(2)}) collective-permute-start(bf16[2,4,16,512]{3,2,1,0:T(8,128)(2,1)S(1)} %collective-permute-done.14.rest_2_), channel_id=1, source_target_pairs={{0,8},{1,9},{2,10},{3,11},{4,12},{5,13},{6,14},{7,15},{8,0},{9,1},... | collective-permute-start | bytes 393224 | tf_op jit(solution)/shard_map/ppermute | solution.py:31
  86.6 34.7 %collective-permute-start.13 = (bf16[2,4,16,512]{3,2,1,0:T(8,128)(2,1)S(1)}, bf16[2,4,16,512]{3,2,1,0:T(8,128)(2,1)S(1)}, u32[]{:S(2)}, u32[]{:S(2)}) collective-permute-start(bf16[2,4,16,512]{3,2,1,0:T(8,128)(2,1)S(1)} %collective-permute-done.12.rest_0_), channel_id=1, source_target_pairs={{0,8},{1,9},{2,10},{3,11},{4,12},{5,13},{6,14},{7,15},{8,0},{9,1},... | collective-permute-start | bytes 393224 | tf_op jit(solution)/shard_map/ppermute | solution.py:31
  110.7 10.6 %collective-permute-start.19 = (bf16[2,4,16,512]{3,2,1,0:T(8,128)(2,1)S(1)}, bf16[2,4,16,512]{3,2,1,0:T(8,128)(2,1)S(1)}, u32[]{:S(2)}, u32[]{:S(2)}) collective-permute-start(bf16[2,4,16,512]{3,2,1,0:T(8,128)(2,1)S(1)} %collective-permute-done.18.rest_6_), channel_id=1, source_target_pairs={{0,8},{1,9},{2,10},{3,11},{4,12},{5,13},{6,14},{7,15},{8,0},{9,1},... | collective-permute-start | bytes 393224 | tf_op jit(solution)/shard_map/ppermute | solution.py:31
  116.7 4.6 %collective-permute-start.17 = (bf16[2,4,16,512]{3,2,1,0:T(8,128)(2,1)S(1)}, bf16[2,4,16,512]{3,2,1,0:T(8,128)(2,1)S(1)}, u32[]{:S(2)}, u32[]{:S(2)}) collective-permute-start(bf16[2,4,16,512]{3,2,1,0:T(8,128)(2,1)S(1)} %collective-permute-done.16.rest_4_), channel_id=1, source_target_pairs={{0,8},{1,9},{2,10},{3,11},{4,12},{5,13},{6,14},{7,15},{8,0},{9,1},... | collective-permute-start | bytes 393224 | tf_op jit(solution)/shard_map/ppermute | solution.py:31
  118.2 1.2 copy-start.1

commit v4 on v3

--- a/solution.py
+++ b/solution.py
@@ -338,19 +338,20 @@
     out, block = rest[-2:]
     b_at = lax.rem(meta[0], 4)
     step = pl.program_id(0)
-    rows = pl.ds(pl.multiple_of(step * 8, 8), 8)
     eye = square_eye()
-    for piece in range(4):
-        mine, partner = rest[piece * 2], rest[piece * 2 + 1]
-        for side, values in enumerate((mine, partner)):
-            from_b = jnp.bitwise_xor(b_at, (piece // 2) * 2 + side)
-            at = pl.multiple_of(from_b * 32 + (piece % 2) * 16, 16)
-            block[pl.ds(at, 16), :] = values[side, step]
-    for part in range(4):
-        turned = dot_nt(eye, block[:, part * 128 : (part + 1) * 128])
-        out[part * 16 : (part + 1) * 16] = own[
-            part * 16 : (part + 1) * 16, rows, :
-        ] + turned.reshape(16, 8, 128)
+    for group in range(2):
+        rows = pl.ds(pl.multiple_of(step * 16 + group * 8, 8), 8)
+        for piece in range(4):
+            for side in range(2):
+                values = rest[piece * 2 + side]
+                from_b = jnp.bitwise_xor(b_at, (piece // 2) * 2 + side)
+                at = pl.multiple_of(from_b * 32 + (piece % 2) * 16, 16)
+                block[group, pl.ds(at, 16), :] = values[side, step * 2 + group]
+        for part in range(4):
+            turned = dot_nt(eye, block[group, :, part * 128 : (part + 1) * 128])
+            out[part * 16 : (part + 1) * 16, group * 8 : (group + 1) * 8, :] = own[
+                part * 16 : (part + 1) * 16, rows, :
+            ] + turned.reshape(16, 8, 128)
 
 
 def join_call(meta, own, pieces):
@@ -359,10 +360,10 @@
         out_shape=jax.ShapeDtypeStruct((64, 32, 128), F32),
         grid_spec=pltpu.PrefetchScalarGridSpec(
             num_scalar_prefetch=1,
-            grid=(4,),
+            grid=(2,),
             in_specs=[VMEM_SPEC] * 9,
-            out_specs=pl.BlockSpec((64, 8, 128), lambda g, m: (0, g, 0)),
-            scratch_shapes=[pltpu.VMEM((128, 512), BF16)],
+            out_specs=pl.BlockSpec((64, 16, 128), lambda g, m: (0, g, 0)),
+            scratch_shapes=[pltpu.VMEM((2, 128, 512), BF16)],
         ),
         compiler_params=pltpu.CompilerParams(vmem_limit_bytes=16 << 20),
         name="join_bins",

time: 124 us -> 124 us (level)
  no operation moved by 1% of the time
where the time goes in v4:
time: 124 us; the launch traced here: 123 us
  starting transfers between devices  74.7 us (60%)
  Pallas kernels  28.5 us (23%)
  waiting for transfers between devices  16.5 us (13%)
  other arithmetic  1.63 us (1%)
  local copies, waits for them, and re-layouts  1.29 us (1%)
    ppermute x20, starting transfers between devices, send(): return lax.ppermute(values, AXES, pairs)  74.7 us
    ppermute x20, waiting for transfers between devices, send(): return lax.ppermute(values, AXES, pairs)  16.5 us
    pallas_call x4, Pallas kernels, rows_call(): pl.pallas_call(functools.partial(rows_kernel, flip=flip, part_at=part_at)...  16 us
    pallas_call x2, Pallas kernels, outer_call(): pl.pallas_call(functools.partial(outer_kernel, flip=flip), out_shape=pltp...  6.46 us
  transfers between devices with their start and end apart: 20, of which 6 were waited for; matrix products, arithmetic and copies ran while one was open for 1% of the time, Pallas kernels for 21%

profile of v4, /device:TPU:105, one launch (start us, length us, event | category | flops | bytes accessed | tf_op | source)
XLA Modules:
  0.0 123.3 jit_solution(14930171395427217599)
XLA Ops:
  0.6 0.0 copy-start
  0.6 4.3 %collective-permute-start.3 = (bf16[1,128,128]{2,1,0:T(8,128)(2,1)}, bf16[1,128,128]{2,1,0:T(8,128)(2,1)S(1)}, u32[]{:S(2)}, u32[]{:S(2)}) collective-permute-start(bf16[1,128,128]{2,1,0:T(8,128)(2,1)} %bitcast.21), channel_id=1, source_target_pairs={{0,0},{1,32},{2,64},{3,96},{4,128},{5,160},{6,192},{7,224},{8,8},{... | collective-permute-start | bytes 98312 | tf_op jit(solution)/shard_map/ppermute | solution.py:31
  5.0 3.1 %collective-permute-done.3 = bf16[1,128,128]{2,1,0:T(8,128)(2,1)S(1)} collective-permute-done((bf16[1,128,128]{2,1,0:T(8,128)(2,1)}, bf16[1,128,128]{2,1,0:T(8,128)(2,1)S(1)}, u32[]{:S(2)}, u32[]{:S(2)}) %collective-permute-start.3) | collective-permute-done | bytes 32800 | tf_op jit(solution)/shard_map/ppermute | solution.py:31
  8.0 3.5 %collective-permute-start.5 = (bf16[1,128,128]{2,1,0:T(8,128)(2,1)S(1)}, bf16[1,128,128]{2,1,0:T(8,128)(2,1)S(1)}, u32[]{:S(2)}, u32[]{:S(2)}) collective-permute-start(bf16[1,128,128]{2,1,0:T(8,128)(2,1)S(1)} %collective-permute-done.3), channel_id=1, source_target_pairs={{0,32},{1,33},{2,34},{3,35},{4,36},{5,37},{6,38},{7,39},{8,40},{9,... | collective-permute-start | bytes 98312 | tf_op jit(solution)/shard_map/ppermute | solution.py:31
  11.5 0.0 collective-permute-start.7
  11.5 7.6 %collective-permute-start.4 = (bf16[1,128,128]{2,1,0:T(8,128)(2,1)S(1)}, bf16[1,128,128]{2,1,0:T(8,128)(2,1)S(1)}, u32[]{:S(2)}, u32[]{:S(2)}) collective-permute-start(bf16[1,128,128]{2,1,0:T(8,128)(2,1)S(1)} %collective-permute-done.3), channel_id=1, source_target_pairs={{0,128},{1,129},{2,130},{3,131},{4,132},{5,133},{6,134},{7,135},{8... | collective-permute-start | bytes 98312 | tf_op jit(solution)/shard_map/ppermute | solution.py:31
  19.1 0.0 collective-permute-done.5
  19.1 0.0 collective-permute-done.7
  19.2 0.5 collective-permute-start.6
  19.6 2.0 %collective-permute-start.8 = (bf16[2,128,128]{2,1,0:T(8,128)(2,1)S(1)}, bf16[2,128,128]{2,1,0:T(8,128)(2,1)S(1)}, u32[]{:S(2)}, u32[]{:S(2)}) collective-permute-start(bf16[2,128,128]{2,1,0:T(8,128)(2,1)S(1)} %get-tuple-element.34), channel_id=1, source_target_pairs={{0,192},{1,193},{2,194},{3,195},{4,196},{5,197},{6,198},{7,199},{8... | collective-permute-start | bytes 196616 | tf_op jit(solution)/shard_map/ppermute | solution.py:31
  21.6 0.0 collective-permute-done.4
  21.6 2.8 %collective-permute-done.6 = bf16[2,128,128]{2,1,0:T(8,128)(2,1)S(1)} collective-permute-done((bf16[2,128,128]{2,1,0:T(8,128)(2,1)S(1)}, bf16[2,128,128]{2,1,0:T(8,128)(2,1)S(1)}, u32[]{:S(2)}, u32[]{:S(2)}) %collective-permute-start.6) | collective-permute-done | bytes 65568 | tf_op jit(solution)/shard_map/ppermute | solution.py:31
  24.4 1.2 collective-permute-done.8
  25.7 1.6 %collective-permute-start.9 = (bf16[8,128,128]{2,1,0:T(8,128)(2,1)S(1)}, bf16[8,128,128]{2,1,0:T(8,128)(2,1)S(1)}, u32[]{:S(2)}, u32[]{:S(2)}) collective-permute-start(bf16[8,128,128]{2,1,0:T(8,128)(2,1)S(1)} %constant_dynamic-update-slice_fusion.right_own), channel_id=1, source_target_pairs={{0,16},{1,17},{2,18},{3,19},{4,20},{5,21},{6,22},{7,23},{8,24},{9,... | collective-permute-start | bytes 786440 | tf_op jit(solution)/shard_map/ppermute | solution.py:31
  27.3 2.6 %collective-permute-start = (bf16[1,128,128]{2,1,0:T(8,128)(2,1)}, bf16[1,128,128]{2,1,0:T(8,128)(2,1)S(1)}, u32[]{:S(2)}, u32[]{:S(2)}) collective-permute-start(bf16[1,128,128]{2,1,0:T(8,128)(2,1)} %bitcast.13), channel_id=1, source_target_pairs={{0,1},{1,0},{2,3},{3,2},{4,5},{5,4},{6,7},{7,6},{8,9},{9,8},{10,11... | collective-permute-start | bytes 98312 | tf_op jit(solution)/shard_map/ppermute | solution.py:31
  29.9 4.1 %collective-permute-done = bf16[1,128,128]{2,1,0:T(8,128)(2,1)S(1)} collective-permute-done((bf16[1,128,128]{2,1,0:T(8,128)(2,1)}, bf16[1,128,128]{2,1,0:T(8,128)(2,1)S(1)}, u32[]{:S(2)}, u32[]{:S(2)}) %collective-permute-start) | collective-permute-done | bytes 32800 | tf_op jit(solution)/shard_map/ppermute | solution.py:31
  34.0 0.8 pad_maximum_fusion.1
  34.8 0.0 collective-permute-start.1
  34.8 5.4 %collective-permute-start.11 = (bf16[8,128,128]{2,1,0:T(8,128)(2,1)S(1)}, bf16[8,128,128]{2,1,0:T(8,128)(2,1)S(1)}, u32[]{:S(2)}, u32[]{:S(2)}) collective-permute-start(bf16[8,128,128]{2,1,0:T(8,128)(2,1)S(1)} %constant_dynamic-update-slice_fusion.right_own), channel_id=1, source_target_pairs={{0,8},{1,9},{2,10},{3,11},{4,12},{5,13},{6,14},{7,15},{8,0},{9,1},... | collective-permute-start | bytes 786440 | tf_op jit(solution)/shard_map/ppermute | solution.py:31
  40.2 0.0 collective-permute-done.9.right_own
  40.2 0.0 collective-permute-start.10
  40.3 0.0 collective-permute-done.1
  40.3 0.8 pad_maximum_fusion.left_near
  41.0 0.9 collective-permute-start.2
  41.9 2.2 %prep.1 = (bf16[128,1024]{1,0:T(8,128)(2,1)S(1)}, bf16[1024,128]{1,0:T(8,128)(2,1)S(1)}, bf16[128,512]{1,0:T(8,128)(2,1)S(1)}, bf16[512,1024]{1,0:T(8,128)(2,1)S...) custom-call(bf16[1024,128]{1,0:T(8,128)(2,1)} %mix.1, ...), custom_call_target="tpu_custom_call" | custom-call | tf_op jit(solution)/shard_map/prep/pallas_call | solution.py:78
  44.1 0.1 pad_add_fusion.meta
  44.2 1.0 collective-permute-done.2.left_far
  45.2 0.0 collective-permute-done.11.right_other
  45.3 3.3 %outer_half.3.outer = bf16[8,1024,256]{2,1,0:T(8,128)(2,1)S(1)} custom-call(s32[2]{0:T(128)S(1)} %pad_add_fusion.meta, s32[1024]{0:T(1024)} %chain_at.3, bf16[4,128,128]{2,1,0:T(8,128)(2,1)S(1)} %pad_maximum_fusion.left_near, bf16[4,128,128]{2,1,0:T(8,128)(2,1)S(1)} %collective-permute-done.2.left_far, ...), custom_call_target="tpu_custom_call" | custom-call | tf_op jit(solution)/shard_map/outer_half/pallas_call | solution.py:202
  48.6 0.0 copy-done
  48.6 4.0 %rows_part.4 = (bf16[32,128,128]{2,1,0:T(8,128)(2,1)}, bf16[2,4,16,512]{3,2,1,0:T(8,128)(2,1)S(1)}) custom-call(s32[2]{0:T(128)S(1)} %pad_add_fusion.meta, bf16[8,1024,256]{2,1,0:T(8,128)(2,1)S(1)} %outer_half.3.outer, bf16[32,128,128]{2,1,0:T(8,128)(2,1)S(1)} %copy-done, bf16[128,1024]{1,0:T(8,128)(2,1)S(1)} %get-tuple-element.19.mixing, ...), custom_call_target="tpu_custom_call" | custom-call | tf_op jit(solution)/shard_map/rows_part/pallas_call | solution.py:299
  52.6 4.0 %rows_part.5 = (bf16[32,128,128]{2,1,0:T(8,128)(2,1)}, bf16[2,4,16,512]{3,2,1,0:T(8,128)(2,1)S(1)}) custom-call(s32[2]{0:T(128)S(1)} %pad_add_fusion.meta, bf16[8,1024,256]{2,1,0:T(8,128)(2,1)S(1)} %outer_half.3.outer, bf16[32,128,128]{2,1,0:T(8,128)(2,1)S(1)} %copy-done, ...), custom_call_target="tpu_custom_call", output_to_operand_aliasing={{0}: (9, {})} | custom-call | tf_op jit(solution)/shard_map/rows_part/pallas_call | solution.py:299
  56.6 3.4 %collective-permute-start.14 = (bf16[2,4,16,512]{3,2,1,0:T(8,128)(2,1)S(1)}, bf16[2,4,16,512]{3,2,1,0:T(8,128)(2,1)S(1)}, u32[]{:S(2)}, u32[]{:S(2)}) collective-permute-start(bf16[2,4,16,512]{3,2,1,0:T(8,128)(2,1)S(1)} %get-tuple-element.31), channel_id=1, source_target_pairs={{0,0},{1,32},{2,64},{3,96},{4,128},{5,160},{6,192},{7,224},{8,8},{... | collective-permute-start | bytes 393224 | tf_op jit(solution)/shard_map/ppermute | solution.py:31
  59.9 4.3 %collective-permute-start.12 = (bf16[2,4,16,512]{3,2,1,0:T(8,128)(2,1)S(1)}, bf16[2,4,16,512]{3,2,1,0:T(8,128)(2,1)S(1)}, u32[]{:S(2)}, u32[]{:S(2)}) collective-permute-start(bf16[2,4,16,512]{3,2,1,0:T(8,128)(2,1)S(1)} %get-tuple-element.30), channel_id=1, source_target_pairs={{0,0},{1,32},{2,64},{3,96},{4,128},{5,160},{6,192},{7,224},{8,8},{... | collective-permute-start | bytes 393224 | tf_op jit(solution)/shard_map/ppermute | solution.py:31
  64.3 0.0 collective-permute-done.10.right_other
  64.3 3.1 %outer_half.2.outer = bf16[8,1024,256]{2,1,0:T(8,128)(2,1)S(1)} custom-call(s32[2]{0:T(128)S(1)} %pad_add_fusion.meta, s32[1024]{0:T(1024)} %chain_at.3, bf16[4,128,128]{2,1,0:T(8,128)(2,1)S(1)} %pad_maximum_fusion.left_near, bf16[4,128,128]{2,1,0:T(8,128)(2,1)S(1)} %collective-permute-done.2.left_far, ...), custom_call_target="tpu_custom_call" | custom-call | tf_op jit(solution)/shard_map/outer_half/pallas_call | solution.py:202
  67.4 4.0 %rows_part.6 = (bf16[32,128,128]{2,1,0:T(8,128)(2,1)}, bf16[2,4,16,512]{3,2,1,0:T(8,128)(2,1)S(1)}) custom-call(s32[2]{0:T(128)S(1)} %pad_add_fusion.meta, bf16[8,1024,256]{2,1,0:T(8,128)(2,1)S(1)} %outer_half.2.outer, bf16[32,128,128]{2,1,0:T(8,128)(2,1)S(1)} %copy-done, ...), custom_call_target="tpu_custom_call", output_to_operand_aliasing={{0}: (9, {})} | custom-call | tf_op jit(solution)/shard_map/rows_part/pallas_call | solution.py:299
  71.4 4.0 %rows_part.7 = (bf16[32,128,128]{2,1,0:T(8,128)(2,1)}, bf16[2,4,16,512]{3,2,1,0:T(8,128)(2,1)S(1)}) custom-call(s32[2]{0:T(128)S(1)} %pad_add_fusion.meta, bf16[8,1024,256]{2,1,0:T(8,128)(2,1)S(1)} %outer_half.2.outer, bf16[32,128,128]{2,1,0:T(8,128)(2,1)S(1)} %copy-done, ...), custom_call_target="tpu_custom_call", output_to_operand_aliasing={{0}: (9, {})} | custom-call | tf_op jit(solution)/shard_map/rows_part/pallas_call | solution.py:299
  75.4 5.8 %collective-permute-start.18 = (bf16[2,4,16,512]{3,2,1,0:T(8,128)(2,1)S(1)}, bf16[2,4,16,512]{3,2,1,0:T(8,128)(2,1)S(1)}, u32[]{:S(2)}, u32[]{:S(2)}) collective-permute-start(bf16[2,4,16,512]{3,2,1,0:T(8,128)(2,1)S(1)} %get-tuple-element.33), channel_id=1, source_target_pairs={{0,16},{1,48},{2,80},{3,112},{4,144},{5,176},{6,208},{7,240},{8,24... | collective-permute-start | bytes 393224 | tf_op jit(solution)/shard_map/ppermute | solution.py:31
  81.2 0.0 collective-permute-start.16
  81.2 0.0 collective-permute-done.14.rest_2_
  81.2 5.3 %collective-permute-start.15 = (bf16[2,4,16,512]{3,2,1,0:T(8,128)(2,1)S(1)}, bf16[2,4,16,512]{3,2,1,0:T(8,128)(2,1)S(1)}, u32[]{:S(2)}, u32[]{:S(2)}) collective-permute-start(bf16[2,4,16,512]{3,2,1,0:T(8,128)(2,1)S(1)} %collective-permute-done.14.rest_2_), channel_id=1, source_target_pairs={{0,8},{1,9},{2,10},{3,11},{4,12},{5,13},{6,14},{7,15},{8,0},{9,1},... | collective-permute-start | bytes 393224 | tf_op jit(solution)/shard_map/ppermute | solution.py:31
  86.6 0.0 collective-permute-done.12.rest_0_
  86.6 19.9 %collective-permute-start.13 = (bf16[2,4,16,512]{3,2,1,0:T(8,128)(2,1)S(1)}, bf16[2,4,16,512]{3,2,1,0:T(8,128)(2,1)S(1)}, u32[]{:S(2)}, u32[]{:S(2)}) collective-permute-start(bf16[2,4,16,512]{3,2,1,0:T(8,128)(2,1)S(1)} %collective-permute-done.12.rest_0_), channel_id=1, source_target_pairs={{0,8},{1,9},{2,10},{3,11},{4,12},{5,13},{6,14},{7,15},{8,0},{9,1},... | collective-permute-start | bytes 393224 | tf_op jit(solution)/shard_map/ppermute | solution.py:31
  106.4 4.3 %collective-permute-done.18.rest_6_ = bf16[2,4,16,512]{3,2,1,0:T(8,128)(2,1)S(1)} collective-permute-done((bf16[2,4,16,512]{3,2,1,0:T(8,128)(2,1)S(1)}, bf16[2,4,16,512]{3,2,1,0:T(8,128)(2,1)S(1)}, u32[]{:S(2)}, u32[]{:S(2)}) %collective-permute-start.18) | collective-permute-done | bytes 131104 | tf_op jit(solution)/shard_map/ppermute | solution.py:31
  110.7 6.0 %collective-permute-start.19 = (bf16[2,4,16,512]{3,2,1,0:T(8,128)(2,1)S(1)}, bf16[2,4,16,512]{3,2,1,0:T(8,128)(2,1)S(1)}, u32[]{:S(2)}, u32[]{:S(2)}) collective-permute-start(bf16[2,4,16,512]{3,2,1,0:T(8,128)(2,1)S(1)} %collective-permute-done.18.rest_6_), channel_id=1, source_target_pairs={{0,8},{1,9},{2,10},{3,11},{4,12},{5,13},{6,14},{7,15},{8,0},{9,1},... | collective-permute-start | bytes 393224 | tf_op jit(solution)/shard_map/ppermute | solution.py:31
  116.7 0.0 collective-permute-done.16.rest_4_
  116.7 1.6 %collective-permute-start.17 = (bf16[2,4,16,512]{3,2,1,0:T(8,128)(2,1)S(1)}, bf16[2,4,16,512]{3,2,1,0:T(8,128)(2,1)S(1)}, u32[]{:S(2)}, u32[]{:S(2)}) collective-permute-start(bf16[2,4,16,512]{3,2,1,0:T(8,128)(2,1)S(1)} %collective-permute-done.16.rest_4_), channel_id=1, source_target_pairs={{0,8},{1,9},{2,10},{3,11},{4,12},{5,13},{6,14},{7,15},{8,0},{9,1},... | collective-permute-start | bytes 393224 | tf_op jit(solution)/shard_map/ppermute | solution.py:31
  118.2 0.0 copy-start.1
  118.2 1.2 copy-done.1
  119.5 1.8 %own_bins.1.own = f32[64,32,128]{2,1,0:T(8,128)S(1)} custom-call(bf16[32,128,128]{2,1,0:T(8,128)(2,1)S(1)} %copy-done.1, bf16[512,1024]{1,0:T(8,128)(2,1)S(1)} %get-tuple-element.22.bins, f32[64,128]{1,0:T(8,128)S(1)} %get-tuple-element.29.bias), custom_call_target="tpu_custom_call" | custom-call | tf_op jit(solution)/shard_map/own_bins/pallas_call | solution.py:326
  121.3 0.0 collective-permute-done.15.rest_3_
  121.3 0.0 collective-permute-done.13.rest_1_
  121.3 0.0 collective-permute-done.19.rest_7_
  121.3 0.0 collective-permute-done.17.rest_5_
  121.3 2.0 %join_bins.1 = f32[64,32,128]{2,1,0:T(8,128)} custom-call(s32[2]{0:T(128)S(1)} %pad_add_fusion.meta, f32[64,32,128]{2,1,0:T(8,128)S(1)} %own_bins.1.own, bf16[2,4,16,512]{3,2,1,0:T(8,128)(2,1)S(1)} %collective-permute-done.12.rest_0_, bf16[2,4,16,512]{3,2,1,0:T(8,128)(2,1)S(1)} %collective-permute-done.13.rest_1_, ...), custom_call_target="tpu_custom_call" | custom-call | tf_op jit(solution)/shard_map/join_bins/pallas_call | solution.py:358
  (7 shorter events, 0.1 us)
Async XLA Ops:
  0.6 48.0 %copy-start = (bf16[32,128,128]{2,1,0:T(8,128)(2,1)S(1)}, bf16[32,128,128]{2,1,0:T(8,128)(2,1)}, u32[]{:S(2)}) copy-start(bf16[32,128,128]{2,1,0:T(8,128)(2,1)} %incoming.7) | copy-start | bytes 3145732
  0.6 7.4 %collective-permute-start.3 = (bf16[1,128,128]{2,1,0:T(8,128)(2,1)}, bf16[1,128,128]{2,1,0:T(8,128)(2,1)S(1)}, u32[]{:S(2)}, u32[]{:S(2)}) collective-permute-start(bf16[1,128,128]{2,1,0:T(8,128)(2,1)} %bitcast.21), channel_id=1, source_target_pairs={{0,0},{1,32},{2,64},{3,96},{4,128},{5,160},{6,192},{7,224},{8,8},{... | collective-permute-start | bytes 98312 | tf_op jit(solution)/shard_map/ppermute | solution.py:31
  8.0 11.1 %collective-permute-start.5 = (bf16[1,128,128]{2,1,0:T(8,128)(2,1)S(1)}, bf16[1,128,128]{2,1,0:T(8,128)(2,1)S(1)}, u32[]{:S(2)}, u32[]{:S(2)}) collective-permute-start(bf16[1,128,128]{2,1,0:T(8,128)(2,1)S(1)} %collective-permute-done.3), channel_id=1, source_target_pairs={{0,32},{1,33},{2,34},{3,35},{4,36},{5,37},{6,38},{7,39},{8,40},{9,... | collective-permute-start | bytes 98312 | tf_op jit(solution)/shard_map/ppermute | solution.py:31
  11.5 7.6 %collective-permute-start.7 = (bf16[1,128,128]{2,1,0:T(8,128)(2,1)S(1)}, bf16[1,128,128]{2,1,0:T(8,128)(2,1)S(1)}, u32[]{:S(2)}, u32[]{:S(2)}) collective-permute-start(bf16[1,128,128]{2,1,0:T(8,128)(2,1)S(1)} %collective-permute-done.3), channel_id=1, source_target_pairs={{0,224},{1,225},{2,226},{3,227},{4,228},{5,229},{6,230},{7,231},{8... | collective-permute-start | bytes 98312 | tf_op jit(solution)/shard_map/ppermute | solution.py:31
  11.5 10.1 %collective-permute-start.4 = (bf16[1,128,128]{2,1,0:T(8,128)(2,1)S(1)}, bf16[1,128,128]{2,1,0:T(8,128)(2,1)S(1)}, u32[]{:S(2)}, u32[]{:S(2)}) collective-permute-start(bf16[1,128,128]{2,1,0:T(8,128)(2,1)S(1)} %collective-permute-done.3), channel_id=1, source_target_pairs={{0,128},{1,129},{2,130},{3,131},{4,132},{5,133},{6,134},{7,135},{8... | collective-permute-start | bytes 98312 | tf_op jit(solution)/shard_map/ppermute | solution.py:31
  19.2 5.2 %collective-permute-start.6 = (bf16[2,128,128]{2,1,0:T(8,128)(2,1)S(1)}, bf16[2,128,128]{2,1,0:T(8,128)(2,1)S(1)}, u32[]{:S(2)}, u32[]{:S(2)}) collective-permute-start(bf16[2,128,128]{2,1,0:T(8,128)(2,1)S(1)} %get-tuple-element.35), channel_id=1, source_target_pairs={{0,64},{1,65},{2,66},{3,67},{4,68},{5,69},{6,70},{7,71},{8,72},{9,... | collective-permute-start | bytes 196616 | tf_op jit(solution)/shard_map/ppermute | solution.py:31
  19.6 6.0 %collective-permute-start.8 = (bf16[2,128,128]{2,1,0:T(8,128)(2,1)S(1)}, bf16[2,128,128]{2,1,0:T(8,128)(2,1)S(1)}, u32[]{:S(2)}, u32[]{:S(2)}) collective-permute-start(bf16[2,128,128]{2,1,0:T(8,128)(2,1)S(1)} %get-tuple-element.34), channel_id=1, source_target_pairs={{0,192},{1,193},{2,194},{3,195},{4,196},{5,197},{6,198},{7,199},{8... | collective-permute-start | bytes 196616 | tf_op jit(solution)/shard_map/ppermute | solution.py:31
  25.7 14.6 %collective-permute-start.9 = (bf16[8,128,128]{2,1,0:T(8,128)(2,1)S(1)}, bf16[8,128,128]{2,1,0:T(8,128)(2,1)S(1)}, u32[]{:S(2)}, u32[]{:S(2)}) collective-permute-start(bf16[8,128,128]{2,1,0:T(8,128)(2,1)S(1)} %constant_dynamic-update-slice_fusion.right_own), channel_id=1, source_target_pairs={{0,16},{1,17},{2,18},{3,19},{4,20},{5,21},{6,22},{7,23},{8,24},{9,... | collective-permute-start | bytes 786440 | tf_op jit(solution)/shard_map/ppermute | solution.py:31
  27.3 6.8 %collective-permute-start = (bf16[1,128,128]{2,1,0:T(8,128)(2,1)}, bf16[1,128,128]{2,1,0:T(8,128)(2,1)S(1)}, u32[]{:S(2)}, u32[]{:S(2)}) collective-permute-start(bf16[1,128,128]{2,1,0:T(8,128)(2,1)} %bitcast.13), channel_id=1, source_target_pairs={{0,1},{1,0},{2,3},{3,2},{4,5},{5,4},{6,7},{7,6},{8,9},{9,8},{10,11... | collective-permute-start | bytes 98312 | tf_op jit(solution)/shard_map/ppermute | solution.py:31
  34.8 5.5 %collective-permute-start.1 = (bf16[2,128,128]{2,1,0:T(8,128)(2,1)S(1)}, bf16[2,128,128]{2,1,0:T(8,128)(2,1)S(1)}, u32[]{:S(2)}, u32[]{:S(2)}) collective-permute-start(bf16[2,128,128]{2,1,0:T(8,128)(2,1)S(1)} %pad_maximum_fusion.1), channel_id=1, source_target_pairs={{0,4},{1,5},{2,6},{3,7},{4,0},{5,1},{6,2},{7,3},{8,12},{9,13},{10,... | collective-permute-start | bytes 196616 | tf_op jit(solution)/shard_map/ppermute | solution.py:31
  34.8 10.5 %collective-permute-start.11 = (bf16[8,128,128]{2,1,0:T(8,128)(2,1)S(1)}, bf16[8,128,128]{2,1,0:T(8,128)(2,1)S(1)}, u32[]{:S(2)}, u32[]{:S(2)}) collective-permute-start(bf16[8,128,128]{2,1,0:T(8,128)(2,1)S(1)} %constant_dynamic-update-slice_fusion.right_own), channel_id=1, source_target_pairs={{0,8},{1,9},{2,10},{3,11},{4,12},{5,13},{6,14},{7,15},{8,0},{9,1},... | collective-permute-start | bytes 786440 | tf_op jit(solution)/shard_map/ppermute | solution.py:31
  40.2 24.0 %collective-permute-start.10 = (bf16[8,128,128]{2,1,0:T(8,128)(2,1)S(1)}, bf16[8,128,128]{2,1,0:T(8,128)(2,1)S(1)}, u32[]{:S(2)}, u32[]{:S(2)}) collective-permute-start(bf16[8,128,128]{2,1,0:T(8,128)(2,1)S(1)} %collective-permute-done.9.right_own), channel_id=1, source_target_pairs={{0,8},{1,9},{2,10},{3,11},{4,12},{5,13},{6,14},{7,15},{8,0},{9,1},... | collective-permute-start | bytes 786440 | tf_op jit(solution)/shard_map/ppermute | solution.py:31
  41.0 4.2 %collective-permute-start.2 = (bf16[4,128,128]{2,1,0:T(8,128)(2,1)S(1)}, bf16[4,128,128]{2,1,0:T(8,128)(2,1)S(1)}, u32[]{:S(2)}, u32[]{:S(2)}) collective-permute-start(bf16[4,128,128]{2,1,0:T(8,128)(2,1)S(1)} %pad_maximum_fusion.left_near), channel_id=1, source_target_pairs={{0,2},{1,3},{2,0},{3,1},{4,6},{5,7},{6,4},{7,5},{8,10},{9,11},{10,... | collective-permute-start | bytes 393224 | tf_op jit(solution)/shard_map/ppermute | solution.py:31
  56.6 24.7 %collective-permute-start.14 = (bf16[2,4,16,512]{3,2,1,0:T(8,128)(2,1)S(1)}, bf16[2,4,16,512]{3,2,1,0:T(8,128)(2,1)S(1)}, u32[]{:S(2)}, u32[]{:S(2)}) collective-permute-start(bf16[2,4,16,512]{3,2,1,0:T(8,128)(2,1)S(1)} %get-tuple-element.31), channel_id=1, source_target_pairs={{0,0},{1,32},{2,64},{3,96},{4,128},{5,160},{6,192},{7,224},{8,8},{... | collective-permute-start | bytes 393224 | tf_op jit(solution)/shard_map/ppermute | solution.py:31
  59.9 26.6 %collective-permute-start.12 = (bf16[2,4,16,512]{3,2,1,0:T(8,128)(2,1)S(1)}, bf16[2,4,16,512]{3,2,1,0:T(8,128)(2,1)S(1)}, u32[]{:S(2)}, u32[]{:S(2)}) collective-permute-start(bf16[2,4,16,512]{3,2,1,0:T(8,128)(2,1)S(1)} %get-tuple-element.30), channel_id=1, source_target_pairs={{0,0},{1,32},{2,64},{3,96},{4,128},{5,160},{6,192},{7,224},{8,8},{... | collective-permute-start | bytes 393224 | tf_op jit(solution)/shard_map/ppermute | solution.py:31
  75.4 35.2 %collective-permute-start.18 = (bf16[2,4,16,512]{3,2,1,0:T(8,128)(2,1)S(1)}, bf16[2,4,16,512]{3,2,1,0:T(8,128)(2,1)S(1)}, u32[]{:S(2)}, u32[]{:S(2)}) collective-permute-start(bf16[2,4,16,512]{3,2,1,0:T(8,128)(2,1)S(1)} %get-tuple-element.33), channel_id=1, source_target_pairs={{0,16},{1,48},{2,80},{3,112},{4,144},{5,176},{6,208},{7,240},{8,24... | collective-permute-start | bytes 393224 | tf_op jit(solution)/shard_map/ppermute | solution.py:31
  81.2 35.5 %collective-permute-start.16 = (bf16[2,4,16,512]{3,2,1,0:T(8,128)(2,1)S(1)}, bf16[2,4,16,512]{3,2,1,0:T(8,128)(2,1)S(1)}, u32[]{:S(2)}, u32[]{:S(2)}) collective-permute-start(bf16[2,4,16,512]{3,2,1,0:T(8,128)(2,1)S(1)} %get-tuple-element.32), channel_id=1, source_target_pairs={{0,16},{1,48},{2,80},{3,112},{4,144},{5,176},{6,208},{7,240},{8,24... | collective-permute-start | bytes 393224 | tf_op jit(solution)/shard_map/ppermute | solution.py:31
  81.2 40.0 %collective-permute-start.15 = (bf16[2,4,16,512]{3,2,1,0:T(8,128)(2,1)S(1)}, bf16[2,4,16,512]{3,2,1,0:T(8,128)(2,1)S(1)}, u32[]{:S(2)}, u32[]{:S(2)}) collective-permute-start(bf16[2,4,16,512]{3,2,1,0:T(8,128)(2,1)S(1)} %collective-permute-done.14.rest_2_), channel_id=1, source_target_pairs={{0,8},{1,9},{2,10},{3,11},{4,12},{5,13},{6,14},{7,15},{8,0},{9,1},... | collective-permute-start | bytes 393224 | tf_op jit(solution)/shard_map/ppermute | solution.py:31
  86.6 34.7 %collective-permute-start.13 = (bf16[2,4,16,512]{3,2,1,0:T(8,128)(2,1)S(1)}, bf16[2,4,16,512]{3,2,1,0:T(8,128)(2,1)S(1)}, u32[]{:S(2)}, u32[]{:S(2)}) collective-permute-start(bf16[2,4,16,512]{3,2,1,0:T(8,128)(2,1)S(1)} %collective-permute-done.12.rest_0_), channel_id=1, source_target_pairs={{0,8},{1,9},{2,10},{3,11},{4,12},{5,13},{6,14},{7,15},{8,0},{9,1},... | collective-permute-start | bytes 393224 | tf_op jit(solution)/shard_map/ppermute | solution.py:31
  110.7 10.6 %collective-permute-start.19 = (bf16[2,4,16,512]{3,2,1,0:T(8,128)(2,1)S(1)}, bf16[2,4,16,512]{3,2,1,0:T(8,128)(2,1)S(1)}, u32[]{:S(2)}, u32[]{:S(2)}) collective-permute-start(bf16[2,4,16,512]{3,2,1,0:T(8,128)(2,1)S(1)} %collective-permute-done.18.rest_6_), channel_id=1, source_target_pairs={{0,8},{1,9},{2,10},{3,11},{4,12},{5,13},{6,14},{7,15},{8,0},{9,1},... | collective-permute-start | bytes 393224 | tf_op jit(solution)/shard_map/ppermute | solution.py:31
  116.7 4.6 %collective-permute-start.17 = (bf16[2,4,16,512]{3,2,1,0:T(8,128)(2,1)S(1)}, bf16[2,4,16,512]{3,2,1,0:T(8,128)(2,1)S(1)}, u32[]{:S(2)}, u32[]{:S(2)}) collective-permute-start(bf16[2,4,16,512]{3,2,1,0:T(8,128)(2,1)S(1)} %collective-permute-done.16.rest_4_), channel_id=1, source_target_pairs={{0,8},{1,9},{2,10},{3,11},{4,12},{5,13},{6,14},{7,15},{8,0},{9,1},... | collective-permute-start | bytes 393224 | tf_op jit(solution)/shard_map/ppermute | solution.py:31
  118.2 1.2 copy-start.1
